TPU v7x, 256 devices: a whole 4x4x8 slice. The times are simulated.
256 devices in a mesh: ctx: 32 (over z, x), head: 8 (over y, core).
Axes of the slice: x: 4, y: 4, z: 8, core: 2. Of those that a mesh axis runs over, the one named last changes fastest.
Arguments:
- projected: bfloat16 [3, 32768, 4096], P(None, ('ctx', 'head')), may hold values from -2.5 to 2.5
- conv_filter: float32 [3, 4, 4096], replicated, may hold values from -2.7 to 2.7
- frequencies: bfloat16 [32, 128, 256], replicated, may hold values from -5 to 5
Outputs:
- attended: bfloat16 [32768, 4096], P(('ctx', 'head'))
All inputs are finite; a program needn't handle non-finite values.
Results may differ from a plain program's by a relative error of at most 0.013.
Values may be sent and summed in bfloat16 or wider, within the bound.
No kernel may reach another device: no remote copies, remote signals or barrier semaphores. Data moves between devices by JAX's collectives and lax.ppermute only.
A program may use at most 384 MiB of HBM per device.

v0:
```python
import jax
import jax.numpy as jnp
from jax import lax
from jax.sharding import PartitionSpec as P

H = 32
DH = 128
M = 256
KC = 4
BLOCK = 512


def passed_along(array, axis, by):
    size = lax.axis_size(axis)
    pairs = [(i, i + by) for i in range(size) if 0 <= i + by < size]
    return lax.ppermute(array, axis, pairs)


def prefix(array, axis, join, neutral):
    place = lax.axis_index(axis)
    gathered = jax.tree.map(
        lambda a, kind: lax.all_gather(a.astype(kind), axis), array, (jnp.bfloat16, jnp.bfloat16)
    )
    state = jax.tree.map(lambda a, e: jnp.zeros_like(a) + jnp.asarray(e, a.dtype), array, neutral)

    def one(step, state):
        return join(
            state,
            jax.tree.map(
                lambda a, own: lax.dynamic_index_in_dim(a, step, 0, False).astype(own.dtype),
                gathered,
                array,
            ),
        )

    return lax.fori_loop(0, place, one, state)


def convolve(padded, conv_taps, row_count):
    summed = jnp.zeros((padded.shape[0], row_count, padded.shape[2]), jnp.float32)
    for offset in range(KC):
        window = padded[:, KC - 1 - offset : KC - 1 - offset + row_count, :]
        summed = summed + conv_taps[:, offset][:, None, :] * window.astype(jnp.float32)
    return summed.astype(jnp.bfloat16)


def feature_maps(conved, head_omega, head_count):
    row_count = conved.shape[1]
    per_head = conved.reshape(3, row_count, head_count, DH)
    feature_scale = DH ** (-0.25)
    query_part = jnp.einsum(
        "lhd,hdm->lhm", per_head[0], head_omega, preferred_element_type=jnp.float32
    )
    query_map = jnp.exp(query_part * feature_scale).astype(jnp.bfloat16)
    keys_wide = per_head[1].astype(jnp.float32)
    halfnorm = jnp.sum(keys_wide * keys_wide, axis=2, keepdims=True) * (
        0.5 * feature_scale * feature_scale
    )
    key_part = jnp.einsum(
        "lhd,hdm->lhm", per_head[1], head_omega, preferred_element_type=jnp.float32
    )
    key_map = jnp.exp(key_part * feature_scale - halfnorm).astype(jnp.bfloat16)
    return (query_map, key_map, per_head[2])


def block_sums(key_map, values, block_rows):
    length, head_count = (key_map.shape[0], key_map.shape[1])
    block_count = length // block_rows
    key_blocks = key_map.reshape(block_count, block_rows, head_count, M)
    value_blocks = values.reshape(block_count, block_rows, head_count, DH)
    states = jnp.einsum(
        "brhm,brhd->bhmd", key_blocks, value_blocks, preferred_element_type=jnp.float32
    )
    totals = jnp.sum(key_blocks.astype(jnp.float32), axis=1)
    return (states, totals)


def split_pair(wide):
    upper = lax.optimization_barrier(wide.astype(jnp.bfloat16))
    lower = (wide - upper.astype(jnp.float32)).astype(jnp.bfloat16)
    return (upper, lower)


def attend(query_map, key_map, values, states, totals, prior_state, prior_total, block_rows):
    length, head_count = (query_map.shape[0], query_map.shape[1])
    block_count = length // block_rows
    causal = jnp.arange(block_rows)[:, None] >= jnp.arange(block_rows)[None, :]

    def advance(carried, pieces):
        running_state_sum, key_total = carried
        block_of_queries, block_of_keys, value_block, block_state, block_total = pieces
        scores = jnp.einsum(
            "qhm,khm->hqk", block_of_queries, block_of_keys, preferred_element_type=jnp.float32
        )
        scores = jnp.where(causal[None], scores, 0.0).astype(jnp.bfloat16)
        numerator = jnp.einsum(
            "hqk,khd->qhd", scores, value_block, preferred_element_type=jnp.float32
        )
        upper_state_part, lower_state_part = split_pair(running_state_sum)
        numerator = numerator + jnp.einsum(
            "tyg,ygl->tyl", block_of_queries, upper_state_part, preferred_element_type=jnp.float32
        )
        numerator = numerator + jnp.einsum(
            "tyg,ygl->tyl", block_of_queries, lower_state_part, preferred_element_type=jnp.float32
        )
        total_upper, total_lower = split_pair(key_total)
        denominator = jnp.sum(scores.astype(jnp.float32), axis=2).T
        denominator = denominator + jnp.einsum(
            "qhm,hm->qh", block_of_queries, total_upper, preferred_element_type=jnp.float32
        )
        denominator = denominator + jnp.einsum(
            "qhm,hm->qh", block_of_queries, total_lower, preferred_element_type=jnp.float32
        )
        attended_output = (numerator / denominator[:, :, None]).astype(jnp.bfloat16)
        return ((running_state_sum + block_state, key_total + block_total), attended_output)

    pieces = (
        query_map.reshape(block_count, block_rows, head_count, M),
        key_map.reshape(block_count, block_rows, head_count, M),
        values.reshape(block_count, block_rows, head_count, DH),
        states,
        totals,
    )
    finals, output_list = lax.scan(advance, (prior_state, prior_total), pieces)
    return output_list.reshape(length, head_count * DH)


def add_pair(preceding_part, latter):
    return (preceding_part[0] + latter[0], preceding_part[1] + latter[1])


def per_device(projected, conv_filter, frequencies):
    row_count = projected.shape[1]
    rim_rows = KC - 1
    group_size = lax.axis_size("head")
    group_heads = H // group_size
    head_start = lax.axis_index("head") * group_heads
    group_omega = lax.dynamic_slice_in_dim(frequencies, head_start, group_heads, 0)
    before_rim = passed_along(projected[:, row_count - rim_rows :, :], ("ctx", "head"), 1)
    source = convolve(jnp.concatenate([before_rim, projected], axis=1), conv_filter, row_count)
    moved = lax.all_to_all(source, "head", split_axis=2, concat_axis=1, tiled=True)
    query_map, key_map, values = feature_maps(moved, group_omega, group_heads)
    states, totals = block_sums(key_map, values, BLOCK)
    identity = (
        jnp.zeros((group_heads, M, DH), jnp.float32),
        jnp.zeros((group_heads, M), jnp.float32),
    )
    prior_state, prior_total = prefix(
        (jnp.sum(states, axis=0), jnp.sum(totals, axis=0)), "ctx", add_pair, identity
    )
    output_list = attend(
        query_map, key_map, values, states, totals, prior_state, prior_total, BLOCK
    )
    return lax.all_to_all(output_list, "head", split_axis=0, concat_axis=1, tiled=True)


def solution(mesh):
    placed = (P(None, ("ctx", "head"), None), P(), P())
    return jax.shard_map(
        per_device, mesh=mesh, in_specs=placed, out_specs=P(("ctx", "head"), None), check_vma=False
    )
```

profile of v0, /device:TPU:230, one launch (start us, length us, event | category | flops | bytes accessed | tf_op | source)
XLA Modules:
  0.0 343.8 jit_solution(14811462566436793422)
XLA Ops:
  6.5 1.1 slice.39
  7.7 1.9 collective-permute-start
  9.6 1.6 fusion.46
  11.2 7.2 %copy.79 = bf16[3,128,4096]{1,0,2:T(4,128)(2,1)} copy(bf16[3,128,4096]{2,1,0:T(8,128)(2,1)} %param.7) | data formatting | bytes 6291456 | tf_op args[0]
  18.3 2.0 copy.110
  20.3 2.0 copy.111
  22.3 2.0 copy.112
  24.3 2.0 copy.113
  26.3 7.7 %fusion.36 = (bf16[3,128,4096]{2,1,0:T(8,128)(2,1)}, bf16[3,128,4096]{2,1,0:T(8,128)(2,1)}, bf16[3,128,4096]{2,1,0:T(8,128)(2,1)}) fusion(bf16[3,3,4096]{2,1,0:T(4,128)(2,1)S(1)} %collective-permute-done, bf16[3,128,4096]{2,1,0:T(8,128)(2,1)} %param.7), kind=kLoop, calls=%fused_computation.57 | loop fusion | flops 18874368 | bytes 12656640 | tf_op jit(solution)/shard_map/concatenate | solution.py:140
  34.0 7.2 %copy.121 = bf16[3,128,4096]{1,0,2:T(4,128)(2,1)} copy(bf16[3,128,4096]{2,1,0:T(8,128)(2,1)} %get-tuple-element.195) | data formatting | bytes 6291456
  41.2 7.2 %copy.122 = bf16[3,128,4096]{1,0,2:T(4,128)(2,1)} copy(bf16[3,128,4096]{2,1,0:T(8,128)(2,1)} %get-tuple-element.197) | data formatting | bytes 6291456
  48.4 7.2 %copy.123 = bf16[3,128,4096]{1,0,2:T(4,128)(2,1)} copy(bf16[3,128,4096]{2,1,0:T(8,128)(2,1)} %get-tuple-element.196) | data formatting | bytes 6291456
  55.5 23.1 %add_convert_fusion = bf16[3,128,4096]{1,0,2:T(4,128)(2,1)} fusion(bf16[3,128,4096]{1,0,2:T(4,128)(2,1)} %copy.123, bf16[3,128,4096]{1,0,2:T(4,128)(2,1)} %copy.122, bf16[3,128,4096]{1,0,2:T(4,128)(2,1)} %copy.121, bf16[3,128,4096]{1,0,2:T(4,128)(2,1)} %copy.79, f32[3,4096]{0,1:T(8,128)} %bitcast.147, f32[3,4096]{0,1:T(8,128)} %bitcast.146, ...), kind=kLoop, calls=%fused_computation.48 | loop fusion | flops 18874368 | bytes 15925248 | tf_op jit(solution)/shard_map/convert_element_type | solution.py:44
  78.6 5.5 %all-to-all-start = ((bf16[3,128,4096]{1,0,2:T(4,128)(2,1)}), bf16[3,128,4096]{1,0,2:T(4,128)(2,1)}, u32[]{:S(2)}, u32[]{:S(2)}) async-start(bf16[3,128,4096]{1,0,2:T(4,128)(2,1)} %add_convert_fusion), calls=%async_computation | async-start | bytes 8388608 | tf_op jit(solution)/shard_map/all_to_all | solution.py:141
  84.3 49.5 %all-to-all-done = bf16[3,128,4096]{1,0,2:T(4,128)(2,1)} async-done(((bf16[3,128,4096]{1,0,2:T(4,128)(2,1)}), bf16[3,128,4096]{1,0,2:T(4,128)(2,1)}, u32[]{:S(2)}, u32[]{:S(2)}) %all-to-all-start) | async-done | bytes 3145760 | tf_op jit(solution)/shard_map/all_to_all | solution.py:141
  133.9 4.8 %copy.136 = bf16[3,128,8,512]{1,2,3,0:T(8,128)(2,1)S(1)} copy(bf16[3,128,8,512]{1,0,3,2:T(4,128)(2,1)} %bitcast.6) | data formatting | bytes 6291456 | tf_op jit(solution)/shard_map/all_to_all | solution.py:141
  138.6 1.7 fusion.45
  140.4 1.5 squeeze.30
  142.1 2.5 fusion.48
  144.6 4.5 %reshape.38 = bf16[2,512,4,256]{1,0,3,2:T(2,128)(2,1)} reshape(bf16[1024,4,256]{0,2,1:T(8,128)(2,1)} %get-tuple-element.208) | data formatting | bytes 4194304 | tf_op jit(solution)/shard_map/reshape | solution.py:69
  149.2 6.1 %copy.97 = bf16[2,512,4,256]{3,1,2,0:T(8,128)(2,1)} copy(bf16[2,512,4,256]{1,0,3,2:T(2,128)(2,1)} %reshape.38) | data formatting | bytes 4194304 | tf_op jit(solution)/shard_map/reshape | solution.py:69
  155.3 1.5 reshape.51
  156.7 4.1 %fusion.47 = (bf16[4,256,128]{2,1,0:T(8,128)(2,1)}, f32[2,4,256,128]{3,2,1,0:T(8,128)}) fusion(bf16[2,512,4,256]{3,1,2,0:T(8,128)(2,1)} %copy.97, bf16[2,512,4,128]{1,0,3,2:T(2,128)(2,1)S(1)} %reshape.51), kind=kOutput, calls=%fused_computation.72 | convolution fusion | flops 268566528 | bytes 4456448 | tf_op jit(solution)/shard_map/brhm,brhd->bhmd/dot_general | solution.py:71
  160.9 1.2 copy.95
  162.9 1.7 convert_reduce_fusion.1
  164.8 1.5 squeeze.31
  166.3 2.2 fusion.37
  168.5 4.5 %reshape.39 = bf16[2,512,4,256]{1,0,3,2:T(2,128)(2,1)} reshape(bf16[1024,4,256]{0,2,1:T(8,128)(2,1)} %fusion.37) | data formatting | bytes 4194304 | tf_op jit(solution)/shard_map/reshape | solution.py:118
  173.0 4.7 %copy.96 = bf16[2,512,4,256]{3,1,2,0:T(8,128)(2,1)S(1)} copy(bf16[2,512,4,256]{1,0,3,2:T(2,128)(2,1)} %reshape.39) | data formatting | bytes 4194304
  177.7 46.5 %all-gather.2 = bf16[32,4,256]{2,1,0:T(4,128)(2,1)S(1)} all-gather(bf16[1,4,256]{2,1,0:T(4,128)(2,1)S(1)} %bitcast.152), channel_id=3, replica_groups=mesh['ctx'=32,'head'=8] {'ctx'}, dimensions={0}, use_global_device_ids=true | all-gather | bytes 67584 | tf_op jit(solution)/shard_map/all_gather | solution.py:22
  224.3 29.6 %all-gather.5.cloned.1.call-done = bf16[128,256,128]{2,1,0:T(8,128)(2,1)} async-done(((bf16[4,256,128]{2,1,0:T(8,128)(2,1)}), bf16[128,256,128]{2,1,0:T(8,128)(2,1)}) %all-gather.5.cloned.1.call-update) | async-done | bytes 8388624 | tf_op jit(solution)/shard_map/all_gather | solution.py:22
  253.9 34.7 %while.27 = (s32[]{:T(128)}, f32[4,256,128]{2,1,0:T(8,128)S(1)}, f32[4,256]{1,0:T(4,128)S(1)}, s32[]{:T(128)}, bf16[32,4,256,128]{3,2,1,0:T(8,128)(2,1)}, /*inde...) while((s32[]{:T(128)}, f32[4,256,128]{2,1,0:T(8,128)S(1)}, f32[4,256]{1,0:T(4,128)S(1)}, ...), condition=%wide.region_4.5_spmd, body=%wide.region_3.0_spmd.sunk | while | flops 264197 | bytes 1321095 | solution.py:36
  257.3 1.1 convert_add_fusion.4
  262.9 1.1 convert_add_fusion.4
  270.7 1.1 convert_add_fusion.4
  288.9 23.2 %while.28 = (s32[]{:T(128)}, f32[4,256,128]{1,2,0:T(8,128)S(1)}, f32[4,256]{1,0:T(4,128)S(1)}, bf16[2,512,4,128]{3,2,1,0:T(4,128)(2,1)}, f32[2,4,256,128]{3,2,1,...) while((s32[]{:T(128)}, f32[4,256,128]{1,2,0:T(8,128)S(1)}, ...), condition=%wide.region_8.9_spmd.clone, body=%wide.region_6.8_spmd.clone.sunk | while | flops 1082006528 | bytes 41250516 | solution.py:124
  289.4 3.5 %convert_reduce_fusion.3 = (f32[4,512]{1,0:T(4,128)S(1)}, bf16[4,512,512]{1,2,0:T(8,128)(2,1)}) fusion(bf16[2,512,4,256]{3,1,2,0:T(8,128)(2,1)} %get-tuple-element.369, s32[]{:T(128)} %get-tuple-element.351, bf16[2,512,4,256]{3,1,2,0:T(8,128)(2,1)S(1)} %get-tuple-element.368, pred[512,512]{0,1:T(8,128)(4,1)S(1)} %iota_compare_fusion.2), kind=kOutput, calls=%fused_computation.3.clone.1 | convolution fusion | flops 541063168 | bytes 4465664 | tf_op jit(solution)/shard_map/while/body/eval_jaxpr/qhm,khm->hqk/dot_general | solution.py:92
  294.3 1.3 fusion.78
  296.8 1.3 fusion.83
  298.1 1.4 copy.148
  301.0 3.5 %convert_reduce_fusion.3 = (f32[4,512]{1,0:T(4,128)S(1)}, bf16[4,512,512]{1,2,0:T(8,128)(2,1)}) fusion(bf16[2,512,4,256]{3,1,2,0:T(8,128)(2,1)} %get-tuple-element.369, s32[]{:T(128)} %get-tuple-element.351, bf16[2,512,4,256]{3,1,2,0:T(8,128)(2,1)S(1)} %get-tuple-element.368, pred[512,512]{0,1:T(8,128)(4,1)S(1)} %iota_compare_fusion.2), kind=kOutput, calls=%fused_computation.3.clone.1 | convolution fusion | flops 541063168 | bytes 4465664 | tf_op jit(solution)/shard_map/while/body/eval_jaxpr/qhm,khm->hqk/dot_general | solution.py:92
  306.0 1.3 fusion.78
  308.4 1.3 fusion.83
  309.7 1.4 copy.148
  312.1 1.6 all_to_all.28
  313.7 20.3 %all_to_all.34 = bf16[8,128,512]{2,1,0:T(8,128)(2,1)} all-to-all(bf16[8,128,512]{2,1,0:T(8,128)(2,1)S(1)} %all_to_all.28), channel_id=1, replica_groups=mesh['ctx'=32,'head'=8] {'head'}, dimensions={0} | all-to-all | bytes 2097152 | tf_op jit(solution)/shard_map/all_to_all | solution.py:154
  334.0 1.6 copy.99
  335.6 1.3 copy.100
  (111 shorter events, 40.3 us)
Async XLA Ops:
  6.5 135.6 %copy-start = (bf16[32,128,256]{2,1,0:T(8,128)(2,1)S(1)}, bf16[32,128,256]{2,1,0:T(8,128)(2,1)}, u32[]{:S(2)}) copy-start(bf16[32,128,256]{2,1,0:T(8,128)(2,1)} %param.9) | copy-start | bytes 6291460
  7.7 18.7 %collective-permute-start = (bf16[3,3,4096]{2,1,0:T(4,128)(2,1)S(1)}, bf16[3,3,4096]{2,1,0:T(4,128)(2,1)S(1)}, u32[]{:S(2)}, u32[]{:S(2)}) collective-permute-start(bf16[3,3,4096]{2,1,0:T(4,128)(2,1)S(1)} %slice.39), channel_id=1, source_target_pairs={{0,1},{1,2},{2,3},{3,4},{4,5},{5,6},{6,7},{7,8},{8,9},{9,10},{10,1... | collective-permute-start | bytes 221192 | tf_op jit(solution)/shard_map/ppermute | solution.py:16
  78.6 55.3 %all-to-all-start = ((bf16[3,128,4096]{1,0,2:T(4,128)(2,1)}), bf16[3,128,4096]{1,0,2:T(4,128)(2,1)}, u32[]{:S(2)}, u32[]{:S(2)}) async-start(bf16[3,128,4096]{1,0,2:T(4,128)(2,1)} %add_convert_fusion), calls=%async_computation | async-start | bytes 8388608 | tf_op jit(solution)/shard_map/all_to_all | solution.py:141
  84.1 169.8 %all-gather.5.cloned.1.call-start = ((), (), s32[]{:S(2)}) async-start(), calls=%async_computation.2 | async-start | bytes 8650752 | tf_op jit(solution)/shard_map/all_gather | solution.py:22
  160.9 2.0 copy-start.3
  289.4 3.9 %copy-start.4 = (f32[2,4,256,128]{3,2,1,0:T(8,128)S(1)}, f32[2,4,256,128]{3,2,1,0:T(8,128)}, u32[]{:S(2)}) copy-start(f32[2,4,256,128]{3,2,1,0:T(8,128)} %get-tuple-element.365) | copy-start | bytes 3145732 | tf_op jit(solution)/shard_map/while
  294.3 1.8 copy-start.2
  294.3 2.0 copy-start.5
  301.0 3.9 %copy-start.4 = (f32[2,4,256,128]{3,2,1,0:T(8,128)S(1)}, f32[2,4,256,128]{3,2,1,0:T(8,128)}, u32[]{:S(2)}) copy-start(f32[2,4,256,128]{3,2,1,0:T(8,128)} %get-tuple-element.365) | copy-start | bytes 3145732 | tf_op jit(solution)/shard_map/while
  305.9 1.8 copy-start.2
  306.0 2.0 copy-start.5
  312.1 24.9 %copy-start.1 = (bf16[32,128,256]{2,1,0:T(8,128)(2,1)S(1)}, bf16[32,128,256]{2,1,0:T(8,128)(2,1)}, u32[]{:S(2)}) copy-start(bf16[32,128,256]{2,1,0:T(8,128)(2,1)} %param.9) | copy-start | bytes 6291460
Sparse Core Ops, SparseCore 0:
  161.0 92.8 all-gather.4
where the time goes:
time: 346 us; the launch traced here: 344 us
  local copies, waits for them, and re-layouts  84.4 us (24%)
  waiting for transfers between devices  79.2 us (23%)
  other arithmetic  69.1 us (20%)
  blocking collectives  66.8 us (19%)
  matrix products  21.7 us (6%)
  between operations  13.6 us (4%)
  starting transfers between devices  7.61 us (2%)
    all_to_all x1, waiting for transfers between devices, per_device(): lax.all_to_all(source, 'head', split_axis=2, concat_axis=1, tiled=True)  49.5 us
    all_gather x1, blocking collectives, prefix(): lax.all_gather(a.astype(kind), axis)  46.5 us
    unnamed x13, local copies, waits for them, and re-layouts  34.6 us
    add x62, other arithmetic, add_pair(): return (preceding_part[0] + latter[0], preceding_part[1] + latter[1])  33.6 us
    all_gather x1, waiting for transfers between devices, prefix(): lax.all_gather(a.astype(kind), axis)  29.6 us
    convert_element_type x1, other arithmetic, convolve(): return summed.astype(jnp.bfloat16)  23.1 us
    all_to_all x1, blocking collectives, per_device(): lax.all_to_all(output_list, 'head', split_axis=0, concat_axis=1, tiled=True)  20.3 us
    reshape x2, local copies, waits for them, and re-layouts, block_sums(): key_blocks = key_map.reshape(block_count, block_rows, head_count, M)  10.6 us
  transfers between devices with their start and end apart: 3, of which 2 were waited for; matrix products, arithmetic and copies ran while one was open for 10% of the time, Pallas kernels for 0%

commit v1 on v0

v1 whole, which is shorter than its diff:
```python
import functools

import jax
import jax.numpy as jnp
from jax import lax
from jax.experimental import pallas as pl
from jax.experimental.pallas import tpu as pltpu
from jax.sharding import Mesh
from jax.sharding import PartitionSpec as P

H = 32
DH = 128
M = 256
KC = 4
D = H * DH

CORES = 2
HEADS = H // CORES
COLS = HEADS * DH
ROWS = 128
CHUNK = CORES * ROWS
RIM = 8
PIECES = 2 * HEADS
STATE_ROWS = DH + 8
GROUP = 4
WIDE = GROUP * DH
STEPS = HEADS // GROUP
FEATURE_SCALE = DH ** (-0.25)
NORM_SCALE = 0.5 * FEATURE_SCALE * FEATURE_SCALE

AXES = ("zh", "zl", "x", "y", "c")
SIZES = (4, 2, 4, 4, 2)
PLANE = ("zl", "x", "y")

f32 = jnp.float32
bf16 = jnp.bfloat16
NT = (((1,), (1,)), ((), ()))


def dot(a, b):
    return jnp.dot(a, b, preferred_element_type=f32)


def dot_nt(a, b):
    return lax.dot_general(a, b, NT, preferred_element_type=f32)


def fill(core, own, other, rim_a, rim_b, rows):
    rows[0:RIM, :] = rim_a[0].astype(f32) + rim_b[0].astype(f32)
    rows[pl.ds(pl.multiple_of(RIM + core * ROWS, 8), ROWS), :] = own[0].astype(f32)
    rows[pl.ds(pl.multiple_of(RIM + (1 - core) * ROWS, 8), ROWS), :] = other[0].astype(f32)


def convolve(rows, taps, head):
    cols = slice(head * DH, (head + 1) * DH)
    summed = taps[0, 0:1, cols] * rows[RIM : RIM + CHUNK, cols]
    for j in range(1, KC):
        summed = summed + taps[0, j : j + 1, cols] * rows[RIM - j : RIM - j + CHUNK, cols]
    return summed.astype(bf16)


def keys_kernel(
    core_ref, own_k, own_v, other_k, other_v, rim_ka, rim_kb, rim_va, rim_vb, taps_k, taps_v,
    omega, state, key_map, values, rows_k, rows_v,
):
    core = core_ref[0]
    fill(core, own_k, other_k, rim_ka, rim_kb, rows_k)
    fill(core, own_v, other_v, rim_va, rim_vb, rows_v)
    ones = jnp.ones((M, M), bf16)
    for head in range(GROUP):
        k = convolve(rows_k, taps_k, head)
        v = convolve(rows_v, taps_v, head)
        k_wide = k.astype(f32)
        square = k_wide * k_wide
        upper = square.astype(bf16)
        lower = (square - upper.astype(f32)).astype(bf16)
        norm = dot(jnp.concatenate([upper, lower], axis=1), ones)
        mapped = jnp.exp(dot(k, omega[head]) * FEATURE_SCALE - norm * NORM_SCALE).astype(bf16)
        key_map[head] = mapped
        values[head] = v
        extended = jnp.concatenate([v.T, jnp.ones((16, CHUNK), bf16)], axis=0)
        sums = dot(extended, mapped)[:STATE_ROWS].astype(bf16)
        state[2 * head] = sums[:, : M // 2]
        state[2 * head + 1] = sums[:, M // 2 :]


def scores_kernel(
    core_ref, own_q, other_q, rim_qa, rim_qb, taps_q, omega, key_map, query_map, scores, rows_q
):
    core = core_ref[0]
    fill(core, own_q, other_q, rim_qa, rim_qb, rows_q)
    causal = lax.broadcasted_iota(jnp.int32, (CHUNK, CHUNK), 0) >= lax.broadcasted_iota(
        jnp.int32, (CHUNK, CHUNK), 1
    )
    for head in range(GROUP):
        q = convolve(rows_q, taps_q, head)
        mapped = jnp.exp(dot(q, omega[head]) * FEATURE_SCALE).astype(bf16)
        query_map[head] = mapped
        scores[head] = jnp.where(causal, dot_nt(mapped, key_map[head]), 0.0).astype(bf16)


def prefix_kernel(before_1, before_2, before_3, sums, out):
    running = before_1[...].astype(f32) + before_2[...].astype(f32) + before_3[...].astype(f32)
    for i in range(PIECES):
        out[i] = running.astype(bf16)
        running = running + sums[i].astype(f32)


def attend_kernel(core_ref, scores, query_map, values, state, out_own, out_other, rows):
    core = core_ref[0]
    ones = jnp.ones((CHUNK, DH), bf16)
    for head in range(GROUP):
        cols = slice(head * DH, (head + 1) * DH)
        prior = jnp.concatenate([state[2 * head], state[2 * head + 1]], axis=1)
        total = jnp.broadcast_to(prior[DH : DH + 1], (DH, M))
        prior = jnp.concatenate([prior[:DH], total], axis=0)
        both = dot(scores[head], jnp.concatenate([values[head], ones], axis=1))
        both = both + dot_nt(query_map[head], prior)
        rows[:, cols] = both[:, :DH] / both[:, DH:]
    out_own[...] = rows[pl.ds(pl.multiple_of(core * ROWS, 8), ROWS), :].astype(bf16)
    out_other[...] = rows[pl.ds(pl.multiple_of((1 - core) * ROWS, 8), ROWS), :].astype(bf16)


def spec(shape, index):
    return pl.BlockSpec(shape, index)


def own_spec(which):
    return spec((1, ROWS, WIDE), lambda i, core: (which, 0, core[0] * STEPS + i))


def other_spec(which):
    return spec((1, ROWS, WIDE), lambda i, core: (which, 0, i))


def rim_spec(which):
    return spec((1, RIM, WIDE), lambda i, core: (which, 0, i))


def taps_spec(which):
    return spec((1, KC, WIDE), lambda i, core: (which, 0, core[0] * STEPS + i))


OMEGA_SPEC = spec((GROUP, DH, M), lambda i, core: (core[0] * STEPS + i, 0, 0))


def head_spec(*dims):
    return spec((GROUP,) + dims, lambda i, core: (i,) + (0,) * len(dims))


STATE_SPEC = spec((2 * GROUP, STATE_ROWS, M // 2), lambda i, core: (i, 0, 0))
OUT_SPEC = spec((ROWS, WIDE), lambda i, core: (0, i))


def shape(*dims, dtype=bf16):
    return jax.ShapeDtypeStruct(dims, dtype)


def call(kernel, in_specs, out_specs, out_shape, scratch, flops, moved):
    return pl.pallas_call(
        kernel,
        grid_spec=pltpu.PrefetchScalarGridSpec(
            num_scalar_prefetch=1,
            grid=(STEPS,),
            in_specs=in_specs,
            out_specs=out_specs,
            scratch_shapes=scratch,
        ),
        out_shape=out_shape,
        compiler_params=pltpu.CompilerParams(
            dimension_semantics=("arbitrary",), vmem_limit_bytes=48 * 2**20
        ),
        cost_estimate=pl.CostEstimate(flops=flops, bytes_accessed=moved, transcendentals=0),
    )


def swap(array):
    return lax.ppermute(array, "c", [(0, 1), (1, 0)])


def per_device(projected, conv_filter, frequencies):
    core = lax.axis_index("c").astype(jnp.int32)
    cores = core.reshape(1)
    sent = lax.dynamic_slice_in_dim(projected, (1 - core) * COLS, COLS, 2)
    other = swap(sent)
    rim = projected[:, ROWS - RIM :, :]
    chips = ("zh", "zl", "x", "y", "c")
    count = 256 // CORES
    rims = [
        lax.ppermute(
            rim[:, :, to * COLS : (to + 1) * COLS],
            chips,
            [(2 * i + 1, 2 * (i + 1) + to) for i in range(count - 1)],
        )
        for to in range(CORES)
    ]
    state, key_map, values = call(
        keys_kernel,
        [own_spec(1), own_spec(2), other_spec(1), other_spec(2)]
        + [rim_spec(1), rim_spec(1), rim_spec(2), rim_spec(2)]
        + [taps_spec(1), taps_spec(2), OMEGA_SPEC],
        [STATE_SPEC, head_spec(CHUNK, M), head_spec(CHUNK, DH)],
        [shape(PIECES, STATE_ROWS, M // 2), shape(HEADS, CHUNK, M), shape(HEADS, CHUNK, DH)],
        [pltpu.VMEM((RIM + CHUNK, WIDE), f32)] * 2,
        flops=4 * 10**9,
        moved=10 * 2**20,
    )(
        cores, projected, projected, other, other, rims[0], rims[1], rims[0], rims[1],
        conv_filter, conv_filter, frequencies,
    )
    gathered = lax.all_to_all(state, PLANE, 0, 0, tiled=True)
    query_map, scores = call(
        scores_kernel,
        [own_spec(0), other_spec(0), rim_spec(0), rim_spec(0), taps_spec(0), OMEGA_SPEC]
        + [head_spec(CHUNK, M)],
        [head_spec(CHUNK, M), head_spec(CHUNK, CHUNK)],
        [shape(HEADS, CHUNK, M), shape(HEADS, CHUNK, CHUNK)],
        [pltpu.VMEM((RIM + CHUNK, WIDE), f32)],
        flops=8 * 10**9,
        moved=20 * 2**20,
    )(cores, projected, other, rims[0], rims[1], conv_filter, frequencies, key_map)
    total = jnp.sum(gathered.astype(f32), axis=0).astype(bf16)
    planes = SIZES[0]
    before = [
        lax.ppermute(total, "zh", [(i, i + by) for i in range(planes - by)])
        for by in range(1, planes)
    ]
    prior = pl.pallas_call(
        prefix_kernel,
        out_shape=shape(PIECES, STATE_ROWS, M // 2),
        compiler_params=pltpu.CompilerParams(vmem_limit_bytes=16 * 2**20),
    )(*before, gathered)
    prior = lax.all_to_all(prior, PLANE, 0, 0, tiled=True)
    out_own, out_other = call(
        attend_kernel,
        [head_spec(CHUNK, CHUNK), head_spec(CHUNK, M), head_spec(CHUNK, DH), STATE_SPEC],
        [OUT_SPEC, OUT_SPEC],
        [shape(ROWS, COLS), shape(ROWS, COLS)],
        [pltpu.VMEM((CHUNK, WIDE), f32)],
        flops=4 * 10**9,
        moved=8 * 2**20,
    )(cores, scores, query_map, values, prior)
    arrived = swap(out_other)
    first = jnp.where(core == 0, out_own, arrived)
    second = jnp.where(core == 0, arrived, out_own)
    return jnp.concatenate([first, second], axis=1)


def solution(mesh):
    devices = Mesh(mesh.devices.reshape(SIZES), AXES)
    placed = (P(None, AXES, None), P(), P())
    return jax.shard_map(
        per_device, mesh=devices, in_specs=placed, out_specs=P(AXES, None), check_vma=False
    )
```

time: 346 us -> 92.3 us (0.27)
  the two profiles are of different devices: /device:TPU:230 before, /device:TPU:1 now
where the time goes in v1:
time: 92.3 us; the launch traced here: 91.7 us
  starting transfers between devices  26.7 us (29%)
  blocking collectives  25.7 us (28%)
  Pallas kernels  16.1 us (17%)
  waiting for transfers between devices  12.8 us (14%)
  local copies, waits for them, and re-layouts  8.95 us (10%)
  other arithmetic  1.3 us (1%)
    all_to_all x1, blocking collectives, per_device(): gathered = lax.all_to_all(state, PLANE, 0, 0, tiled=True)  25.7 us
    ppermute x3, starting transfers between devices, per_device(): lax.ppermute(total, 'zh', [(i, i + by) for i in range(planes - by)])  12.3 us
    all_to_all x1, waiting for transfers between devices, per_device(): prior = lax.all_to_all(prior, PLANE, 0, 0, tiled=True)  8.65 us
    pallas_call x1, Pallas kernels, per_device(): call(keys_kernel, [own_spec(1), own_spec(2), other_spec(1), other_spec(2)...  6.8 us
    unnamed x12, local copies, waits for them, and re-layouts  6.45 us
    ppermute x2, starting transfers between devices, swap(): return lax.ppermute(array, 'c', [(0, 1), (1, 0)])  5.6 us
    ppermute x2, starting transfers between devices, per_device(): lax.ppermute(rim[:, :, to * COLS:(to + 1) * COLS], chips, [(2 * i + 1, 2...  4.58 us
    pallas_call x1, Pallas kernels, per_device(): call(scores_kernel, [own_spec(0), other_spec(0), rim_spec(0), rim_spec(0)...  4.41 us
  transfers between devices with their start and end apart: 8, of which 4 were waited for; matrix products, arithmetic and copies ran while one was open for 1% of the time, Pallas kernels for 5%

profile of v1, /device:TPU:1, one launch (start us, length us, event | category | flops | bytes accessed | tf_op | source)
XLA Modules:
  0.0 91.7 jit_solution(9893179784492426404)
XLA Ops:
  0.0 0.0 copy-start
  0.0 1.5 %constant_dynamic-slice_fusion = bf16[3,128,2048]{2,1,0:T(8,128)(2,1)S(1)} fusion(bf16[3,128,4096]{2,1,0:T(8,128)(2,1)} %own_q.1, s32[]{:T(128)S(6)} %select_n.16), kind=kLoop, calls=%fused_computation.3 | loop fusion | bytes 3145732 | tf_op jit(solution)/shard_map/dynamic_slice | solution.py:184
  1.6 3.3 %collective-permute-start = (bf16[3,128,2048]{2,1,0:T(8,128)(2,1)S(1)}, bf16[3,128,2048]{2,1,0:T(8,128)(2,1)S(1)}, u32[]{:S(2)}, u32[]{:S(2)}) collective-permute-start(bf16[3,128,2048]{2,1,0:T(8,128)(2,1)S(1)} %constant_dynamic-slice_fusion), channel_id=1, source_target_pairs={{0,1},{1,0},{2,3},{3,2},{4,5},{5,4},{6,7},{7,6},{8,9},{9,8},{10,11... | collective-permute-start | bytes 4718600 | tf_op jit(solution)/shard_map/ppermute | solution.py:178
  4.9 1.0 %fusion = (bf16[3,8,2048]{2,1,0:T(8,128)(2,1)S(1)}, bf16[3,8,2048]{2,1,0:T(8,128)(2,1)S(1)}) fusion(bf16[3,128,4096]{2,1,0:T(8,128)(2,1)} %own_q.1), kind=kLoop, calls=%fused_computation.4 | loop fusion | bytes 393216 | tf_op jit(solution)/shard_map/slice | solution.py:191
  5.8 1.4 %collective-permute-start.1 = (bf16[3,8,2048]{2,1,0:T(8,128)(2,1)S(1)}, bf16[3,8,2048]{2,1,0:T(8,128)(2,1)S(1)}, u32[]{:S(2)}, u32[]{:S(2)}) collective-permute-start(bf16[3,8,2048]{2,1,0:T(8,128)(2,1)S(1)} %get-tuple-element.20), channel_id=1, source_target_pairs={{1,2},{3,4},{5,6},{7,8},{9,10},{11,12},{13,14},{15,16},{17,18},{19... | collective-permute-start | bytes 294920 | tf_op jit(solution)/shard_map/ppermute | solution.py:190
  7.2 3.2 %collective-permute-start.2 = (bf16[3,8,2048]{2,1,0:T(8,128)(2,1)S(1)}, bf16[3,8,2048]{2,1,0:T(8,128)(2,1)S(1)}, u32[]{:S(2)}, u32[]{:S(2)}) collective-permute-start(bf16[3,8,2048]{2,1,0:T(8,128)(2,1)S(1)} %get-tuple-element.19), channel_id=1, source_target_pairs={{1,3},{3,5},{5,7},{7,9},{9,11},{11,13},{13,15},{15,17},{17,19},{19... | collective-permute-start | bytes 294920 | tf_op jit(solution)/shard_map/ppermute | solution.py:190
  10.4 0.0 collective-permute-done.1.rim_ka.rim_va.rim_qa
  10.4 1.6 %collective-permute-done.2.rim_kb.rim_vb.rim_qb = bf16[3,8,2048]{2,1,0:T(8,128)(2,1)S(1)} collective-permute-done((bf16[3,8,2048]{2,1,0:T(8,128)(2,1)S(1)}, bf16[3,8,2048]{2,1,0:T(8,128)(2,1)S(1)}, u32[]{:S(2)}, u32[]{:S(2)}) %collective-permute-start.2) | collective-permute-done | bytes 98336 | tf_op jit(solution)/shard_map/ppermute | solution.py:190
  12.1 0.0 collective-permute-done.other_k.other_v.other_q
  12.1 0.0 copy-done
  12.1 6.8 %shard_map.37 = (bf16[32,136,128]{2,1,0:T(8,128)(2,1)S(1)}, bf16[16,256,256]{2,1,0:T(8,128)(2,1)}, bf16[16,256,128]{2,1,0:T(8,128)(2,1)S(1)}) custom-call(s32[1]{0:T(128)} %bitcast.core_ref, bf16[3,128,4096]{2,1,0:T(8,128)(2,1)} %own_q.1, bf16[3,128,4096]{2,1,0:T(8,128)(2,1)} %own_q.1, ...), custom_call_target="tpu_custom_call" | custom-call | flops 4000000000 | bytes 10485760 | tf_op jit(solution)/shard_map/pallas_call | solution.py:197
  18.9 0.0 copy-start.1
  18.9 1.0 %copy-done.1 = bf16[16,256,128]{2,1,0:T(8,128)(2,1)} copy-done((bf16[16,256,128]{2,1,0:T(8,128)(2,1)}, bf16[16,256,128]{2,1,0:T(8,128)(2,1)S(1)}, u32[]{:S(2)}) %copy-start.1) | copy-done | bytes 1048600
  19.8 25.7 %all_to_all.10.sums = bf16[32,136,128]{2,1,0:T(8,128)(2,1)S(1)} all-to-all(bf16[32,136,128]{2,1,0:T(8,128)(2,1)S(1)} %get-tuple-element.16), channel_id=1, replica_groups=mesh['zh'=4,'zl'=2,'x'=4,'y'=4,'c'=2] {'zl','x','y'}, dimensions={0} | all-to-all | bytes 2228224 | tf_op jit(solution)/shard_map/all_to_all | solution.py:211
  45.5 0.2 reduce_sum.12
  45.7 4.9 %collective-permute-start.3 = (bf16[136,128]{1,0:T(8,128)(2,1)S(1)}, bf16[136,128]{1,0:T(8,128)(2,1)S(1)}, u32[]{:S(2)}, u32[]{:S(2)}) collective-permute-start(bf16[136,128]{1,0:T(8,128)(2,1)S(1)} %reduce_sum.12), channel_id=1, source_target_pairs={{0,64},{64,128},{128,192},{1,65},{65,129},{129,193},{2,66},{66,130... | collective-permute-start | bytes 104456 | tf_op jit(solution)/shard_map/ppermute | solution.py:225
  50.6 6.1 %collective-permute-start.4 = (bf16[136,128]{1,0:T(8,128)(2,1)S(1)}, bf16[136,128]{1,0:T(8,128)(2,1)S(1)}, u32[]{:S(2)}, u32[]{:S(2)}) collective-permute-start(bf16[136,128]{1,0:T(8,128)(2,1)S(1)} %reduce_sum.12), channel_id=1, source_target_pairs={{0,128},{64,192},{1,129},{65,193},{2,130},{66,194},{3,131},{67,195... | collective-permute-start | bytes 104456 | tf_op jit(solution)/shard_map/ppermute | solution.py:225
  56.7 1.3 %collective-permute-start.5 = (bf16[136,128]{1,0:T(8,128)(2,1)S(1)}, bf16[136,128]{1,0:T(8,128)(2,1)S(1)}, u32[]{:S(2)}, u32[]{:S(2)}) collective-permute-start(bf16[136,128]{1,0:T(8,128)(2,1)S(1)} %reduce_sum.12), channel_id=1, source_target_pairs={{0,192},{1,193},{2,194},{3,195},{4,196},{5,197},{6,198},{7,199},{8... | collective-permute-start | bytes 104456 | tf_op jit(solution)/shard_map/ppermute | solution.py:225
  58.0 0.0 collective-permute-done.3.before_1
  58.0 0.0 collective-permute-done.4.before_2
  58.1 1.0 %collective-permute-done.5.before_3 = bf16[136,128]{1,0:T(8,128)(2,1)S(1)} collective-permute-done((bf16[136,128]{1,0:T(8,128)(2,1)S(1)}, bf16[136,128]{1,0:T(8,128)(2,1)S(1)}, u32[]{:S(2)}, u32[]{:S(2)}) %collective-permute-start.5) | collective-permute-done | bytes 34848 | tf_op jit(solution)/shard_map/ppermute | solution.py:225
  59.1 1.2 %shard_map.39 = bf16[32,136,128]{2,1,0:T(8,128)(2,1)} custom-call(bf16[136,128]{1,0:T(8,128)(2,1)S(1)} %collective-permute-done.3.before_1, bf16[136,128]{1,0:T(8,128)(2,1)S(1)} %collective-permute-done.4.before_2, bf16[136,128]{1,0:T(8,128)(2,1)S(1)} %collective-permute-done.5.before_3, bf16[32,136,128]{2,1,0:T(8,128)(2,1)S(1)} %all_to_all.10.sums), custom_call_target="tpu_custom_call" | custom-call | tf_op jit(solution)/shard_map/pallas_call | solution.py:228
  60.2 4.2 %all-to-all-start.1 = ((bf16[32,136,128]{2,1,0:T(8,128)(2,1)}), bf16[32,136,128]{2,1,0:T(8,128)(2,1)S(1)}, u32[]{:S(2)}, u32[]{:S(2)}) async-start(bf16[32,136,128]{2,1,0:T(8,128)(2,1)} %shard_map.39), calls=%async_computation.1 | async-start | bytes 2228224 | tf_op jit(solution)/shard_map/all_to_all | solution.py:233
  64.4 4.4 %shard_map.38 = (bf16[16,256,256]{2,1,0:T(8,128)(2,1)S(1)}, bf16[16,256,256]{2,1,0:T(8,128)(2,1)S(1)}) custom-call(s32[1]{0:T(128)} %bitcast.core_ref, bf16[3,128,4096]{2,1,0:T(8,128)(2,1)} %own_q.1, bf16[3,128,2048]{2,1,0:T(8,128)(2,1)S(1)} %collective-permute-done.other_k.other_v.other_q, ...), custom_call_target="tpu_custom_call" | custom-call | flops 8000000000 | bytes 20971520 | tf_op jit(solution)/shard_map/pallas_call | solution.py:212
  68.8 0.0 copy-start.3
  68.8 1.3 %copy-done.3 = bf16[16,256,256]{2,1,0:T(8,128)(2,1)} copy-done((bf16[16,256,256]{2,1,0:T(8,128)(2,1)}, bf16[16,256,256]{2,1,0:T(8,128)(2,1)S(1)}, u32[]{:S(2)}) %copy-start.3) | copy-done | bytes 2097176
  70.2 0.0 copy-start.4
  70.2 1.3 %copy-done.4 = bf16[16,256,256]{2,1,0:T(8,128)(2,1)} copy-done((bf16[16,256,256]{2,1,0:T(8,128)(2,1)}, bf16[16,256,256]{2,1,0:T(8,128)(2,1)S(1)}, u32[]{:S(2)}) %copy-start.4) | copy-done | bytes 2097176
  71.5 8.7 %all-to-all-done.1.state = bf16[32,136,128]{2,1,0:T(8,128)(2,1)S(1)} async-done(((bf16[32,136,128]{2,1,0:T(8,128)(2,1)}), bf16[32,136,128]{2,1,0:T(8,128)(2,1)S(1)}, u32[]{:S(2)}, u32[]{:S(2)}) %all-to-all-start.1) | async-done | bytes 1114144 | tf_op jit(solution)/shard_map/all_to_all | solution.py:233
  80.2 0.0 copy-start.2
  80.2 1.2 %copy-done.2 = bf16[16,256,128]{2,1,0:T(8,128)(2,1)S(1)} copy-done((bf16[16,256,128]{2,1,0:T(8,128)(2,1)S(1)}, bf16[16,256,128]{2,1,0:T(8,128)(2,1)}, u32[]{:S(2)}) %copy-start.2) | copy-done | bytes 1048600
  81.4 0.0 copy-start.5
  81.4 1.6 %copy-done.5 = bf16[16,256,256]{2,1,0:T(8,128)(2,1)S(1)} copy-done((bf16[16,256,256]{2,1,0:T(8,128)(2,1)S(1)}, bf16[16,256,256]{2,1,0:T(8,128)(2,1)}, u32[]{:S(2)}) %copy-start.5) | copy-done | bytes 2097176
  83.0 3.7 %shard_map.40 = (bf16[128,2048]{1,0:T(8,128)(2,1)S(1)}, bf16[128,2048]{1,0:T(8,128)(2,1)S(1)}) custom-call(s32[1]{0:T(128)} %bitcast.core_ref, bf16[16,256,256]{2,1,0:T(8,128)(2,1)S(1)} %copy-done.5, bf16[16,256,256]{2,1,0:T(8,128)(2,1)} %copy-done.3, bf16[16,256,128]{2,1,0:T(8,128)(2,1)S(1)} %copy-done.2, bf16[32,136,128]{2,1,0:T(8,128)(2,1)S(1)} %all-to-all-done.1.state), custom_call_target="tpu_custom_call" | custom-call | flops 4000000000 | bytes 8388608 | tf_op jit(solution)/shard_map/pallas_call | solution.py:234
  86.7 2.3 %collective-permute-start.6 = (bf16[128,2048]{1,0:T(8,128)(2,1)S(1)}, bf16[128,2048]{1,0:T(8,128)(2,1)S(1)}, u32[]{:S(2)}, u32[]{:S(2)}) collective-permute-start(bf16[128,2048]{1,0:T(8,128)(2,1)S(1)} %get-tuple-element.18), channel_id=1, source_target_pairs={{0,1},{1,0},{2,3},{3,2},{4,5},{5,4},{6,7},{7,6},{8,9},{9,8},{10,11... | collective-permute-start | bytes 1572872 | tf_op jit(solution)/shard_map/ppermute | solution.py:178
  89.0 1.5 %collective-permute-done.6 = bf16[128,2048]{1,0:T(8,128)(2,1)S(1)} collective-permute-done((bf16[128,2048]{1,0:T(8,128)(2,1)S(1)}, bf16[128,2048]{1,0:T(8,128)(2,1)S(1)}, u32[]{:S(2)}, u32[]{:S(2)}) %collective-permute-start.6) | collective-permute-done | bytes 524320 | tf_op jit(solution)/shard_map/ppermute | solution.py:178
  90.5 0.1 broadcast_select_fusion.1
  90.6 1.1 %pad_maximum_fusion = bf16[128,4096]{1,0:T(8,128)(2,1)} fusion(bf16[128,2048]{1,0:T(8,128)(2,1)S(1)} %get-tuple-element.22, bf16[128,2048]{1,0:T(8,128)(2,1)S(1)} %get-tuple-element.21), kind=kLoop, calls=%fused_computation | loop fusion | flops 2097152 | bytes 2097152 | tf_op jit(solution)/shard_map/concatenate | solution.py:246
Async XLA Ops:
  0.0 12.1 %copy-start = (f32[3,4,4096]{2,1,0:T(4,128)S(1)}, f32[3,4,4096]{2,1,0:T(4,128)}, u32[]{:S(2)}) copy-start(f32[3,4,4096]{2,1,0:T(4,128)} %taps_q.1) | copy-start | bytes 589828
  1.6 10.5 %collective-permute-start = (bf16[3,128,2048]{2,1,0:T(8,128)(2,1)S(1)}, bf16[3,128,2048]{2,1,0:T(8,128)(2,1)S(1)}, u32[]{:S(2)}, u32[]{:S(2)}) collective-permute-start(bf16[3,128,2048]{2,1,0:T(8,128)(2,1)S(1)} %constant_dynamic-slice_fusion), channel_id=1, source_target_pairs={{0,1},{1,0},{2,3},{3,2},{4,5},{5,4},{6,7},{7,6},{8,9},{9,8},{10,11... | collective-permute-start | bytes 4718600 | tf_op jit(solution)/shard_map/ppermute | solution.py:178
  5.8 4.6 %collective-permute-start.1 = (bf16[3,8,2048]{2,1,0:T(8,128)(2,1)S(1)}, bf16[3,8,2048]{2,1,0:T(8,128)(2,1)S(1)}, u32[]{:S(2)}, u32[]{:S(2)}) collective-permute-start(bf16[3,8,2048]{2,1,0:T(8,128)(2,1)S(1)} %get-tuple-element.20), channel_id=1, source_target_pairs={{1,2},{3,4},{5,6},{7,8},{9,10},{11,12},{13,14},{15,16},{17,18},{19... | collective-permute-start | bytes 294920 | tf_op jit(solution)/shard_map/ppermute | solution.py:190
  7.2 4.8 %collective-permute-start.2 = (bf16[3,8,2048]{2,1,0:T(8,128)(2,1)S(1)}, bf16[3,8,2048]{2,1,0:T(8,128)(2,1)S(1)}, u32[]{:S(2)}, u32[]{:S(2)}) collective-permute-start(bf16[3,8,2048]{2,1,0:T(8,128)(2,1)S(1)} %get-tuple-element.19), channel_id=1, source_target_pairs={{1,3},{3,5},{5,7},{7,9},{9,11},{11,13},{13,15},{15,17},{17,19},{19... | collective-permute-start | bytes 294920 | tf_op jit(solution)/shard_map/ppermute | solution.py:190
  18.9 1.0 %copy-start.1 = (bf16[16,256,128]{2,1,0:T(8,128)(2,1)}, bf16[16,256,128]{2,1,0:T(8,128)(2,1)S(1)}, u32[]{:S(2)}) copy-start(bf16[16,256,128]{2,1,0:T(8,128)(2,1)S(1)} %get-tuple-element.15.values) | copy-start | bytes 3145732
  45.7 12.3 %collective-permute-start.3 = (bf16[136,128]{1,0:T(8,128)(2,1)S(1)}, bf16[136,128]{1,0:T(8,128)(2,1)S(1)}, u32[]{:S(2)}, u32[]{:S(2)}) collective-permute-start(bf16[136,128]{1,0:T(8,128)(2,1)S(1)} %reduce_sum.12), channel_id=1, source_target_pairs={{0,64},{64,128},{128,192},{1,65},{65,129},{129,193},{2,66},{66,130... | collective-permute-start | bytes 104456 | tf_op jit(solution)/shard_map/ppermute | solution.py:225
  50.6 7.4 %collective-permute-start.4 = (bf16[136,128]{1,0:T(8,128)(2,1)S(1)}, bf16[136,128]{1,0:T(8,128)(2,1)S(1)}, u32[]{:S(2)}, u32[]{:S(2)}) collective-permute-start(bf16[136,128]{1,0:T(8,128)(2,1)S(1)} %reduce_sum.12), channel_id=1, source_target_pairs={{0,128},{64,192},{1,129},{65,193},{2,130},{66,194},{3,131},{67,195... | collective-permute-start | bytes 104456 | tf_op jit(solution)/shard_map/ppermute | solution.py:225
  56.7 2.3 %collective-permute-start.5 = (bf16[136,128]{1,0:T(8,128)(2,1)S(1)}, bf16[136,128]{1,0:T(8,128)(2,1)S(1)}, u32[]{:S(2)}, u32[]{:S(2)}) collective-permute-start(bf16[136,128]{1,0:T(8,128)(2,1)S(1)} %reduce_sum.12), channel_id=1, source_target_pairs={{0,192},{1,193},{2,194},{3,195},{4,196},{5,197},{6,198},{7,199},{8... | collective-permute-start | bytes 104456 | tf_op jit(solution)/shard_map/ppermute | solution.py:225
  60.2 19.9 %all-to-all-start.1 = ((bf16[32,136,128]{2,1,0:T(8,128)(2,1)}), bf16[32,136,128]{2,1,0:T(8,128)(2,1)S(1)}, u32[]{:S(2)}, u32[]{:S(2)}) async-start(bf16[32,136,128]{2,1,0:T(8,128)(2,1)} %shard_map.39), calls=%async_computation.1 | async-start | bytes 2228224 | tf_op jit(solution)/shard_map/all_to_all | solution.py:233
  68.8 1.3 %copy-start.3 = (bf16[16,256,256]{2,1,0:T(8,128)(2,1)}, bf16[16,256,256]{2,1,0:T(8,128)(2,1)S(1)}, u32[]{:S(2)}) copy-start(bf16[16,256,256]{2,1,0:T(8,128)(2,1)S(1)} %get-tuple-element.14.query_map) | copy-start | bytes 6291460
  70.2 1.3 %copy-start.4 = (bf16[16,256,256]{2,1,0:T(8,128)(2,1)}, bf16[16,256,256]{2,1,0:T(8,128)(2,1)S(1)}, u32[]{:S(2)}) copy-start(bf16[16,256,256]{2,1,0:T(8,128)(2,1)S(1)} %get-tuple-element.13.scores) | copy-start | bytes 6291460
  80.2 1.2 %copy-start.2 = (bf16[16,256,128]{2,1,0:T(8,128)(2,1)S(1)}, bf16[16,256,128]{2,1,0:T(8,128)(2,1)}, u32[]{:S(2)}) copy-start(bf16[16,256,128]{2,1,0:T(8,128)(2,1)} %copy-done.1) | copy-start | bytes 3145732
  81.4 1.6 %copy-start.5 = (bf16[16,256,256]{2,1,0:T(8,128)(2,1)S(1)}, bf16[16,256,256]{2,1,0:T(8,128)(2,1)}, u32[]{:S(2)}) copy-start(bf16[16,256,256]{2,1,0:T(8,128)(2,1)} %copy-done.4) | copy-start | bytes 6291460
  86.7 3.8 %collective-permute-start.6 = (bf16[128,2048]{1,0:T(8,128)(2,1)S(1)}, bf16[128,2048]{1,0:T(8,128)(2,1)S(1)}, u32[]{:S(2)}, u32[]{:S(2)}) collective-permute-start(bf16[128,2048]{1,0:T(8,128)(2,1)S(1)} %get-tuple-element.18), channel_id=1, source_target_pairs={{0,1},{1,0},{2,3},{3,2},{4,5},{5,4},{6,7},{7,6},{8,9},{9,8},{10,11... | collective-permute-start | bytes 1572872 | tf_op jit(solution)/shard_map/ppermute | solution.py:178

commit v2 on v1

v2 whole, which is shorter than its diff:
```python
import functools

import jax
import jax.numpy as jnp
from jax import lax
from jax.experimental import pallas as pl
from jax.experimental.pallas import tpu as pltpu
from jax.sharding import Mesh
from jax.sharding import PartitionSpec as P

H = 32
DH = 128
M = 256
KC = 4
D = H * DH

CORES = 2
HEADS = H // CORES
COLS = HEADS * DH
ROWS = 128
CHUNK = CORES * ROWS
RIM = 8
PIECES = 2 * HEADS
STATE_ROWS = DH + 8
GROUP = 4
WIDE = GROUP * DH
STEPS = HEADS // GROUP
FEATURE_SCALE = DH ** (-0.25)
NORM_SCALE = 0.5 * FEATURE_SCALE * FEATURE_SCALE

AXES = ("zh", "zl", "x", "y", "c")
SIZES = (4, 2, 4, 4, 2)
PLANE = ("zl", "x", "y")

f32 = jnp.float32
bf16 = jnp.bfloat16
NT = (((1,), (1,)), ((), ()))


def dot(a, b):
    return jnp.dot(a, b, preferred_element_type=f32)


def dot_nt(a, b):
    return lax.dot_general(a, b, NT, preferred_element_type=f32)


def fill(core, own, other, rim_a, rim_b, rows):
    rows[0:RIM, :] = rim_a[0].astype(f32) + rim_b[0].astype(f32)
    rows[pl.ds(pl.multiple_of(RIM + core * ROWS, 8), ROWS), :] = own[0].astype(f32)
    rows[pl.ds(pl.multiple_of(RIM + (1 - core) * ROWS, 8), ROWS), :] = other[0].astype(f32)


def convolve(rows, taps, head):
    cols = slice(head * DH, (head + 1) * DH)
    summed = taps[0, 0:1, cols] * rows[RIM : RIM + CHUNK, cols]
    for j in range(1, KC):
        summed = summed + taps[0, j : j + 1, cols] * rows[RIM - j : RIM - j + CHUNK, cols]
    return summed.astype(bf16)


def keys_kernel(
    core_ref, own, other, rim_a, rim_b, taps, omega,
    state, key_map, values, rows_k, rows_v, maps, convolved, sems,
):
    core = core_ref[0]
    ones = jnp.ones((M, M), bf16)

    def copies(group):
        heads = pl.ds(group * GROUP, GROUP)
        return (
            pltpu.make_async_copy(maps.at[heads], key_map.at[heads], sems.at[0, group]),
            pltpu.make_async_copy(convolved.at[heads], values.at[heads], sems.at[1, group]),
        )

    def one(group, carried):
        cols = columns(group * WIDE, WIDE)
        for which, rows in ((0, rows_k), (1, rows_v)):
            fill(
                core,
                own.at[pl.ds(which, 1), :, cols],
                other.at[pl.ds(which, 1), :, cols],
                rim_a.at[pl.ds(which + 1, 1), :, cols],
                rim_b.at[pl.ds(which + 1, 1), :, cols],
                rows,
            )
        for part in range(GROUP):
            head = group * GROUP + part
            k = convolve(rows_k, taps.at[pl.ds(1, 1), :, cols], part)
            v = convolve(rows_v, taps.at[pl.ds(2, 1), :, cols], part)
            k_wide = k.astype(f32)
            square = k_wide * k_wide
            upper = square.astype(bf16)
            lower = (square - upper.astype(f32)).astype(bf16)
            norm = dot(jnp.concatenate([upper, lower], axis=1), ones)
            mapped = jnp.exp(dot(k, omega[head]) * FEATURE_SCALE - norm * NORM_SCALE).astype(bf16)
            maps[head] = mapped
            convolved[head] = v
            extended = jnp.concatenate([v.T, jnp.ones((16, CHUNK), bf16)], axis=0)
            sums = dot(extended, mapped)[:STATE_ROWS].astype(bf16)
            state[2 * head] = sums[:, : M // 2]
            state[2 * head + 1] = sums[:, M // 2 :]
        for copy in copies(group):
            copy.start()
        return carried

    lax.fori_loop(0, STEPS, one, 0)
    for group in range(STEPS):
        for copy in copies(group):
            copy.wait()


def scores_kernel(
    core_ref, own_q, other_q, rim_qa, rim_qb, taps_q, omega, key_map, query_map, scores, rows_q
):
    core = core_ref[0]
    fill(core, own_q, other_q, rim_qa, rim_qb, rows_q)
    causal = lax.broadcasted_iota(jnp.int32, (CHUNK, CHUNK), 0) >= lax.broadcasted_iota(
        jnp.int32, (CHUNK, CHUNK), 1
    )
    for head in range(GROUP):
        q = convolve(rows_q, taps_q, head)
        mapped = jnp.exp(dot(q, omega[head]) * FEATURE_SCALE).astype(bf16)
        query_map[head] = mapped
        scores[head] = jnp.where(causal, dot_nt(mapped, key_map[head]), 0.0).astype(bf16)


def total_kernel(sums, out):
    total = sums[0].astype(f32)
    for i in range(1, PIECES):
        total = total + sums[i].astype(f32)
    out[...] = total.astype(bf16)


def prefix_kernel(before_1, before_2, before_3, sums, out):
    running = before_1[...].astype(f32) + before_2[...].astype(f32) + before_3[...].astype(f32)
    for i in range(PIECES):
        out[i] = running.astype(bf16)
        running = running + sums[i].astype(f32)


def attend_rows(rows, scores, query_map, values, state, put):
    ones = jnp.ones((CHUNK, DH), bf16)

    def one(head, carried):
        prior = jnp.concatenate([state[2 * head], state[2 * head + 1]], axis=1)
        total = jnp.broadcast_to(prior[DH : DH + 1], (DH, M))
        prior = jnp.concatenate([prior[:DH], total], axis=0)
        both = dot(scores[head, rows, :], jnp.concatenate([values[head], ones], axis=1))
        both = both + dot_nt(query_map[head, rows, :], prior)
        put(head, (both[:, :DH] / both[:, DH:]).astype(bf16))
        return carried

    lax.fori_loop(0, HEADS, one, 0, unroll=4)


def columns(start, size):
    return pl.ds(pl.multiple_of(start, DH), size)


def attend_other_kernel(core_ref, scores, query_map, values, state, out):
    start = pl.multiple_of((1 - core_ref[0]) * ROWS, ROWS)

    def put(head, block):
        out[:, columns(head * DH, DH)] = block

    attend_rows(pl.ds(start, ROWS), scores, query_map, values, state, put)


def attend_own_kernel(core_ref, scores, query_map, values, state, out, block_rows, sem):
    core = core_ref[0]
    start = pl.multiple_of(core * ROWS, ROWS)

    def put(head, block):
        block_rows[:, columns(head * DH, DH)] = block

    attend_rows(pl.ds(start, ROWS), scores, query_map, values, state, put)
    copy = pltpu.make_async_copy(block_rows, out.at[:, columns(core * COLS, COLS)], sem)
    copy.start()
    copy.wait()


def finish_kernel(core_ref, arrived, partial, out, sem):
    copy = pltpu.make_async_copy(arrived, out.at[:, columns((1 - core_ref[0]) * COLS, COLS)], sem)
    copy.start()
    copy.wait()


def run_copies(pairs, sems):
    copies = [
        pltpu.make_async_copy(source, target, sems.at[i])
        for i, (source, target) in enumerate(pairs)
    ]
    for copy in copies:
        copy.start()
    for copy in copies:
        copy.wait()


def split_kernel(core_ref, projected, rim_a, rim_b, sent, sent_q, sems):
    cols = columns((1 - core_ref[0]) * COLS, COLS)
    last = pl.ds(ROWS - RIM, RIM)
    pairs = [
        (projected.at[:, last, pl.ds(0, COLS)], rim_a),
        (projected.at[:, last, pl.ds(COLS, COLS)], rim_b),
        (projected.at[pl.ds(1, 2), :, cols], sent),
        (projected.at[pl.ds(0, 1), :, cols], sent_q),
    ]
    run_copies(pairs, sems)


def fetch_kernel(core_ref, projected, taps, omega, own, own_taps, own_omega, sems):
    cols = columns(core_ref[0] * COLS, COLS)
    pairs = [
        (projected.at[pl.ds(1, 2), :, cols], own),
        (taps.at[:, :, cols], own_taps),
        (omega.at[pl.ds(core_ref[0] * HEADS, HEADS)], own_omega),
    ]
    run_copies(pairs, sems)


def spec(shape, index):
    return pl.BlockSpec(shape, index)


def own_spec(which):
    return spec((1, ROWS, WIDE), lambda i, core: (which, 0, core[0] * STEPS + i))


def other_spec(which):
    return spec((1, ROWS, WIDE), lambda i, core: (which, 0, i))


def rim_spec(which):
    return spec((1, RIM, WIDE), lambda i, core: (which, 0, i))


def taps_spec(which):
    return spec((1, KC, WIDE), lambda i, core: (which, 0, core[0] * STEPS + i))


OMEGA_SPEC = spec((GROUP, DH, M), lambda i, core: (core[0] * STEPS + i, 0, 0))


def head_spec(*dims):
    return spec((GROUP,) + dims, lambda i, core: (i,) + (0,) * len(dims))


STATE_SPEC = spec((2 * GROUP, STATE_ROWS, M // 2), lambda i, core: (i, 0, 0))
SCALAR = pl.BlockSpec(memory_space=pltpu.SMEM)
WHOLE = pl.BlockSpec(memory_space=pltpu.VMEM)
ANYWHERE = pl.BlockSpec(memory_space=pl.ANY)


def chip(*dims):
    return pltpu.VMEM(dims, bf16)


def main(*dims):
    return pltpu.HBM(dims, bf16)


def in_chip(*arrays):
    return [pltpu.with_memory_space_constraint(a, pltpu.VMEM) for a in arrays]


def in_main(*arrays):
    return [pltpu.with_memory_space_constraint(a, pltpu.HBM) for a in arrays]


def small_call(kernel, in_specs, out_specs, out_shape, scratch, flops, moved, aliases=None):
    return pl.pallas_call(
        kernel,
        in_specs=in_specs,
        out_specs=out_specs,
        out_shape=out_shape,
        scratch_shapes=scratch,
        input_output_aliases=aliases or {},
        compiler_params=pltpu.CompilerParams(vmem_limit_bytes=16 * 2**20),
        cost_estimate=pl.CostEstimate(flops=flops, bytes_accessed=moved, transcendentals=0),
    )


def call(kernel, in_specs, out_specs, out_shape, scratch, flops, moved):
    return pl.pallas_call(
        kernel,
        grid_spec=pltpu.PrefetchScalarGridSpec(
            num_scalar_prefetch=1,
            grid=(STEPS,),
            in_specs=in_specs,
            out_specs=out_specs,
            scratch_shapes=scratch,
        ),
        out_shape=out_shape,
        compiler_params=pltpu.CompilerParams(
            dimension_semantics=("arbitrary",), vmem_limit_bytes=20 * 2**20
        ),
        cost_estimate=pl.CostEstimate(flops=flops, bytes_accessed=moved, transcendentals=0),
    )


def swap(array):
    return lax.ppermute(array, "c", [(0, 1), (1, 0)])


def per_device(projected, conv_filter, frequencies):
    core = lax.axis_index("c").astype(jnp.int32)
    cores = core.reshape(1)
    projected, conv_filter, frequencies = in_main(projected, conv_filter, frequencies)
    *halves, sent, sent_q = small_call(
        split_kernel,
        [SCALAR, ANYWHERE],
        [WHOLE] * 4,
        [chip(3, RIM, COLS), chip(3, RIM, COLS), chip(2, ROWS, COLS), chip(1, ROWS, COLS)],
        [pltpu.SemaphoreType.DMA((4,))],
        flops=0,
        moved=3 * 2**20,
    )(cores, projected)
    count = 256 // CORES
    rims = [
        lax.ppermute(
            halves[to], AXES, [(2 * i + 1, 2 * (i + 1) + to) for i in range(count - 1)]
        )
        for to in range(CORES)
    ]
    other, other_q = swap(sent), swap(sent_q)
    fetched = small_call(
        fetch_kernel,
        [SCALAR] + [ANYWHERE] * 3,
        [WHOLE] * 3,
        [chip(2, ROWS, COLS), pltpu.VMEM((3, KC, COLS), f32), chip(HEADS, DH, M)],
        [pltpu.SemaphoreType.DMA((3,))],
        flops=0,
        moved=5 * 2**20,
    )(cores, projected, conv_filter, frequencies)
    own, own_taps, own_omega, other, *rims = in_chip(*fetched, other, *rims)
    state, key_map, values = small_call(
        keys_kernel,
        [SCALAR] + [WHOLE] * 6,
        [WHOLE, ANYWHERE, ANYWHERE],
        [chip(PIECES, STATE_ROWS, M // 2), main(HEADS, CHUNK, M), main(HEADS, CHUNK, DH)],
        [pltpu.VMEM((RIM + CHUNK, WIDE), f32)] * 2
        + [pltpu.VMEM((HEADS, CHUNK, M), bf16), pltpu.VMEM((HEADS, CHUNK, DH), bf16)]
        + [pltpu.SemaphoreType.DMA((2, STEPS))],
        flops=4 * 10**9,
        moved=10 * 2**20,
    )(cores, own, other, *rims, own_taps, own_omega)
    gathered = lax.all_to_all(state, PLANE, 0, 0, tiled=True)
    key_map, values = in_main(key_map, values)
    query_map, scores = call(
        scores_kernel,
        [own_spec(0), other_spec(0), rim_spec(0), rim_spec(0), taps_spec(0), OMEGA_SPEC]
        + [head_spec(CHUNK, M)],
        [head_spec(CHUNK, M), head_spec(CHUNK, CHUNK)],
        [main(HEADS, CHUNK, M), main(HEADS, CHUNK, CHUNK)],
        [pltpu.VMEM((RIM + CHUNK, WIDE), f32)],
        flops=8 * 10**9,
        moved=20 * 2**20,
    )(cores, projected, other_q, rims[0], rims[1], conv_filter, frequencies, key_map)
    gathered, query_map, scores = lax.optimization_barrier((gathered, query_map, scores))
    total = small_call(
        total_kernel, [WHOLE], WHOLE, chip(STATE_ROWS, M // 2), [], flops=10**6, moved=2**20
    )(*in_chip(gathered))
    planes = SIZES[0]
    before = [
        lax.ppermute(total, "zh", [(i, i + by) for i in range(planes - by)])
        for by in range(1, planes)
    ]
    prior = small_call(
        prefix_kernel, [WHOLE] * 4, WHOLE, chip(PIECES, STATE_ROWS, M // 2), [],
        flops=10**6, moved=2 * 2**20,
    )(*in_chip(*before, gathered))
    prior = lax.all_to_all(prior, PLANE, 0, 0, tiled=True)
    operands = in_chip(scores, query_map, values, prior)
    attended = small_call(
        attend_other_kernel, [SCALAR] + [WHOLE] * 4, WHOLE, chip(ROWS, COLS), [],
        flops=2 * 10**9, moved=4 * 2**20,
    )(cores, *operands)
    arrived = swap(attended)
    partial = small_call(
        attend_own_kernel, [SCALAR] + [WHOLE] * 4, ANYWHERE, main(ROWS, D),
        [pltpu.VMEM((ROWS, COLS), bf16), pltpu.SemaphoreType.DMA],
        flops=2 * 10**9, moved=4 * 2**20,
    )(cores, *operands)
    return small_call(
        finish_kernel, [SCALAR, WHOLE, ANYWHERE], ANYWHERE, main(ROWS, D),
        [pltpu.SemaphoreType.DMA], flops=0, moved=2**20, aliases={2: 0},
    )(cores, *in_chip(arrived), *in_main(partial))


def solution(mesh):
    devices = Mesh(mesh.devices.reshape(SIZES), AXES)
    placed = (P(None, AXES, None), P(), P())
    return jax.shard_map(
        per_device, mesh=devices, in_specs=placed, out_specs=P(AXES, None), check_vma=False
    )
```

time: 92.3 us -> 86 us (0.932)
  local copies, waits for them, and re-layouts: 8.95 us -> 0.01 us
  starting transfers between devices: 26.7 us -> 31.1 us
  Pallas kernels: 16.1 us -> 20.5 us
  blocking collectives: 25.7 us -> 22.5 us
  waiting for transfers between devices: 12.8 us -> 11.2 us
  other arithmetic: 1.3 us -> 0 us
    unnamed x12 -> x6, local copies, waits for them, and re-layouts: 6.45 us -> 0.01 us
    all_to_all x1, starting transfers between devices: 4.17 us -> 8.62 us  [per_device(): gathered = lax.all_to_all(state, PLANE, 0, 0, tiled=True)]
    pallas_call x3 -> x8, Pallas kernels: 11.7 us -> 15 us  [the longest x1 6.61 us: per_device(): small_call(keys_kernel, [SCALAR] + [WHOLE] * 6, [WHOLE, ANYWHERE, ANYWHER...]
    all_to_all x1, blocking collectives: 25.7 us -> 22.5 us  [per_device(): prior = lax.all_to_all(prior, PLANE, 0, 0, tiled=True)]
    ppermute x2, waiting for transfers between devices: 1.61 us -> 0.01 us  [per_device(): lax.ppermute(halves[to], AXES, [(2 * i + 1, 2 * (i + 1) + to) for i in ra...]
    dynamic_slice x1 -> x0, local copies, waits for them, and re-layouts: 1.55 us -> none  [per_device(): sent = lax.dynamic_slice_in_dim(projected, (1 - core) * COLS, COLS, 2)]
    pallas_call x1, Pallas kernels: 4.41 us -> 5.53 us  [per_device(): call(scores_kernel, [own_spec(0), other_spec(0), rim_spec(0), rim_spec(0)...]
    concatenate x1 -> x0, other arithmetic: 1.06 us -> none  [per_device(): return jnp.concatenate([first, second], axis=1)]
  transfers between devices with their start and end apart: 8 -> 9, of which waited for: 4 -> 3; matrix products, arithmetic and copies ran while one was open for 1% -> 0% of each run, Pallas kernels for 5% -> 11%
where the time goes in v2:
time: 86 us; the launch traced here: 85.6 us
  starting transfers between devices  31.1 us (36%)
  blocking collectives  22.5 us (26%)
  Pallas kernels  20.5 us (24%)
  waiting for transfers between devices  11.2 us (13%)
    all_to_all x1, blocking collectives, per_device(): prior = lax.all_to_all(prior, PLANE, 0, 0, tiled=True)  22.5 us
    ppermute x3, starting transfers between devices, per_device(): lax.ppermute(total, 'zh', [(i, i + by) for i in range(planes - by)])  13 us
    all_to_all x1, starting transfers between devices, per_device(): gathered = lax.all_to_all(state, PLANE, 0, 0, tiled=True)  8.62 us
    all_to_all x1, waiting for transfers between devices, per_device(): gathered = lax.all_to_all(state, PLANE, 0, 0, tiled=True)  8.32 us
    pallas_call x1, Pallas kernels, per_device(): small_call(keys_kernel, [SCALAR] + [WHOLE] * 6, [WHOLE, ANYWHERE, ANYWHER...  6.61 us
    pallas_call x1, Pallas kernels, per_device(): call(scores_kernel, [own_spec(0), other_spec(0), rim_spec(0), rim_spec(0)...  5.53 us
    ppermute x3, starting transfers between devices, swap(): return lax.ppermute(array, 'c', [(0, 1), (1, 0)])  4.96 us
    ppermute x2, starting transfers between devices, per_device(): lax.ppermute(halves[to], AXES, [(2 * i + 1, 2 * (i + 1) + to) for i in ra...  4.57 us
  transfers between devices with their start and end apart: 9, of which 3 were waited for; matrix products, arithmetic and copies ran while one was open for 0% of the time, Pallas kernels for 11%

profile of v2, /device:TPU:1, one launch (start us, length us, event | category | flops | bytes accessed | tf_op | source)
XLA Modules:
  0.0 85.6 jit_solution(6898033133633207349)
XLA Ops:
  0.0 1.5 %shard_map.38 = (bf16[3,8,2048]{2,1,0:T(8,128)(2,1)S(1)}, bf16[3,8,2048]{2,1,0:T(8,128)(2,1)S(1)}, bf16[2,128,2048]{2,1,0:T(8,128)(2,1)S(1)}, bf16[1,128,2048]{2,1,0:T(8,128)(2,1)S(1)}) custom-call(s32[1]{0:T(128)} %bitcast.core_ref, bf16[3,128,4096]{2,1,0:T(8,128)(2,1)} %own_q.1), custom_call_target="tpu_custom_call" | custom-call | bytes 3145728 | tf_op jit(solution)/shard_map/pallas_call | solution.py:310
  1.5 3.3 %collective-permute-start = (bf16[2,128,2048]{2,1,0:T(8,128)(2,1)S(1)}, bf16[2,128,2048]{2,1,0:T(8,128)(2,1)S(1)}, u32[]{:S(2)}, u32[]{:S(2)}) collective-permute-start(bf16[2,128,2048]{2,1,0:T(8,128)(2,1)S(1)} %get-tuple-element.21), channel_id=1, source_target_pairs={{0,1},{1,0},{2,3},{3,2},{4,5},{5,4},{6,7},{7,6},{8,9},{9,8},{10,11... | collective-permute-start | bytes 3145736 | tf_op jit(solution)/shard_map/ppermute | solution.py:303
  4.8 1.4 %collective-permute-start.1 = (bf16[3,8,2048]{2,1,0:T(8,128)(2,1)S(1)}, bf16[3,8,2048]{2,1,0:T(8,128)(2,1)S(1)}, u32[]{:S(2)}, u32[]{:S(2)}) collective-permute-start(bf16[3,8,2048]{2,1,0:T(8,128)(2,1)S(1)} %get-tuple-element.22), channel_id=1, source_target_pairs={{1,2},{3,4},{5,6},{7,8},{9,10},{11,12},{13,14},{15,16},{17,18},{19... | collective-permute-start | bytes 294920 | tf_op jit(solution)/shard_map/ppermute | solution.py:321
  6.2 3.2 %collective-permute-start.2 = (bf16[3,8,2048]{2,1,0:T(8,128)(2,1)S(1)}, bf16[3,8,2048]{2,1,0:T(8,128)(2,1)S(1)}, u32[]{:S(2)}, u32[]{:S(2)}) collective-permute-start(bf16[3,8,2048]{2,1,0:T(8,128)(2,1)S(1)} %get-tuple-element.23), channel_id=1, source_target_pairs={{1,3},{3,5},{5,7},{7,9},{9,11},{11,13},{13,15},{15,17},{17,19},{19... | collective-permute-start | bytes 294920 | tf_op jit(solution)/shard_map/ppermute | solution.py:321
  9.4 1.6 %shard_map.37 = (bf16[2,128,2048]{2,1,0:T(8,128)(2,1)S(1)}, f32[3,4,2048]{2,1,0:T(4,128)S(1)}, bf16[16,128,256]{2,1,0:T(8,128)(2,1)S(1)}) custom-call(s32[1]{0:T(128)} %bitcast.core_ref, bf16[3,128,4096]{2,1,0:T(8,128)(2,1)} %own_q.1, f32[3,4,4096]{2,1,0:T(4,128)} %taps_q.1, bf16[32,128,256]{2,1,0:T(8,128)(2,1)} %omega.3), custom_call_target="tpu_custom_call" | custom-call | bytes 5242880 | tf_op jit(solution)/shard_map/pallas_call | solution.py:327
  11.0 0.0 collective-permute-done.1.rim_a.rim_qa
  11.0 0.0 collective-permute-done.2.rim_b.rim_qb
  11.1 0.0 collective-permute-done.other
  11.1 6.6 %shard_map.39 = (bf16[32,136,128]{2,1,0:T(8,128)(2,1)}, bf16[16,256,256]{2,1,0:T(8,128)(2,1)}, bf16[16,256,128]{2,1,0:T(8,128)(2,1)}) custom-call(s32[1]{0:T(128)} %bitcast.core_ref, bf16[2,128,2048]{2,1,0:T(8,128)(2,1)S(1)} %get-tuple-element.20.own, bf16[2,128,2048]{2,1,0:T(8,128)(2,1)S(1)} %collective-permute-done.other, ...), custom_call_target="tpu_custom_call" | custom-call | flops 4000000000 | bytes 10485760 | tf_op jit(solution)/shard_map/pallas_call | solution.py:337
  17.7 8.6 %all-to-all-start = ((bf16[32,136,128]{2,1,0:T(8,128)(2,1)}), bf16[32,136,128]{2,1,0:T(8,128)(2,1)S(1)}, u32[]{:S(2)}, u32[]{:S(2)}) async-start(bf16[32,136,128]{2,1,0:T(8,128)(2,1)} %get-tuple-element.26), calls=%async_computation | async-start | bytes 2228224 | tf_op jit(solution)/shard_map/all_to_all | solution.py:348
  26.3 0.1 collective-permute-start.3
  26.4 1.9 %collective-permute-done.3.other_q = bf16[1,128,2048]{2,1,0:T(8,128)(2,1)S(1)} collective-permute-done((bf16[1,128,2048]{2,1,0:T(8,128)(2,1)S(1)}, bf16[1,128,2048]{2,1,0:T(8,128)(2,1)S(1)}, u32[]{:S(2)}, u32[]{:S(2)}) %collective-permute-start.3) | collective-permute-done | bytes 524320 | tf_op jit(solution)/shard_map/ppermute | solution.py:303
  28.3 5.5 %shard_map.40 = (bf16[16,256,256]{2,1,0:T(8,128)(2,1)}, bf16[16,256,256]{2,1,0:T(8,128)(2,1)}) custom-call(s32[1]{0:T(128)} %bitcast.core_ref, bf16[3,128,4096]{2,1,0:T(8,128)(2,1)} %own_q.1, bf16[1,128,2048]{2,1,0:T(8,128)(2,1)S(1)} %collective-permute-done.3.other_q, bf16[3,8,2048]{2,1,0:T(8,128)(2,1)S(1)} %collective-permute-done.1.rim_a.rim_qa, ...), custom_call_target="tpu_custom_call" | custom-call | flops 8000000000 | bytes 20971520 | tf_op jit(solution)/shard_map/pallas_call | solution.py:350
  33.8 8.3 %all-to-all-done.sums = bf16[32,136,128]{2,1,0:T(8,128)(2,1)S(1)} async-done(((bf16[32,136,128]{2,1,0:T(8,128)(2,1)}), bf16[32,136,128]{2,1,0:T(8,128)(2,1)S(1)}, u32[]{:S(2)}, u32[]{:S(2)}) %all-to-all-start) | async-done | bytes 1114144 | tf_op jit(solution)/shard_map/all_to_all | solution.py:348
  42.2 0.0 copy-start.2
  42.2 0.2 shard_map.41
  42.3 0.0 copy-start
  42.3 0.0 copy-start.1
  42.3 7.7 %collective-permute-start.6 = (bf16[136,128]{1,0:T(8,128)(2,1)S(1)}, bf16[136,128]{1,0:T(8,128)(2,1)S(1)}, u32[]{:S(2)}, u32[]{:S(2)}) collective-permute-start(bf16[136,128]{1,0:T(8,128)(2,1)S(1)} %shard_map.41), channel_id=1, source_target_pairs={{0,192},{1,193},{2,194},{3,195},{4,196},{5,197},{6,198},{7,199},{8... | collective-permute-start | bytes 104456 | tf_op jit(solution)/shard_map/ppermute | solution.py:366
  50.0 2.8 %collective-permute-start.5 = (bf16[136,128]{1,0:T(8,128)(2,1)S(1)}, bf16[136,128]{1,0:T(8,128)(2,1)S(1)}, u32[]{:S(2)}, u32[]{:S(2)}) collective-permute-start(bf16[136,128]{1,0:T(8,128)(2,1)S(1)} %shard_map.41), channel_id=1, source_target_pairs={{0,128},{64,192},{1,129},{65,193},{2,130},{66,194},{3,131},{67,195... | collective-permute-start | bytes 104456 | tf_op jit(solution)/shard_map/ppermute | solution.py:366
  52.8 2.5 %collective-permute-start.4 = (bf16[136,128]{1,0:T(8,128)(2,1)S(1)}, bf16[136,128]{1,0:T(8,128)(2,1)S(1)}, u32[]{:S(2)}, u32[]{:S(2)}) collective-permute-start(bf16[136,128]{1,0:T(8,128)(2,1)S(1)} %shard_map.41), channel_id=1, source_target_pairs={{0,64},{64,128},{128,192},{1,65},{65,129},{129,193},{2,66},{66,130... | collective-permute-start | bytes 104456 | tf_op jit(solution)/shard_map/ppermute | solution.py:366
  55.3 0.0 collective-permute-done.6.before_3
  55.3 0.0 collective-permute-done.5.before_2
  55.3 1.0 %collective-permute-done.4.before_1 = bf16[136,128]{1,0:T(8,128)(2,1)S(1)} collective-permute-done((bf16[136,128]{1,0:T(8,128)(2,1)S(1)}, bf16[136,128]{1,0:T(8,128)(2,1)S(1)}, u32[]{:S(2)}, u32[]{:S(2)}) %collective-permute-start.4) | collective-permute-done | bytes 34848 | tf_op jit(solution)/shard_map/ppermute | solution.py:366
  56.3 0.2 shard_map.42
  56.5 22.5 %all_to_all.10.state = bf16[32,136,128]{2,1,0:T(8,128)(2,1)S(1)} all-to-all(bf16[32,136,128]{2,1,0:T(8,128)(2,1)S(1)} %shard_map.42), channel_id=1, replica_groups=mesh['zh'=4,'zl'=2,'x'=4,'y'=4,'c'=2] {'zl','x','y'}, dimensions={0} | all-to-all | bytes 2228224 | tf_op jit(solution)/shard_map/all_to_all | solution.py:373
  79.0 0.0 copy-done.2
  79.1 0.0 copy-done
  79.1 0.0 copy-done.1
  79.1 1.7 %shard_map.43 = bf16[128,2048]{1,0:T(8,128)(2,1)S(1)} custom-call(s32[1]{0:T(128)} %bitcast.core_ref, bf16[16,256,256]{2,1,0:T(8,128)(2,1)S(1)} %copy-done.1, bf16[16,256,256]{2,1,0:T(8,128)(2,1)S(1)} %copy-done, bf16[16,256,128]{2,1,0:T(8,128)(2,1)S(1)} %copy-done.2, bf16[32,136,128]{2,1,0:T(8,128)(2,1)S(1)} %all_to_all.10.state), custom_call_target="tpu_custom_call" | custom-call | flops 2000000000 | bytes 4194304 | tf_op jit(solution)/shard_map/pallas_call | solution.py:375
  80.7 1.5 %collective-permute-start.7 = (bf16[128,2048]{1,0:T(8,128)(2,1)S(1)}, bf16[128,2048]{1,0:T(8,128)(2,1)S(1)}, u32[]{:S(2)}, u32[]{:S(2)}) collective-permute-start(bf16[128,2048]{1,0:T(8,128)(2,1)S(1)} %shard_map.43), channel_id=1, source_target_pairs={{0,1},{1,0},{2,3},{3,2},{4,5},{5,4},{6,7},{7,6},{8,9},{9,8},{10,11... | collective-permute-start | bytes 1572872 | tf_op jit(solution)/shard_map/ppermute | solution.py:303
  82.3 2.5 %shard_map.44.partial = bf16[128,4096]{1,0:T(8,128)(2,1)} custom-call(s32[1]{0:T(128)} %bitcast.core_ref, bf16[16,256,256]{2,1,0:T(8,128)(2,1)S(1)} %copy-done.1, bf16[16,256,256]{2,1,0:T(8,128)(2,1)S(1)} %copy-done, bf16[16,256,128]{2,1,0:T(8,128)(2,1)S(1)} %copy-done.2, bf16[32,136,128]{2,1,0:T(8,128)(2,1)S(1)} %all_to_all.10.state), custom_call_target="tpu_custom_call" | custom-call | flops 2000000000 | bytes 4194304 | tf_op jit(solution)/shard_map/pallas_call | solution.py:380
  84.8 0.0 collective-permute-done.7.arrived
  84.8 0.8 shard_map.45
Async XLA Ops:
  1.5 9.6 %collective-permute-start = (bf16[2,128,2048]{2,1,0:T(8,128)(2,1)S(1)}, bf16[2,128,2048]{2,1,0:T(8,128)(2,1)S(1)}, u32[]{:S(2)}, u32[]{:S(2)}) collective-permute-start(bf16[2,128,2048]{2,1,0:T(8,128)(2,1)S(1)} %get-tuple-element.21), channel_id=1, source_target_pairs={{0,1},{1,0},{2,3},{3,2},{4,5},{5,4},{6,7},{7,6},{8,9},{9,8},{10,11... | collective-permute-start | bytes 3145736 | tf_op jit(solution)/shard_map/ppermute | solution.py:303
  4.8 6.2 %collective-permute-start.1 = (bf16[3,8,2048]{2,1,0:T(8,128)(2,1)S(1)}, bf16[3,8,2048]{2,1,0:T(8,128)(2,1)S(1)}, u32[]{:S(2)}, u32[]{:S(2)}) collective-permute-start(bf16[3,8,2048]{2,1,0:T(8,128)(2,1)S(1)} %get-tuple-element.22), channel_id=1, source_target_pairs={{1,2},{3,4},{5,6},{7,8},{9,10},{11,12},{13,14},{15,16},{17,18},{19... | collective-permute-start | bytes 294920 | tf_op jit(solution)/shard_map/ppermute | solution.py:321
  6.2 4.8 %collective-permute-start.2 = (bf16[3,8,2048]{2,1,0:T(8,128)(2,1)S(1)}, bf16[3,8,2048]{2,1,0:T(8,128)(2,1)S(1)}, u32[]{:S(2)}, u32[]{:S(2)}) collective-permute-start(bf16[3,8,2048]{2,1,0:T(8,128)(2,1)S(1)} %get-tuple-element.23), channel_id=1, source_target_pairs={{1,3},{3,5},{5,7},{7,9},{9,11},{11,13},{13,15},{15,17},{17,19},{19... | collective-permute-start | bytes 294920 | tf_op jit(solution)/shard_map/ppermute | solution.py:321
  17.7 24.5 %all-to-all-start = ((bf16[32,136,128]{2,1,0:T(8,128)(2,1)}), bf16[32,136,128]{2,1,0:T(8,128)(2,1)S(1)}, u32[]{:S(2)}, u32[]{:S(2)}) async-start(bf16[32,136,128]{2,1,0:T(8,128)(2,1)} %get-tuple-element.26), calls=%async_computation | async-start | bytes 2228224 | tf_op jit(solution)/shard_map/all_to_all | solution.py:348
  26.3 2.0 %collective-permute-start.3 = (bf16[1,128,2048]{2,1,0:T(8,128)(2,1)S(1)}, bf16[1,128,2048]{2,1,0:T(8,128)(2,1)S(1)}, u32[]{:S(2)}, u32[]{:S(2)}) collective-permute-start(bf16[1,128,2048]{2,1,0:T(8,128)(2,1)S(1)} %get-tuple-element.27), channel_id=1, source_target_pairs={{0,1},{1,0},{2,3},{3,2},{4,5},{5,4},{6,7},{7,6},{8,9},{9,8},{10,11... | collective-permute-start | bytes 1572872 | tf_op jit(solution)/shard_map/ppermute | solution.py:303
  42.2 36.9 %copy-start.2 = (bf16[16,256,128]{2,1,0:T(8,128)(2,1)S(1)}, bf16[16,256,128]{2,1,0:T(8,128)(2,1)}, u32[]{:S(2)}) copy-start(bf16[16,256,128]{2,1,0:T(8,128)(2,1)} %get-tuple-element.33.values) | copy-start | bytes 3145732
  42.3 36.7 %copy-start = (bf16[16,256,256]{2,1,0:T(8,128)(2,1)S(1)}, bf16[16,256,256]{2,1,0:T(8,128)(2,1)}, u32[]{:S(2)}) copy-start(bf16[16,256,256]{2,1,0:T(8,128)(2,1)} %get-tuple-element.32.query_map) | copy-start | bytes 6291460
  42.3 36.7 %copy-start.1 = (bf16[16,256,256]{2,1,0:T(8,128)(2,1)S(1)}, bf16[16,256,256]{2,1,0:T(8,128)(2,1)}, u32[]{:S(2)}) copy-start(bf16[16,256,256]{2,1,0:T(8,128)(2,1)} %get-tuple-element.31.scores) | copy-start | bytes 6291460
  42.3 13.0 %collective-permute-start.6 = (bf16[136,128]{1,0:T(8,128)(2,1)S(1)}, bf16[136,128]{1,0:T(8,128)(2,1)S(1)}, u32[]{:S(2)}, u32[]{:S(2)}) collective-permute-start(bf16[136,128]{1,0:T(8,128)(2,1)S(1)} %shard_map.41), channel_id=1, source_target_pairs={{0,192},{1,193},{2,194},{3,195},{4,196},{5,197},{6,198},{7,199},{8... | collective-permute-start | bytes 104456 | tf_op jit(solution)/shard_map/ppermute | solution.py:366
  50.0 5.3 %collective-permute-start.5 = (bf16[136,128]{1,0:T(8,128)(2,1)S(1)}, bf16[136,128]{1,0:T(8,128)(2,1)S(1)}, u32[]{:S(2)}, u32[]{:S(2)}) collective-permute-start(bf16[136,128]{1,0:T(8,128)(2,1)S(1)} %shard_map.41), channel_id=1, source_target_pairs={{0,128},{64,192},{1,129},{65,193},{2,130},{66,194},{3,131},{67,195... | collective-permute-start | bytes 104456 | tf_op jit(solution)/shard_map/ppermute | solution.py:366
  52.8 3.6 %collective-permute-start.4 = (bf16[136,128]{1,0:T(8,128)(2,1)S(1)}, bf16[136,128]{1,0:T(8,128)(2,1)S(1)}, u32[]{:S(2)}, u32[]{:S(2)}) collective-permute-start(bf16[136,128]{1,0:T(8,128)(2,1)S(1)} %shard_map.41), channel_id=1, source_target_pairs={{0,64},{64,128},{128,192},{1,65},{65,129},{129,193},{2,66},{66,130... | collective-permute-start | bytes 104456 | tf_op jit(solution)/shard_map/ppermute | solution.py:366
  80.7 4.0 %collective-permute-start.7 = (bf16[128,2048]{1,0:T(8,128)(2,1)S(1)}, bf16[128,2048]{1,0:T(8,128)(2,1)S(1)}, u32[]{:S(2)}, u32[]{:S(2)}) collective-permute-start(bf16[128,2048]{1,0:T(8,128)(2,1)S(1)} %shard_map.43), channel_id=1, source_target_pairs={{0,1},{1,0},{2,3},{3,2},{4,5},{5,4},{6,7},{7,6},{8,9},{9,8},{10,11... | collective-permute-start | bytes 1572872 | tf_op jit(solution)/shard_map/ppermute | solution.py:303

commit v3 on v2

--- a/solution.py
+++ b/solution.py
@@ -27,6 +27,8 @@
 STEPS = HEADS // GROUP
 FEATURE_SCALE = DH ** (-0.25)
 NORM_SCALE = 0.5 * FEATURE_SCALE * FEATURE_SCALE
+LOG2_E = 1.4426950408889634
+EDGE = 16
 
 AXES = ("zh", "zl", "x", "y", "c")
 SIZES = (4, 2, 4, 4, 2)
@@ -45,82 +47,121 @@
     return lax.dot_general(a, b, NT, preferred_element_type=f32)
 
 
-def fill(core, own, other, rim_a, rim_b, rows):
-    rows[0:RIM, :] = rim_a[0].astype(f32) + rim_b[0].astype(f32)
-    rows[pl.ds(pl.multiple_of(RIM + core * ROWS, 8), ROWS), :] = own[0].astype(f32)
-    rows[pl.ds(pl.multiple_of(RIM + (1 - core) * ROWS, 8), ROWS), :] = other[0].astype(f32)
-
-
-def convolve(rows, taps, head):
-    cols = slice(head * DH, (head + 1) * DH)
-    summed = taps[0, 0:1, cols] * rows[RIM : RIM + CHUNK, cols]
+def fill(core, own, other, rows):
+    rows[pl.ds(pl.multiple_of(RIM + core * ROWS, 8), ROWS), :] = own[...].astype(f32)
+    rows[pl.ds(pl.multiple_of(RIM + (1 - core) * ROWS, 8), ROWS), :] = other[...].astype(f32)
+
+
+def convolve(rows, taps, length):
+    summed = taps[0:1, :] * rows[RIM : RIM + length, :]
     for j in range(1, KC):
-        summed = summed + taps[0, j : j + 1, cols] * rows[RIM - j : RIM - j + CHUNK, cols]
+        summed = summed + taps[j : j + 1, :] * rows[RIM - j : RIM - j + length, :]
     return summed.astype(bf16)
 
 
-def keys_kernel(
-    core_ref, own, other, rim_a, rim_b, taps, omega,
-    state, key_map, values, rows_k, rows_v, maps, convolved, sems,
-):
+def key_features(projection, norm):
+    return jnp.exp2(
+        projection * (FEATURE_SCALE * LOG2_E) - norm * (NORM_SCALE * LOG2_E)
+    ).astype(bf16)
+
+
+def query_features(projection):
+    return jnp.exp2(projection * (FEATURE_SCALE * LOG2_E)).astype(bf16)
+
+
+def maps_kernel(core_ref, own, other, taps, omega, maps, convolved, rows_k, rows_v):
     core = core_ref[0]
     ones = jnp.ones((M, M), bf16)
-
-    def copies(group):
-        heads = pl.ds(group * GROUP, GROUP)
-        return (
-            pltpu.make_async_copy(maps.at[heads], key_map.at[heads], sems.at[0, group]),
-            pltpu.make_async_copy(convolved.at[heads], values.at[heads], sems.at[1, group]),
-        )
+    for part in range(GROUP):
+        rows_k[part, 0:RIM, :] = jnp.zeros((RIM, DH), f32)
+        rows_v[part, 0:RIM, :] = jnp.zeros((RIM, DH), f32)
 
     def one(group, carried):
-        cols = columns(group * WIDE, WIDE)
-        for which, rows in ((0, rows_k), (1, rows_v)):
-            fill(
-                core,
-                own.at[pl.ds(which, 1), :, cols],
-                other.at[pl.ds(which, 1), :, cols],
-                rim_a.at[pl.ds(which + 1, 1), :, cols],
-                rim_b.at[pl.ds(which + 1, 1), :, cols],
-                rows,
-            )
         for part in range(GROUP):
             head = group * GROUP + part
-            k = convolve(rows_k, taps.at[pl.ds(1, 1), :, cols], part)
-            v = convolve(rows_v, taps.at[pl.ds(2, 1), :, cols], part)
+            cols = columns(head * DH, DH)
+            fill(core, own.at[0, :, cols], other.at[1, :, cols], rows_k.at[part])
+            fill(core, own.at[1, :, cols], other.at[2, :, cols], rows_v.at[part])
+            k = convolve(rows_k.at[part], taps[1, :, cols], CHUNK)
+            convolved[head] = convolve(rows_v.at[part], taps[2, :, cols], CHUNK)
             k_wide = k.astype(f32)
             square = k_wide * k_wide
             upper = square.astype(bf16)
             lower = (square - upper.astype(f32)).astype(bf16)
             norm = dot(jnp.concatenate([upper, lower], axis=1), ones)
-            mapped = jnp.exp(dot(k, omega[head]) * FEATURE_SCALE - norm * NORM_SCALE).astype(bf16)
-            maps[head] = mapped
-            convolved[head] = v
+            maps[head] = key_features(dot(k, omega[head]), norm)
+        return carried
+
+    lax.fori_loop(0, STEPS, one, 0)
+
+
+def state_kernel(
+    core_ref, own, other, rim, taps, omega, maps, convolved,
+    state, key_map, values, other_q, rows_k, rows_v, edge_k, edge_v, sems,
+):
+    core = core_ref[0]
+    late = pl.ds(EDGE, CHUNK - EDGE)
+    early = pl.ds(0, EDGE)
+    moves = [
+        pltpu.make_async_copy(maps.at[:, late, :], key_map.at[:, late, :], sems.at[0]),
+        pltpu.make_async_copy(convolved.at[:, late, :], values.at[:, late, :], sems.at[1]),
+        pltpu.make_async_copy(other.at[pl.ds(0, 1)], other_q, sems.at[2]),
+    ]
+    for move in moves:
+        move.start()
+
+    def edge(group, carried):
+        for part in range(GROUP):
+            head = group * GROUP + part
+            cols = columns(head * DH, DH)
+            for which, rows in ((0, rows_k), (1, rows_v)):
+                rows[part, 0:RIM, :] = rim[which + 1, :, cols].astype(f32)
+                mine = own[which, 0:EDGE, cols].astype(f32)
+                theirs = other[which + 1, 0:EDGE, cols].astype(f32)
+                rows[part, RIM : RIM + EDGE, :] = jnp.where(core == 0, mine, theirs)
+            k = convolve(rows_k.at[part], taps[1, :, cols], EDGE)
+            k_wide = k.astype(f32)
+            norm = jnp.sum(k_wide * k_wide, axis=1, keepdims=True)
+            edge_k[head] = key_features(dot(k, omega[head]), norm)
+            edge_v[head] = convolve(rows_v.at[part], taps[2, :, cols], EDGE)
+        return carried
+
+    def one(group, carried):
+        for part in range(GROUP):
+            head = group * GROUP + part
+            mapped = jnp.concatenate([edge_k[head], maps[head, EDGE:, :]], axis=0)
+            v = jnp.concatenate([edge_v[head], convolved[head, EDGE:, :]], axis=0)
             extended = jnp.concatenate([v.T, jnp.ones((16, CHUNK), bf16)], axis=0)
             sums = dot(extended, mapped)[:STATE_ROWS].astype(bf16)
             state[2 * head] = sums[:, : M // 2]
             state[2 * head + 1] = sums[:, M // 2 :]
-        for copy in copies(group):
-            copy.start()
         return carried
 
-    lax.fori_loop(0, STEPS, one, 0)
-    for group in range(STEPS):
-        for copy in copies(group):
-            copy.wait()
+    lax.fori_loop(0, STEPS, edge, 0, unroll=2)
+    last = [
+        pltpu.make_async_copy(edge_k, key_map.at[:, early, :], sems.at[3]),
+        pltpu.make_async_copy(edge_v, values.at[:, early, :], sems.at[4]),
+    ]
+    for move in last:
+        move.start()
+    lax.fori_loop(0, STEPS, one, 0, unroll=2)
+    for move in moves + last:
+        move.wait()
 
 
 def scores_kernel(
-    core_ref, own_q, other_q, rim_qa, rim_qb, taps_q, omega, key_map, query_map, scores, rows_q
+    core_ref, own_q, other_q, rim_q, taps_q, omega, key_map, query_map, scores, rows_q
 ):
     core = core_ref[0]
-    fill(core, own_q, other_q, rim_qa, rim_qb, rows_q)
     causal = lax.broadcasted_iota(jnp.int32, (CHUNK, CHUNK), 0) >= lax.broadcasted_iota(
         jnp.int32, (CHUNK, CHUNK), 1
     )
     for head in range(GROUP):
-        q = convolve(rows_q, taps_q, head)
-        mapped = jnp.exp(dot(q, omega[head]) * FEATURE_SCALE).astype(bf16)
+        cols = slice(head * DH, (head + 1) * DH)
+        rows_q[head, 0:RIM, :] = rim_q[0, :, cols].astype(f32)
+        fill(core, own_q.at[0, :, cols], other_q.at[0, :, cols], rows_q.at[head])
+        q = convolve(rows_q.at[head], taps_q[0, :, cols], CHUNK)
+        mapped = query_features(dot(q, omega[head]))
         query_map[head] = mapped
         scores[head] = jnp.where(causal, dot_nt(mapped, key_map[head]), 0.0).astype(bf16)
 
@@ -197,16 +238,19 @@
         copy.wait()
 
 
-def split_kernel(core_ref, projected, rim_a, rim_b, sent, sent_q, sems):
-    cols = columns((1 - core_ref[0]) * COLS, COLS)
+def split_kernel(core_ref, projected, sent, rim_own, sems):
+    core = core_ref[0]
     last = pl.ds(ROWS - RIM, RIM)
     pairs = [
-        (projected.at[:, last, pl.ds(0, COLS)], rim_a),
-        (projected.at[:, last, pl.ds(COLS, COLS)], rim_b),
-        (projected.at[pl.ds(1, 2), :, cols], sent),
-        (projected.at[pl.ds(0, 1), :, cols], sent_q),
+        (projected.at[:, :, columns((1 - core) * COLS, COLS)], sent),
+        (projected.at[:, last, columns(core * COLS, COLS)], rim_own),
     ]
     run_copies(pairs, sems)
+
+
+def rim_kernel(core_ref, rim_own, other, out):
+    theirs = other[:, ROWS - RIM :, :]
+    out[...] = jnp.where(core_ref[0] == 0, theirs.astype(f32), rim_own[...].astype(f32)).astype(bf16)
 
 
 def fetch_kernel(core_ref, projected, taps, omega, own, own_taps, own_omega, sems):
@@ -307,23 +351,22 @@
     core = lax.axis_index("c").astype(jnp.int32)
     cores = core.reshape(1)
     projected, conv_filter, frequencies = in_main(projected, conv_filter, frequencies)
-    *halves, sent, sent_q = small_call(
+    sent, rim_own = small_call(
         split_kernel,
         [SCALAR, ANYWHERE],
-        [WHOLE] * 4,
-        [chip(3, RIM, COLS), chip(3, RIM, COLS), chip(2, ROWS, COLS), chip(1, ROWS, COLS)],
-        [pltpu.SemaphoreType.DMA((4,))],
+        [WHOLE] * 2,
+        [chip(3, ROWS, COLS), chip(3, RIM, COLS)],
+        [pltpu.SemaphoreType.DMA((2,))],
         flops=0,
         moved=3 * 2**20,
     )(cores, projected)
-    count = 256 // CORES
-    rims = [
-        lax.ppermute(
-            halves[to], AXES, [(2 * i + 1, 2 * (i + 1) + to) for i in range(count - 1)]
-        )
-        for to in range(CORES)
-    ]
-    other, other_q = swap(sent), swap(sent_q)
+    other = swap(sent)
+    (other,) = in_chip(other)
+    rim = small_call(
+        rim_kernel, [SCALAR, WHOLE, WHOLE], WHOLE, chip(3, RIM, COLS), [], flops=0, moved=2**18
+    )(cores, *in_chip(rim_own), other)
+    count = 256 - CORES
+    rim = lax.ppermute(rim, AXES, [(i, i + CORES) for i in range(count)])
     fetched = small_call(
         fetch_kernel,
         [SCALAR] + [ANYWHERE] * 3,
@@ -333,30 +376,41 @@
         flops=0,
         moved=5 * 2**20,
     )(cores, projected, conv_filter, frequencies)
-    own, own_taps, own_omega, other, *rims = in_chip(*fetched, other, *rims)
-    state, key_map, values = small_call(
-        keys_kernel,
-        [SCALAR] + [WHOLE] * 6,
-        [WHOLE, ANYWHERE, ANYWHERE],
-        [chip(PIECES, STATE_ROWS, M // 2), main(HEADS, CHUNK, M), main(HEADS, CHUNK, DH)],
-        [pltpu.VMEM((RIM + CHUNK, WIDE), f32)] * 2
-        + [pltpu.VMEM((HEADS, CHUNK, M), bf16), pltpu.VMEM((HEADS, CHUNK, DH), bf16)]
-        + [pltpu.SemaphoreType.DMA((2, STEPS))],
-        flops=4 * 10**9,
-        moved=10 * 2**20,
-    )(cores, own, other, *rims, own_taps, own_omega)
+    own, own_taps, own_omega, rim = in_chip(*fetched, rim)
+    raw = [pltpu.VMEM((GROUP, RIM + CHUNK, DH), f32)] * 2
+    maps, convolved = small_call(
+        maps_kernel,
+        [SCALAR] + [WHOLE] * 4,
+        [WHOLE, WHOLE],
+        [chip(HEADS, CHUNK, M), chip(HEADS, CHUNK, DH)],
+        raw,
+        flops=3 * 10**9,
+        moved=6 * 2**20,
+    )(cores, own, other, own_taps, own_omega)
+    state, key_map, values, other_q = small_call(
+        state_kernel,
+        [SCALAR] + [WHOLE] * 7,
+        [WHOLE] + [ANYWHERE] * 3,
+        [chip(PIECES, STATE_ROWS, M // 2), main(HEADS, CHUNK, M), main(HEADS, CHUNK, DH)]
+        + [main(1, ROWS, COLS)],
+        [pltpu.VMEM((GROUP, RIM + EDGE, DH), f32)] * 2
+        + [pltpu.VMEM((HEADS, EDGE, M), bf16), pltpu.VMEM((HEADS, EDGE, DH), bf16)]
+        + [pltpu.SemaphoreType.DMA((5,))],
+        flops=2 * 10**9,
+        moved=6 * 2**20,
+    )(cores, own, other, rim, own_taps, own_omega, *in_chip(maps, convolved))
     gathered = lax.all_to_all(state, PLANE, 0, 0, tiled=True)
-    key_map, values = in_main(key_map, values)
+    key_map, values, other_q = in_main(key_map, values, other_q)
     query_map, scores = call(
         scores_kernel,
-        [own_spec(0), other_spec(0), rim_spec(0), rim_spec(0), taps_spec(0), OMEGA_SPEC]
+        [own_spec(0), other_spec(0), rim_spec(0), taps_spec(0), OMEGA_SPEC]
         + [head_spec(CHUNK, M)],
         [head_spec(CHUNK, M), head_spec(CHUNK, CHUNK)],
         [main(HEADS, CHUNK, M), main(HEADS, CHUNK, CHUNK)],
-        [pltpu.VMEM((RIM + CHUNK, WIDE), f32)],
+        [pltpu.VMEM((GROUP, RIM + CHUNK, DH), f32)],
         flops=8 * 10**9,
         moved=20 * 2**20,
-    )(cores, projected, other_q, rims[0], rims[1], conv_filter, frequencies, key_map)
+    )(cores, projected, other_q, rim, conv_filter, frequencies, key_map)
     gathered, query_map, scores = lax.optimization_barrier((gathered, query_map, scores))
     total = small_call(
         total_kernel, [WHOLE], WHOLE, chip(STATE_ROWS, M // 2), [], flops=10**6, moved=2**20

time: 86 us -> 83.5 us (0.971)
  blocking collectives: 22.5 us -> 20.5 us
  starting transfers between devices: 31.1 us -> 29.7 us
  waiting for transfers between devices: 11.2 us -> 12.3 us
    ppermute x2 -> x1, starting transfers between devices: 4.57 us -> 1.47 us  [per_device(): rim = lax.ppermute(rim, AXES, [(i, i + CORES) for i in range(count)])]
    ppermute x3 -> x2, starting transfers between devices: 4.96 us -> 7.96 us  [swap(): return lax.ppermute(array, 'c', [(0, 1), (1, 0)])]
    all_to_all x1, blocking collectives: 22.5 us -> 20.5 us  [per_device(): prior = lax.all_to_all(prior, PLANE, 0, 0, tiled=True)]
    all_to_all x1, waiting for transfers between devices: 8.32 us -> 9.89 us  [per_device(): gathered = lax.all_to_all(state, PLANE, 0, 0, tiled=True)]
    ppermute x3 -> x2, waiting for transfers between devices: 1.9 us -> 1.44 us  [swap(): return lax.ppermute(array, 'c', [(0, 1), (1, 0)])]
    pallas_call x3 -> x5, Pallas kernels: 13.6 us -> 13.6 us  [the longest x1 5.76 us: per_device(): call(scores_kernel, [own_spec(0), other_spec(0), rim_spec(0), taps_spec(0...]
  transfers between devices with their start and end apart: 9 -> 7, of which waited for: 3 -> 3; matrix products, arithmetic and copies ran while one was open for 0% -> 0% of each run, Pallas kernels for 11% -> 16%
where the time goes in v3:
time: 83.5 us; the launch traced here: 83.1 us
  starting transfers between devices  29.7 us (36%)
  Pallas kernels  20.5 us (25%)
  blocking collectives  20.5 us (25%)
  waiting for transfers between devices  12.3 us (15%)
    all_to_all x1, blocking collectives, per_device(): prior = lax.all_to_all(prior, PLANE, 0, 0, tiled=True)  20.5 us
    ppermute x3, starting transfers between devices, per_device(): lax.ppermute(total, 'zh', [(i, i + by) for i in range(planes - by)])  12.1 us
    all_to_all x1, waiting for transfers between devices, per_device(): gathered = lax.all_to_all(state, PLANE, 0, 0, tiled=True)  9.89 us
    all_to_all x1, starting transfers between devices, per_device(): gathered = lax.all_to_all(state, PLANE, 0, 0, tiled=True)  8.11 us
    ppermute x2, starting transfers between devices, swap(): return lax.ppermute(array, 'c', [(0, 1), (1, 0)])  7.96 us
    pallas_call x1, Pallas kernels, per_device(): call(scores_kernel, [own_spec(0), other_spec(0), rim_spec(0), taps_spec(0...  5.76 us
    pallas_call x1, Pallas kernels, per_device(): small_call(maps_kernel, [SCALAR] + [WHOLE] * 4, [WHOLE, WHOLE], [chip(HEA...  3.53 us
    pallas_call x1, Pallas kernels, per_device(): small_call(state_kernel, [SCALAR] + [WHOLE] * 7, [WHOLE] + [ANYWHERE] * 3...  2.87 us
  transfers between devices with their start and end apart: 7, of which 3 were waited for; matrix products, arithmetic and copies ran while one was open for 0% of the time, Pallas kernels for 16%

profile of v3, /device:TPU:1, one launch (start us, length us, event | category | flops | bytes accessed | tf_op | source)
XLA Modules:
  0.0 83.1 jit_solution(3765762846624100965)
XLA Ops:
  0.0 1.4 %shard_map.38 = (bf16[3,128,2048]{2,1,0:T(8,128)(2,1)S(1)}, bf16[3,8,2048]{2,1,0:T(8,128)(2,1)S(1)}) custom-call(s32[1]{0:T(128)} %bitcast.core_ref, bf16[3,128,4096]{2,1,0:T(8,128)(2,1)} %own_q.1), custom_call_target="tpu_custom_call" | custom-call | bytes 3145728 | tf_op jit(solution)/shard_map/pallas_call | solution.py:354
  1.4 3.3 %collective-permute-start = (bf16[3,128,2048]{2,1,0:T(8,128)(2,1)S(1)}, bf16[3,128,2048]{2,1,0:T(8,128)(2,1)S(1)}, u32[]{:S(2)}, u32[]{:S(2)}) collective-permute-start(bf16[3,128,2048]{2,1,0:T(8,128)(2,1)S(1)} %get-tuple-element.22), channel_id=1, source_target_pairs={{0,1},{1,0},{2,3},{3,2},{4,5},{5,4},{6,7},{7,6},{8,9},{9,8},{10,11... | collective-permute-start | bytes 4718600 | tf_op jit(solution)/shard_map/ppermute | solution.py:347
  4.8 1.6 %shard_map.37 = (bf16[2,128,2048]{2,1,0:T(8,128)(2,1)S(1)}, f32[3,4,2048]{2,1,0:T(4,128)S(1)}, bf16[16,128,256]{2,1,0:T(8,128)(2,1)S(1)}) custom-call(s32[1]{0:T(128)} %bitcast.core_ref, bf16[3,128,4096]{2,1,0:T(8,128)(2,1)} %own_q.1, f32[3,4,4096]{2,1,0:T(4,128)} %taps_q.1, bf16[32,128,256]{2,1,0:T(8,128)(2,1)} %omega.3), custom_call_target="tpu_custom_call" | custom-call | bytes 5242880 | tf_op jit(solution)/shard_map/pallas_call | solution.py:370
  6.4 1.4 %collective-permute-done.other = bf16[3,128,2048]{2,1,0:T(8,128)(2,1)S(1)} collective-permute-done((bf16[3,128,2048]{2,1,0:T(8,128)(2,1)S(1)}, bf16[3,128,2048]{2,1,0:T(8,128)(2,1)S(1)}, u32[]{:S(2)}, u32[]{:S(2)}) %collective-permute-start) | collective-permute-done | bytes 1572896 | tf_op jit(solution)/shard_map/ppermute | solution.py:347
  7.8 1.5 %collective-permute-start.1 = (bf16[3,8,2048]{2,1,0:T(8,128)(2,1)S(1)}, bf16[3,8,2048]{2,1,0:T(8,128)(2,1)S(1)}, u32[]{:S(2)}, u32[]{:S(2)}) collective-permute-start(bf16[3,8,2048]{2,1,0:T(8,128)(2,1)S(1)} %shard_map.39), channel_id=1, source_target_pairs={{0,2},{1,3},{2,4},{3,5},{4,6},{5,7},{6,8},{7,9},{8,10},{9,11},{10,... | collective-permute-start | bytes 294920 | tf_op jit(solution)/shard_map/ppermute | solution.py:369
  9.3 3.5 %shard_map.40 = (bf16[16,256,256]{2,1,0:T(8,128)(2,1)S(1)}, bf16[16,256,128]{2,1,0:T(8,128)(2,1)S(1)}) custom-call(s32[1]{0:T(128)} %bitcast.core_ref, bf16[2,128,2048]{2,1,0:T(8,128)(2,1)S(1)} %get-tuple-element.21.own, bf16[3,128,2048]{2,1,0:T(8,128)(2,1)S(1)} %collective-permute-done.other, f32[3,4,2048]{2,1,0:T(4,128)S(1)} %get-tuple-element.24.taps, ...), custom_call_target="tpu_custom_call" | custom-call | flops 3000000000 | bytes 6291456 | tf_op jit(solution)/shard_map/pallas_call | solution.py:381
  12.8 0.0 collective-permute-done.1.rim.rim_q
  12.8 2.9 %shard_map.41 = (bf16[32,136,128]{2,1,0:T(8,128)(2,1)}, bf16[16,256,256]{2,1,0:T(8,128)(2,1)}, bf16[16,256,128]{2,1,0:T(8,128)(2,1)}, bf16[1,128,2048]{2,1,0:T(8,128)(2,1)}) custom-call(s32[1]{0:T(128)} %bitcast.core_ref, bf16[2,128,2048]{2,1,0:T(8,128)(2,1)S(1)} %get-tuple-element.21.own, bf16[3,128,2048]{2,1,0:T(8,128)(2,1)S(1)} %collective-permute-done.other, ...), custom_call_target="tpu_custom_call" | custom-call | flops 2000000000 | bytes 6291456 | tf_op jit(solution)/shard_map/pallas_call | solution.py:390
  15.7 8.1 %all-to-all-start = ((bf16[32,136,128]{2,1,0:T(8,128)(2,1)}), bf16[32,136,128]{2,1,0:T(8,128)(2,1)S(1)}, u32[]{:S(2)}, u32[]{:S(2)}) async-start(bf16[32,136,128]{2,1,0:T(8,128)(2,1)} %get-tuple-element.28), calls=%async_computation | async-start | bytes 2228224 | tf_op jit(solution)/shard_map/all_to_all | solution.py:402
  23.8 5.8 %shard_map.42 = (bf16[16,256,256]{2,1,0:T(8,128)(2,1)}, bf16[16,256,256]{2,1,0:T(8,128)(2,1)}) custom-call(s32[1]{0:T(128)} %bitcast.core_ref, bf16[3,128,4096]{2,1,0:T(8,128)(2,1)} %own_q.1, bf16[1,128,2048]{2,1,0:T(8,128)(2,1)} %get-tuple-element.29.other_q, bf16[3,8,2048]{2,1,0:T(8,128)(2,1)S(1)} %collective-permute-done.1.rim.rim_q, ...), custom_call_target="tpu_custom_call" | custom-call | flops 8000000000 | bytes 20971520 | tf_op jit(solution)/shard_map/pallas_call | solution.py:404
  29.6 9.9 %all-to-all-done.sums = bf16[32,136,128]{2,1,0:T(8,128)(2,1)S(1)} async-done(((bf16[32,136,128]{2,1,0:T(8,128)(2,1)}), bf16[32,136,128]{2,1,0:T(8,128)(2,1)S(1)}, u32[]{:S(2)}, u32[]{:S(2)}) %all-to-all-start) | async-done | bytes 1114144 | tf_op jit(solution)/shard_map/all_to_all | solution.py:402
  39.5 0.0 copy-start.2
  39.5 0.2 shard_map.43
  39.7 0.0 copy-start
  39.7 0.0 copy-start.1
  39.7 6.9 %collective-permute-start.4 = (bf16[136,128]{1,0:T(8,128)(2,1)S(1)}, bf16[136,128]{1,0:T(8,128)(2,1)S(1)}, u32[]{:S(2)}, u32[]{:S(2)}) collective-permute-start(bf16[136,128]{1,0:T(8,128)(2,1)S(1)} %shard_map.43), channel_id=1, source_target_pairs={{0,192},{1,193},{2,194},{3,195},{4,196},{5,197},{6,198},{7,199},{8... | collective-permute-start | bytes 104456 | tf_op jit(solution)/shard_map/ppermute | solution.py:420
  46.5 2.8 %collective-permute-start.3 = (bf16[136,128]{1,0:T(8,128)(2,1)S(1)}, bf16[136,128]{1,0:T(8,128)(2,1)S(1)}, u32[]{:S(2)}, u32[]{:S(2)}) collective-permute-start(bf16[136,128]{1,0:T(8,128)(2,1)S(1)} %shard_map.43), channel_id=1, source_target_pairs={{0,128},{64,192},{1,129},{65,193},{2,130},{66,194},{3,131},{67,195... | collective-permute-start | bytes 104456 | tf_op jit(solution)/shard_map/ppermute | solution.py:420
  49.3 2.5 %collective-permute-start.2 = (bf16[136,128]{1,0:T(8,128)(2,1)S(1)}, bf16[136,128]{1,0:T(8,128)(2,1)S(1)}, u32[]{:S(2)}, u32[]{:S(2)}) collective-permute-start(bf16[136,128]{1,0:T(8,128)(2,1)S(1)} %shard_map.43), channel_id=1, source_target_pairs={{0,64},{64,128},{128,192},{1,65},{65,129},{129,193},{2,66},{66,130... | collective-permute-start | bytes 104456 | tf_op jit(solution)/shard_map/ppermute | solution.py:420
  51.8 0.0 collective-permute-done.4.before_3
  51.9 0.0 collective-permute-done.3.before_2
  51.9 1.0 %collective-permute-done.2.before_1 = bf16[136,128]{1,0:T(8,128)(2,1)S(1)} collective-permute-done((bf16[136,128]{1,0:T(8,128)(2,1)S(1)}, bf16[136,128]{1,0:T(8,128)(2,1)S(1)}, u32[]{:S(2)}, u32[]{:S(2)}) %collective-permute-start.2) | collective-permute-done | bytes 34848 | tf_op jit(solution)/shard_map/ppermute | solution.py:420
  52.9 0.2 shard_map.44
  53.1 20.5 %all_to_all.10.state = bf16[32,136,128]{2,1,0:T(8,128)(2,1)S(1)} all-to-all(bf16[32,136,128]{2,1,0:T(8,128)(2,1)S(1)} %shard_map.44), channel_id=1, replica_groups=mesh['zh'=4,'zl'=2,'x'=4,'y'=4,'c'=2] {'zl','x','y'}, dimensions={0} | all-to-all | bytes 2228224 | tf_op jit(solution)/shard_map/all_to_all | solution.py:427
  73.5 0.0 copy-done.2
  73.5 0.0 copy-done
  73.5 0.0 copy-done.1
  73.5 1.7 %shard_map.45 = bf16[128,2048]{1,0:T(8,128)(2,1)S(1)} custom-call(s32[1]{0:T(128)} %bitcast.core_ref, bf16[16,256,256]{2,1,0:T(8,128)(2,1)S(1)} %copy-done.1, bf16[16,256,256]{2,1,0:T(8,128)(2,1)S(1)} %copy-done, bf16[16,256,128]{2,1,0:T(8,128)(2,1)S(1)} %copy-done.2, bf16[32,136,128]{2,1,0:T(8,128)(2,1)S(1)} %all_to_all.10.state), custom_call_target="tpu_custom_call" | custom-call | flops 2000000000 | bytes 4194304 | tf_op jit(solution)/shard_map/pallas_call | solution.py:429
  75.2 4.6 %collective-permute-start.5 = (bf16[128,2048]{1,0:T(8,128)(2,1)S(1)}, bf16[128,2048]{1,0:T(8,128)(2,1)S(1)}, u32[]{:S(2)}, u32[]{:S(2)}) collective-permute-start(bf16[128,2048]{1,0:T(8,128)(2,1)S(1)} %shard_map.45), channel_id=1, source_target_pairs={{0,1},{1,0},{2,3},{3,2},{4,5},{5,4},{6,7},{7,6},{8,9},{9,8},{10,11... | collective-permute-start | bytes 1572872 | tf_op jit(solution)/shard_map/ppermute | solution.py:347
  79.8 2.5 %shard_map.46.partial = bf16[128,4096]{1,0:T(8,128)(2,1)} custom-call(s32[1]{0:T(128)} %bitcast.core_ref, bf16[16,256,256]{2,1,0:T(8,128)(2,1)S(1)} %copy-done.1, bf16[16,256,256]{2,1,0:T(8,128)(2,1)S(1)} %copy-done, bf16[16,256,128]{2,1,0:T(8,128)(2,1)S(1)} %copy-done.2, bf16[32,136,128]{2,1,0:T(8,128)(2,1)S(1)} %all_to_all.10.state), custom_call_target="tpu_custom_call" | custom-call | flops 2000000000 | bytes 4194304 | tf_op jit(solution)/shard_map/pallas_call | solution.py:434
  82.3 0.0 collective-permute-done.5.arrived
  82.3 0.8 shard_map.47
  (1 shorter events, 0.0 us)
Async XLA Ops:
  1.4 6.4 %collective-permute-start = (bf16[3,128,2048]{2,1,0:T(8,128)(2,1)S(1)}, bf16[3,128,2048]{2,1,0:T(8,128)(2,1)S(1)}, u32[]{:S(2)}, u32[]{:S(2)}) collective-permute-start(bf16[3,128,2048]{2,1,0:T(8,128)(2,1)S(1)} %get-tuple-element.22), channel_id=1, source_target_pairs={{0,1},{1,0},{2,3},{3,2},{4,5},{5,4},{6,7},{7,6},{8,9},{9,8},{10,11... | collective-permute-start | bytes 4718600 | tf_op jit(solution)/shard_map/ppermute | solution.py:347
  7.8 5.0 %collective-permute-start.1 = (bf16[3,8,2048]{2,1,0:T(8,128)(2,1)S(1)}, bf16[3,8,2048]{2,1,0:T(8,128)(2,1)S(1)}, u32[]{:S(2)}, u32[]{:S(2)}) collective-permute-start(bf16[3,8,2048]{2,1,0:T(8,128)(2,1)S(1)} %shard_map.39), channel_id=1, source_target_pairs={{0,2},{1,3},{2,4},{3,5},{4,6},{5,7},{6,8},{7,9},{8,10},{9,11},{10,... | collective-permute-start | bytes 294920 | tf_op jit(solution)/shard_map/ppermute | solution.py:369
  15.7 23.8 %all-to-all-start = ((bf16[32,136,128]{2,1,0:T(8,128)(2,1)}), bf16[32,136,128]{2,1,0:T(8,128)(2,1)S(1)}, u32[]{:S(2)}, u32[]{:S(2)}) async-start(bf16[32,136,128]{2,1,0:T(8,128)(2,1)} %get-tuple-element.28), calls=%async_computation | async-start | bytes 2228224 | tf_op jit(solution)/shard_map/all_to_all | solution.py:402
  39.5 34.0 %copy-start.2 = (bf16[16,256,128]{2,1,0:T(8,128)(2,1)S(1)}, bf16[16,256,128]{2,1,0:T(8,128)(2,1)}, u32[]{:S(2)}) copy-start(bf16[16,256,128]{2,1,0:T(8,128)(2,1)} %get-tuple-element.35.values) | copy-start | bytes 3145732
  39.7 33.9 %copy-start = (bf16[16,256,256]{2,1,0:T(8,128)(2,1)S(1)}, bf16[16,256,256]{2,1,0:T(8,128)(2,1)}, u32[]{:S(2)}) copy-start(bf16[16,256,256]{2,1,0:T(8,128)(2,1)} %get-tuple-element.34.query_map) | copy-start | bytes 6291460
  39.7 33.9 %copy-start.1 = (bf16[16,256,256]{2,1,0:T(8,128)(2,1)S(1)}, bf16[16,256,256]{2,1,0:T(8,128)(2,1)}, u32[]{:S(2)}) copy-start(bf16[16,256,256]{2,1,0:T(8,128)(2,1)} %get-tuple-element.33.scores) | copy-start | bytes 6291460
  39.7 12.2 %collective-permute-start.4 = (bf16[136,128]{1,0:T(8,128)(2,1)S(1)}, bf16[136,128]{1,0:T(8,128)(2,1)S(1)}, u32[]{:S(2)}, u32[]{:S(2)}) collective-permute-start(bf16[136,128]{1,0:T(8,128)(2,1)S(1)} %shard_map.43), channel_id=1, source_target_pairs={{0,192},{1,193},{2,194},{3,195},{4,196},{5,197},{6,198},{7,199},{8... | collective-permute-start | bytes 104456 | tf_op jit(solution)/shard_map/ppermute | solution.py:420
  46.5 5.3 %collective-permute-start.3 = (bf16[136,128]{1,0:T(8,128)(2,1)S(1)}, bf16[136,128]{1,0:T(8,128)(2,1)S(1)}, u32[]{:S(2)}, u32[]{:S(2)}) collective-permute-start(bf16[136,128]{1,0:T(8,128)(2,1)S(1)} %shard_map.43), channel_id=1, source_target_pairs={{0,128},{64,192},{1,129},{65,193},{2,130},{66,194},{3,131},{67,195... | collective-permute-start | bytes 104456 | tf_op jit(solution)/shard_map/ppermute | solution.py:420
  49.3 3.5 %collective-permute-start.2 = (bf16[136,128]{1,0:T(8,128)(2,1)S(1)}, bf16[136,128]{1,0:T(8,128)(2,1)S(1)}, u32[]{:S(2)}, u32[]{:S(2)}) collective-permute-start(bf16[136,128]{1,0:T(8,128)(2,1)S(1)} %shard_map.43), channel_id=1, source_target_pairs={{0,64},{64,128},{128,192},{1,65},{65,129},{129,193},{2,66},{66,130... | collective-permute-start | bytes 104456 | tf_op jit(solution)/shard_map/ppermute | solution.py:420
  75.2 7.1 %collective-permute-start.5 = (bf16[128,2048]{1,0:T(8,128)(2,1)S(1)}, bf16[128,2048]{1,0:T(8,128)(2,1)S(1)}, u32[]{:S(2)}, u32[]{:S(2)}) collective-permute-start(bf16[128,2048]{1,0:T(8,128)(2,1)S(1)} %shard_map.45), channel_id=1, source_target_pairs={{0,1},{1,0},{2,3},{3,2},{4,5},{5,4},{6,7},{7,6},{8,9},{9,8},{10,11... | collective-permute-start | bytes 1572872 | tf_op jit(solution)/shard_map/ppermute | solution.py:347

commit v4 on v3

--- a/solution.py
+++ b/solution.py
@@ -95,8 +95,12 @@
     lax.fori_loop(0, STEPS, one, 0)
 
 
+def piece_of(head, flip):
+    return lax.rem(2 * head + flip * HEADS, PIECES)
+
+
 def state_kernel(
-    core_ref, own, other, rim, taps, omega, maps, convolved,
+    core_ref, flip_ref, own, other, rim, taps, omega, maps, convolved,
     state, key_map, values, other_q, rows_k, rows_v, edge_k, edge_v, sems,
 ):
     core = core_ref[0]
@@ -133,8 +137,9 @@
             v = jnp.concatenate([edge_v[head], convolved[head, EDGE:, :]], axis=0)
             extended = jnp.concatenate([v.T, jnp.ones((16, CHUNK), bf16)], axis=0)
             sums = dot(extended, mapped)[:STATE_ROWS].astype(bf16)
-            state[2 * head] = sums[:, : M // 2]
-            state[2 * head + 1] = sums[:, M // 2 :]
+            piece = piece_of(head, flip_ref[0])
+            state[piece] = sums[:, : M // 2]
+            state[piece + 1] = sums[:, M // 2 :]
         return carried
 
     lax.fori_loop(0, STEPS, edge, 0, unroll=2)
@@ -180,51 +185,67 @@
         running = running + sums[i].astype(f32)
 
 
-def attend_rows(rows, scores, query_map, values, state, put):
+def attend_rows(rows, flip, scores, query_map, values, state, put, group):
     ones = jnp.ones((CHUNK, DH), bf16)
-
-    def one(head, carried):
-        prior = jnp.concatenate([state[2 * head], state[2 * head + 1]], axis=1)
+    for head in range(group * GROUP, (group + 1) * GROUP):
+        piece = piece_of(head, flip)
+        prior = jnp.concatenate([state[piece], state[piece + 1]], axis=1)
         total = jnp.broadcast_to(prior[DH : DH + 1], (DH, M))
         prior = jnp.concatenate([prior[:DH], total], axis=0)
         both = dot(scores[head, rows, :], jnp.concatenate([values[head], ones], axis=1))
         both = both + dot_nt(query_map[head, rows, :], prior)
         put(head, (both[:, :DH] / both[:, DH:]).astype(bf16))
-        return carried
-
-    lax.fori_loop(0, HEADS, one, 0, unroll=4)
 
 
 def columns(start, size):
     return pl.ds(pl.multiple_of(start, DH), size)
 
 
-def attend_other_kernel(core_ref, scores, query_map, values, state, out):
+def attend_other_kernel(core_ref, flip_ref, scores, query_map, values, state, out):
     start = pl.multiple_of((1 - core_ref[0]) * ROWS, ROWS)
 
     def put(head, block):
         out[:, columns(head * DH, DH)] = block
 
-    attend_rows(pl.ds(start, ROWS), scores, query_map, values, state, put)
-
-
-def attend_own_kernel(core_ref, scores, query_map, values, state, out, block_rows, sem):
+    for group in range(STEPS):
+        attend_rows(
+            pl.ds(start, ROWS), flip_ref[0], scores, query_map, values, state, put, group
+        )
+
+
+def attend_own_kernel(
+    core_ref, flip_ref, scores, query_map, values, state, out, block_rows, sems
+):
     core = core_ref[0]
-    start = pl.multiple_of(core * ROWS, ROWS)
+    rows = pl.ds(pl.multiple_of(core * ROWS, ROWS), ROWS)
 
     def put(head, block):
         block_rows[:, columns(head * DH, DH)] = block
 
-    attend_rows(pl.ds(start, ROWS), scores, query_map, values, state, put)
-    copy = pltpu.make_async_copy(block_rows, out.at[:, columns(core * COLS, COLS)], sem)
-    copy.start()
-    copy.wait()
-
-
-def finish_kernel(core_ref, arrived, partial, out, sem):
-    copy = pltpu.make_async_copy(arrived, out.at[:, columns((1 - core_ref[0]) * COLS, COLS)], sem)
-    copy.start()
-    copy.wait()
+    def copy(group):
+        return pltpu.make_async_copy(
+            block_rows.at[:, pl.ds(group * WIDE, WIDE)],
+            out.at[:, columns(core * COLS + group * WIDE, WIDE)],
+            sems.at[group],
+        )
+
+    for group in range(STEPS):
+        attend_rows(rows, flip_ref[0], scores, query_map, values, state, put, group)
+        copy(group).start()
+    for group in range(STEPS):
+        copy(group).wait()
+
+
+def finish_kernel(core_ref, arrived, partial, out, sems):
+    start = (1 - core_ref[0]) * COLS
+    pairs = [
+        (
+            arrived.at[:, pl.ds(group * WIDE, WIDE)],
+            out.at[:, columns(start + group * WIDE, WIDE)],
+        )
+        for group in range(STEPS)
+    ]
+    run_copies(pairs, sems)
 
 
 def run_copies(pairs, sems):
@@ -350,6 +371,7 @@
 def per_device(projected, conv_filter, frequencies):
     core = lax.axis_index("c").astype(jnp.int32)
     cores = core.reshape(1)
+    flips = (lax.axis_index("zh") // 2).astype(jnp.int32).reshape(1)
     projected, conv_filter, frequencies = in_main(projected, conv_filter, frequencies)
     sent, rim_own = small_call(
         split_kernel,
@@ -389,7 +411,7 @@
     )(cores, own, other, own_taps, own_omega)
     state, key_map, values, other_q = small_call(
         state_kernel,
-        [SCALAR] + [WHOLE] * 7,
+        [SCALAR] * 2 + [WHOLE] * 7,
         [WHOLE] + [ANYWHERE] * 3,
         [chip(PIECES, STATE_ROWS, M // 2), main(HEADS, CHUNK, M), main(HEADS, CHUNK, DH)]
         + [main(1, ROWS, COLS)],
@@ -398,7 +420,7 @@
         + [pltpu.SemaphoreType.DMA((5,))],
         flops=2 * 10**9,
         moved=6 * 2**20,
-    )(cores, own, other, rim, own_taps, own_omega, *in_chip(maps, convolved))
+    )(cores, flips, own, other, rim, own_taps, own_omega, *in_chip(maps, convolved))
     gathered = lax.all_to_all(state, PLANE, 0, 0, tiled=True)
     key_map, values, other_q = in_main(key_map, values, other_q)
     query_map, scores = call(
@@ -415,10 +437,22 @@
     total = small_call(
         total_kernel, [WHOLE], WHOLE, chip(STATE_ROWS, M // 2), [], flops=10**6, moved=2**20
     )(*in_chip(gathered))
-    planes = SIZES[0]
+    groups = SIZES[0]
+
+    def owner(group, plane):
+        return 2 * group + (plane + group // 2) % 2
+
     before = [
-        lax.ppermute(total, "zh", [(i, i + by) for i in range(planes - by)])
-        for by in range(1, planes)
+        lax.ppermute(
+            total,
+            ("zh", "zl"),
+            [
+                (owner(group, plane), owner(group + by, plane))
+                for group in range(groups - by)
+                for plane in range(2)
+            ],
+        )
+        for by in reversed(range(1, groups))
     ]
     prior = small_call(
         prefix_kernel, [WHOLE] * 4, WHOLE, chip(PIECES, STATE_ROWS, M // 2), [],
@@ -427,18 +461,18 @@
     prior = lax.all_to_all(prior, PLANE, 0, 0, tiled=True)
     operands = in_chip(scores, query_map, values, prior)
     attended = small_call(
-        attend_other_kernel, [SCALAR] + [WHOLE] * 4, WHOLE, chip(ROWS, COLS), [],
+        attend_other_kernel, [SCALAR] * 2 + [WHOLE] * 4, WHOLE, chip(ROWS, COLS), [],
         flops=2 * 10**9, moved=4 * 2**20,
-    )(cores, *operands)
+    )(cores, flips, *operands)
     arrived = swap(attended)
     partial = small_call(
-        attend_own_kernel, [SCALAR] + [WHOLE] * 4, ANYWHERE, main(ROWS, D),
-        [pltpu.VMEM((ROWS, COLS), bf16), pltpu.SemaphoreType.DMA],
+        attend_own_kernel, [SCALAR] * 2 + [WHOLE] * 4, ANYWHERE, main(ROWS, D),
+        [pltpu.VMEM((ROWS, COLS), bf16), pltpu.SemaphoreType.DMA((STEPS,))],
         flops=2 * 10**9, moved=4 * 2**20,
-    )(cores, *operands)
+    )(cores, flips, *operands)
     return small_call(
         finish_kernel, [SCALAR, WHOLE, ANYWHERE], ANYWHERE, main(ROWS, D),
-        [pltpu.SemaphoreType.DMA], flops=0, moved=2**20, aliases={2: 0},
+        [pltpu.SemaphoreType.DMA((STEPS,))], flops=0, moved=2**20, aliases={2: 0},
     )(cores, *in_chip(arrived), *in_main(partial))
 
 

time: 83.5 us -> 81.7 us (0.978)
  blocking collectives: 20.5 us -> 19.3 us
  Pallas kernels: 20.5 us -> 19.5 us
    all_to_all x1, blocking collectives: 20.5 us -> 19.3 us  [per_device(): prior = lax.all_to_all(prior, PLANE, 0, 0, tiled=True)]
    pallas_call x3, Pallas kernels: 7.01 us -> 5.96 us  [the longest x1 2.87 us: per_device(): small_call(state_kernel, [SCALAR] * 2 + [WHOLE] * 7, [WHOLE] + [ANYWHERE]...]
where the time goes in v4:
time: 81.7 us; the launch traced here: 81.3 us
  starting transfers between devices  30 us (37%)
  Pallas kernels  19.5 us (24%)
  blocking collectives  19.3 us (24%)
  waiting for transfers between devices  12.4 us (15%)
    all_to_all x1, blocking collectives, per_device(): prior = lax.all_to_all(prior, PLANE, 0, 0, tiled=True)  19.3 us
    ppermute x3, starting transfers between devices, per_device(): lax.ppermute(total, ('zh', 'zl'), [(owner(group, plane), owner(group + by...  12.3 us
    all_to_all x1, waiting for transfers between devices, per_device(): gathered = lax.all_to_all(state, PLANE, 0, 0, tiled=True)  9.89 us
    all_to_all x1, starting transfers between devices, per_device(): gathered = lax.all_to_all(state, PLANE, 0, 0, tiled=True)  8.11 us
    ppermute x2, starting transfers between devices, swap(): return lax.ppermute(array, 'c', [(0, 1), (1, 0)])  8.1 us
    pallas_call x1, Pallas kernels, per_device(): call(scores_kernel, [own_spec(0), other_spec(0), rim_spec(0), taps_spec(0...  5.76 us
    pallas_call x1, Pallas kernels, per_device(): small_call(maps_kernel, [SCALAR] + [WHOLE] * 4, [WHOLE, WHOLE], [chip(HEA...  3.52 us
    pallas_call x1, Pallas kernels, per_device(): small_call(state_kernel, [SCALAR] * 2 + [WHOLE] * 7, [WHOLE] + [ANYWHERE]...  2.87 us
  transfers between devices with their start and end apart: 7, of which 3 were waited for; matrix products, arithmetic and copies ran while one was open for 0% of the time, Pallas kernels for 16%

profile of v4, /device:TPU:1, one launch (start us, length us, event | category | flops | bytes accessed | tf_op | source)
XLA Modules:
  0.0 81.3 jit_solution(7122776265055950816)
XLA Ops:
  0.0 1.4 %shard_map.38 = (bf16[3,128,2048]{2,1,0:T(8,128)(2,1)S(1)}, bf16[3,8,2048]{2,1,0:T(8,128)(2,1)S(1)}) custom-call(s32[1]{0:T(128)} %bitcast.core_ref, bf16[3,128,4096]{2,1,0:T(8,128)(2,1)} %own_q.1), custom_call_target="tpu_custom_call" | custom-call | bytes 3145728 | tf_op jit(solution)/shard_map/pallas_call | solution.py:376
  1.4 3.3 %collective-permute-start = (bf16[3,128,2048]{2,1,0:T(8,128)(2,1)S(1)}, bf16[3,128,2048]{2,1,0:T(8,128)(2,1)S(1)}, u32[]{:S(2)}, u32[]{:S(2)}) collective-permute-start(bf16[3,128,2048]{2,1,0:T(8,128)(2,1)S(1)} %get-tuple-element.22), channel_id=1, source_target_pairs={{0,1},{1,0},{2,3},{3,2},{4,5},{5,4},{6,7},{7,6},{8,9},{9,8},{10,11... | collective-permute-start | bytes 4718600 | tf_op jit(solution)/shard_map/ppermute | solution.py:368
  4.8 1.6 %shard_map.37 = (bf16[2,128,2048]{2,1,0:T(8,128)(2,1)S(1)}, f32[3,4,2048]{2,1,0:T(4,128)S(1)}, bf16[16,128,256]{2,1,0:T(8,128)(2,1)S(1)}) custom-call(s32[1]{0:T(128)} %bitcast.core_ref, bf16[3,128,4096]{2,1,0:T(8,128)(2,1)} %own_q.1, f32[3,4,4096]{2,1,0:T(4,128)} %taps_q.1, bf16[32,128,256]{2,1,0:T(8,128)(2,1)} %omega.3), custom_call_target="tpu_custom_call" | custom-call | bytes 5242880 | tf_op jit(solution)/shard_map/pallas_call | solution.py:392
  6.4 1.4 %collective-permute-done.other = bf16[3,128,2048]{2,1,0:T(8,128)(2,1)S(1)} collective-permute-done((bf16[3,128,2048]{2,1,0:T(8,128)(2,1)S(1)}, bf16[3,128,2048]{2,1,0:T(8,128)(2,1)S(1)}, u32[]{:S(2)}, u32[]{:S(2)}) %collective-permute-start) | collective-permute-done | bytes 1572896 | tf_op jit(solution)/shard_map/ppermute | solution.py:368
  7.8 1.5 %collective-permute-start.1 = (bf16[3,8,2048]{2,1,0:T(8,128)(2,1)S(1)}, bf16[3,8,2048]{2,1,0:T(8,128)(2,1)S(1)}, u32[]{:S(2)}, u32[]{:S(2)}) collective-permute-start(bf16[3,8,2048]{2,1,0:T(8,128)(2,1)S(1)} %shard_map.39), channel_id=1, source_target_pairs={{0,2},{1,3},{2,4},{3,5},{4,6},{5,7},{6,8},{7,9},{8,10},{9,11},{10,... | collective-permute-start | bytes 294920 | tf_op jit(solution)/shard_map/ppermute | solution.py:391
  9.3 3.5 %shard_map.40 = (bf16[16,256,256]{2,1,0:T(8,128)(2,1)S(1)}, bf16[16,256,128]{2,1,0:T(8,128)(2,1)S(1)}) custom-call(s32[1]{0:T(128)} %bitcast.core_ref, bf16[2,128,2048]{2,1,0:T(8,128)(2,1)S(1)} %get-tuple-element.21.own, bf16[3,128,2048]{2,1,0:T(8,128)(2,1)S(1)} %collective-permute-done.other, f32[3,4,2048]{2,1,0:T(4,128)S(1)} %get-tuple-element.24.taps, ...), custom_call_target="tpu_custom_call" | custom-call | flops 3000000000 | bytes 6291456 | tf_op jit(solution)/shard_map/pallas_call | solution.py:403
  12.8 0.0 collective-permute-done.1.rim.rim_q
  12.8 2.9 %shard_map.41 = (bf16[32,136,128]{2,1,0:T(8,128)(2,1)}, bf16[16,256,256]{2,1,0:T(8,128)(2,1)}, bf16[16,256,128]{2,1,0:T(8,128)(2,1)}, bf16[1,128,2048]{2,1,0:T(8,128)(2,1)}) custom-call(s32[1]{0:T(128)} %bitcast.core_ref, s32[1]{0:T(128)} %bitcast.1.flip_ref, bf16[2,128,2048]{2,1,0:T(8,128)(2,1)S(1)} %get-tuple-element.21.own, ...), custom_call_target="tpu_custom_call" | custom-call | flops 2000000000 | bytes 6291456 | tf_op jit(solution)/shard_map/pallas_call | solution.py:412
  15.7 8.1 %all-to-all-start = ((bf16[32,136,128]{2,1,0:T(8,128)(2,1)}), bf16[32,136,128]{2,1,0:T(8,128)(2,1)S(1)}, u32[]{:S(2)}, u32[]{:S(2)}) async-start(bf16[32,136,128]{2,1,0:T(8,128)(2,1)} %get-tuple-element.28), calls=%async_computation | async-start | bytes 2228224 | tf_op jit(solution)/shard_map/all_to_all | solution.py:424
  23.8 5.8 %shard_map.42 = (bf16[16,256,256]{2,1,0:T(8,128)(2,1)}, bf16[16,256,256]{2,1,0:T(8,128)(2,1)}) custom-call(s32[1]{0:T(128)} %bitcast.core_ref, bf16[3,128,4096]{2,1,0:T(8,128)(2,1)} %own_q.1, bf16[1,128,2048]{2,1,0:T(8,128)(2,1)} %get-tuple-element.29.other_q, bf16[3,8,2048]{2,1,0:T(8,128)(2,1)S(1)} %collective-permute-done.1.rim.rim_q, ...), custom_call_target="tpu_custom_call" | custom-call | flops 8000000000 | bytes 20971520 | tf_op jit(solution)/shard_map/pallas_call | solution.py:426
  29.6 9.9 %all-to-all-done.sums = bf16[32,136,128]{2,1,0:T(8,128)(2,1)S(1)} async-done(((bf16[32,136,128]{2,1,0:T(8,128)(2,1)}), bf16[32,136,128]{2,1,0:T(8,128)(2,1)S(1)}, u32[]{:S(2)}, u32[]{:S(2)}) %all-to-all-start) | async-done | bytes 1114144 | tf_op jit(solution)/shard_map/all_to_all | solution.py:424
  39.5 0.0 copy-start.2
  39.5 0.2 shard_map.43
  39.7 0.0 copy-start
  39.7 0.0 copy-start.1
  39.7 6.1 %collective-permute-start.4 = (bf16[136,128]{1,0:T(8,128)(2,1)S(1)}, bf16[136,128]{1,0:T(8,128)(2,1)S(1)}, u32[]{:S(2)}, u32[]{:S(2)}) collective-permute-start(bf16[136,128]{1,0:T(8,128)(2,1)S(1)} %shard_map.43), channel_id=1, source_target_pairs={{0,64},{32,96},{64,160},{96,128},{160,224},{128,192},{1,65},{33,97... | collective-permute-start | bytes 104456 | tf_op jit(solution)/shard_map/ppermute | solution.py:446
  45.8 4.9 %collective-permute-start.3 = (bf16[136,128]{1,0:T(8,128)(2,1)S(1)}, bf16[136,128]{1,0:T(8,128)(2,1)S(1)}, u32[]{:S(2)}, u32[]{:S(2)}) collective-permute-start(bf16[136,128]{1,0:T(8,128)(2,1)S(1)} %shard_map.43), channel_id=1, source_target_pairs={{0,160},{32,128},{64,224},{96,192},{1,161},{33,129},{65,225},{97,1... | collective-permute-start | bytes 104456 | tf_op jit(solution)/shard_map/ppermute | solution.py:446
  50.7 1.3 %collective-permute-start.2 = (bf16[136,128]{1,0:T(8,128)(2,1)S(1)}, bf16[136,128]{1,0:T(8,128)(2,1)S(1)}, u32[]{:S(2)}, u32[]{:S(2)}) collective-permute-start(bf16[136,128]{1,0:T(8,128)(2,1)S(1)} %shard_map.43), channel_id=1, source_target_pairs={{0,224},{32,192},{1,225},{33,193},{2,226},{34,194},{3,227},{35,195... | collective-permute-start | bytes 104456 | tf_op jit(solution)/shard_map/ppermute | solution.py:446
  52.0 0.0 collective-permute-done.4.before_3
  52.1 0.0 collective-permute-done.3.before_2
  52.1 1.0 %collective-permute-done.2.before_1 = bf16[136,128]{1,0:T(8,128)(2,1)S(1)} collective-permute-done((bf16[136,128]{1,0:T(8,128)(2,1)S(1)}, bf16[136,128]{1,0:T(8,128)(2,1)S(1)}, u32[]{:S(2)}, u32[]{:S(2)}) %collective-permute-start.2) | collective-permute-done | bytes 34848 | tf_op jit(solution)/shard_map/ppermute | solution.py:446
  53.1 0.2 shard_map.44
  53.3 19.3 %all_to_all.10.state = bf16[32,136,128]{2,1,0:T(8,128)(2,1)S(1)} all-to-all(bf16[32,136,128]{2,1,0:T(8,128)(2,1)S(1)} %shard_map.44), channel_id=1, replica_groups=mesh['zh'=4,'zl'=2,'x'=4,'y'=4,'c'=2] {'zl','x','y'}, dimensions={0} | all-to-all | bytes 2228224 | tf_op jit(solution)/shard_map/all_to_all | solution.py:461
  72.6 0.0 copy-done.2
  72.6 0.0 copy-done
  72.6 0.0 copy-done.1
  72.6 1.2 %shard_map.45 = bf16[128,2048]{1,0:T(8,128)(2,1)S(1)} custom-call(s32[1]{0:T(128)} %bitcast.core_ref, s32[1]{0:T(128)} %bitcast.1.flip_ref, bf16[16,256,256]{2,1,0:T(8,128)(2,1)S(1)} %copy-done.1, bf16[16,256,256]{2,1,0:T(8,128)(2,1)S(1)} %copy-done, bf16[16,256,128]{2,1,0:T(8,128)(2,1)S(1)} %copy-done.2, bf16[32,136,128]{2,1,0:T(8,128)(2,1)S(1)} %all_to_all.10.state), custom_call_target="tpu_custom_call" | custom-call | flops 2000000000 | bytes 4194304 | tf_op jit(solution)/shard_map/pallas_call | solution.py:463
  73.8 4.8 %collective-permute-start.5 = (bf16[128,2048]{1,0:T(8,128)(2,1)S(1)}, bf16[128,2048]{1,0:T(8,128)(2,1)S(1)}, u32[]{:S(2)}, u32[]{:S(2)}) collective-permute-start(bf16[128,2048]{1,0:T(8,128)(2,1)S(1)} %shard_map.45), channel_id=1, source_target_pairs={{0,1},{1,0},{2,3},{3,2},{4,5},{5,4},{6,7},{7,6},{8,9},{9,8},{10,11... | collective-permute-start | bytes 1572872 | tf_op jit(solution)/shard_map/ppermute | solution.py:368
  78.6 1.9 %shard_map.46.partial = bf16[128,4096]{1,0:T(8,128)(2,1)} custom-call(s32[1]{0:T(128)} %bitcast.core_ref, s32[1]{0:T(128)} %bitcast.1.flip_ref, bf16[16,256,256]{2,1,0:T(8,128)(2,1)S(1)} %copy-done.1, bf16[16,256,256]{2,1,0:T(8,128)(2,1)S(1)} %copy-done, bf16[16,256,128]{2,1,0:T(8,128)(2,1)S(1)} %copy-done.2, bf16[32,136,128]{2,1,0:T(8,128)(2,1)S(1)} %all_to_all.10.state), custom_call_target="tpu_custom_call" | custom-call | flops 2000000000 | bytes 4194304 | tf_op jit(solution)/shard_map/pallas_call | solution.py:468
  80.5 0.0 collective-permute-done.5.arrived
  80.5 0.8 %shard_map.47 = bf16[128,4096]{1,0:T(8,128)(2,1)} custom-call(s32[1]{0:T(128)} %bitcast.core_ref, bf16[128,2048]{1,0:T(8,128)(2,1)S(1)} %collective-permute-done.5.arrived, bf16[128,4096]{1,0:T(8,128)(2,1)} %shard_map.46.partial), custom_call_target="tpu_custom_call", output_to_operand_aliasing={{}: (2, {})} | custom-call | bytes 1048576 | tf_op jit(solution)/shard_map/pallas_call | solution.py:473
  (1 shorter events, 0.0 us)
Async XLA Ops:
  1.4 6.4 %collective-permute-start = (bf16[3,128,2048]{2,1,0:T(8,128)(2,1)S(1)}, bf16[3,128,2048]{2,1,0:T(8,128)(2,1)S(1)}, u32[]{:S(2)}, u32[]{:S(2)}) collective-permute-start(bf16[3,128,2048]{2,1,0:T(8,128)(2,1)S(1)} %get-tuple-element.22), channel_id=1, source_target_pairs={{0,1},{1,0},{2,3},{3,2},{4,5},{5,4},{6,7},{7,6},{8,9},{9,8},{10,11... | collective-permute-start | bytes 4718600 | tf_op jit(solution)/shard_map/ppermute | solution.py:368
  7.8 5.0 %collective-permute-start.1 = (bf16[3,8,2048]{2,1,0:T(8,128)(2,1)S(1)}, bf16[3,8,2048]{2,1,0:T(8,128)(2,1)S(1)}, u32[]{:S(2)}, u32[]{:S(2)}) collective-permute-start(bf16[3,8,2048]{2,1,0:T(8,128)(2,1)S(1)} %shard_map.39), channel_id=1, source_target_pairs={{0,2},{1,3},{2,4},{3,5},{4,6},{5,7},{6,8},{7,9},{8,10},{9,11},{10,... | collective-permute-start | bytes 294920 | tf_op jit(solution)/shard_map/ppermute | solution.py:391
  15.7 23.8 %all-to-all-start = ((bf16[32,136,128]{2,1,0:T(8,128)(2,1)}), bf16[32,136,128]{2,1,0:T(8,128)(2,1)S(1)}, u32[]{:S(2)}, u32[]{:S(2)}) async-start(bf16[32,136,128]{2,1,0:T(8,128)(2,1)} %get-tuple-element.28), calls=%async_computation | async-start | bytes 2228224 | tf_op jit(solution)/shard_map/all_to_all | solution.py:424
  39.5 33.1 %copy-start.2 = (bf16[16,256,128]{2,1,0:T(8,128)(2,1)S(1)}, bf16[16,256,128]{2,1,0:T(8,128)(2,1)}, u32[]{:S(2)}) copy-start(bf16[16,256,128]{2,1,0:T(8,128)(2,1)} %get-tuple-element.35.values) | copy-start | bytes 3145732
  39.7 32.9 %copy-start = (bf16[16,256,256]{2,1,0:T(8,128)(2,1)S(1)}, bf16[16,256,256]{2,1,0:T(8,128)(2,1)}, u32[]{:S(2)}) copy-start(bf16[16,256,256]{2,1,0:T(8,128)(2,1)} %get-tuple-element.34.query_map) | copy-start | bytes 6291460
  39.7 32.9 %copy-start.1 = (bf16[16,256,256]{2,1,0:T(8,128)(2,1)S(1)}, bf16[16,256,256]{2,1,0:T(8,128)(2,1)}, u32[]{:S(2)}) copy-start(bf16[16,256,256]{2,1,0:T(8,128)(2,1)} %get-tuple-element.33.scores) | copy-start | bytes 6291460
  39.7 12.4 %collective-permute-start.4 = (bf16[136,128]{1,0:T(8,128)(2,1)S(1)}, bf16[136,128]{1,0:T(8,128)(2,1)S(1)}, u32[]{:S(2)}, u32[]{:S(2)}) collective-permute-start(bf16[136,128]{1,0:T(8,128)(2,1)S(1)} %shard_map.43), channel_id=1, source_target_pairs={{0,64},{32,96},{64,160},{96,128},{160,224},{128,192},{1,65},{33,97... | collective-permute-start | bytes 104456 | tf_op jit(solution)/shard_map/ppermute | solution.py:446
  45.8 6.2 %collective-permute-start.3 = (bf16[136,128]{1,0:T(8,128)(2,1)S(1)}, bf16[136,128]{1,0:T(8,128)(2,1)S(1)}, u32[]{:S(2)}, u32[]{:S(2)}) collective-permute-start(bf16[136,128]{1,0:T(8,128)(2,1)S(1)} %shard_map.43), channel_id=1, source_target_pairs={{0,160},{32,128},{64,224},{96,192},{1,161},{33,129},{65,225},{97,1... | collective-permute-start | bytes 104456 | tf_op jit(solution)/shard_map/ppermute | solution.py:446
  50.7 2.4 %collective-permute-start.2 = (bf16[136,128]{1,0:T(8,128)(2,1)S(1)}, bf16[136,128]{1,0:T(8,128)(2,1)S(1)}, u32[]{:S(2)}, u32[]{:S(2)}) collective-permute-start(bf16[136,128]{1,0:T(8,128)(2,1)S(1)} %shard_map.43), channel_id=1, source_target_pairs={{0,224},{32,192},{1,225},{33,193},{2,226},{34,194},{3,227},{35,195... | collective-permute-start | bytes 104456 | tf_op jit(solution)/shard_map/ppermute | solution.py:446
  73.8 6.7 %collective-permute-start.5 = (bf16[128,2048]{1,0:T(8,128)(2,1)S(1)}, bf16[128,2048]{1,0:T(8,128)(2,1)S(1)}, u32[]{:S(2)}, u32[]{:S(2)}) collective-permute-start(bf16[128,2048]{1,0:T(8,128)(2,1)S(1)} %shard_map.45), channel_id=1, source_target_pairs={{0,1},{1,0},{2,3},{3,2},{4,5},{5,4},{6,7},{7,6},{8,9},{9,8},{10,11... | collective-permute-start | bytes 1572872 | tf_op jit(solution)/shard_map/ppermute | solution.py:368

commit v5 on v4

--- a/solution.py
+++ b/solution.py
@@ -37,6 +37,7 @@
 f32 = jnp.float32
 bf16 = jnp.bfloat16
 NT = (((1,), (1,)), ((), ()))
+TN = (((0,), (0,)), ((), ()))
 
 
 def dot(a, b):
@@ -69,8 +70,21 @@
     return jnp.exp2(projection * (FEATURE_SCALE * LOG2_E)).astype(bf16)
 
 
-def maps_kernel(core_ref, own, other, taps, omega, maps, convolved, rows_k, rows_v):
+def key_map_of(k, omega, ones):
+    k_wide = k.astype(f32)
+    square = k_wide * k_wide
+    upper = square.astype(bf16)
+    lower = (square - upper.astype(f32)).astype(bf16)
+    norm = dot(jnp.concatenate([upper, lower], axis=1), ones)
+    return key_features(dot(k, omega), norm)
+
+
+def maps_kernel(
+    core_ref, own, other, taps, omega, partial, other_out, rows_k, rows_v, sem
+):
     core = core_ref[0]
+    move = pltpu.make_async_copy(other, other_out, sem)
+    move.start()
     ones = jnp.ones((M, M), bf16)
     for part in range(GROUP):
         rows_k[part, 0:RIM, :] = jnp.zeros((RIM, DH), f32)
@@ -83,16 +97,15 @@
             fill(core, own.at[0, :, cols], other.at[1, :, cols], rows_k.at[part])
             fill(core, own.at[1, :, cols], other.at[2, :, cols], rows_v.at[part])
             k = convolve(rows_k.at[part], taps[1, :, cols], CHUNK)
-            convolved[head] = convolve(rows_v.at[part], taps[2, :, cols], CHUNK)
-            k_wide = k.astype(f32)
-            square = k_wide * k_wide
-            upper = square.astype(bf16)
-            lower = (square - upper.astype(f32)).astype(bf16)
-            norm = dot(jnp.concatenate([upper, lower], axis=1), ones)
-            maps[head] = key_features(dot(k, omega[head]), norm)
+            v = convolve(rows_v.at[part], taps[2, :, cols], CHUNK)
+            extended = jnp.concatenate([v.T, jnp.ones((16, CHUNK), bf16)], axis=0)
+            mapped = key_map_of(k, omega[head], ones)
+            mapped = jnp.concatenate([jnp.zeros((EDGE, M), bf16), mapped[EDGE:]], axis=0)
+            partial[head] = dot(extended, mapped)[:STATE_ROWS]
         return carried
 
-    lax.fori_loop(0, STEPS, one, 0)
+    lax.fori_loop(0, STEPS, one, 0, unroll=2)
+    move.wait()
 
 
 def piece_of(head, flip):
@@ -100,75 +113,67 @@
 
 
 def state_kernel(
-    core_ref, flip_ref, own, other, rim, taps, omega, maps, convolved,
-    state, key_map, values, other_q, rows_k, rows_v, edge_k, edge_v, sems,
+    core_ref, flip_ref, own, other, rim, taps, omega, partial, state, rows_k, rows_v
 ):
     core = core_ref[0]
-    late = pl.ds(EDGE, CHUNK - EDGE)
-    early = pl.ds(0, EDGE)
-    moves = [
-        pltpu.make_async_copy(maps.at[:, late, :], key_map.at[:, late, :], sems.at[0]),
-        pltpu.make_async_copy(convolved.at[:, late, :], values.at[:, late, :], sems.at[1]),
-        pltpu.make_async_copy(other.at[pl.ds(0, 1)], other_q, sems.at[2]),
-    ]
-    for move in moves:
-        move.start()
-
-    def edge(group, carried):
-        for part in range(GROUP):
-            head = group * GROUP + part
-            cols = columns(head * DH, DH)
-            for which, rows in ((0, rows_k), (1, rows_v)):
-                rows[part, 0:RIM, :] = rim[which + 1, :, cols].astype(f32)
-                mine = own[which, 0:EDGE, cols].astype(f32)
-                theirs = other[which + 1, 0:EDGE, cols].astype(f32)
-                rows[part, RIM : RIM + EDGE, :] = jnp.where(core == 0, mine, theirs)
-            k = convolve(rows_k.at[part], taps[1, :, cols], EDGE)
-            k_wide = k.astype(f32)
-            norm = jnp.sum(k_wide * k_wide, axis=1, keepdims=True)
-            edge_k[head] = key_features(dot(k, omega[head]), norm)
-            edge_v[head] = convolve(rows_v.at[part], taps[2, :, cols], EDGE)
-        return carried
-
-    def one(group, carried):
-        for part in range(GROUP):
-            head = group * GROUP + part
-            mapped = jnp.concatenate([edge_k[head], maps[head, EDGE:, :]], axis=0)
-            v = jnp.concatenate([edge_v[head], convolved[head, EDGE:, :]], axis=0)
-            extended = jnp.concatenate([v.T, jnp.ones((16, CHUNK), bf16)], axis=0)
-            sums = dot(extended, mapped)[:STATE_ROWS].astype(bf16)
-            piece = piece_of(head, flip_ref[0])
-            state[piece] = sums[:, : M // 2]
-            state[piece + 1] = sums[:, M // 2 :]
-        return carried
-
-    lax.fori_loop(0, STEPS, edge, 0, unroll=2)
-    last = [
-        pltpu.make_async_copy(edge_k, key_map.at[:, early, :], sems.at[3]),
-        pltpu.make_async_copy(edge_v, values.at[:, early, :], sems.at[4]),
-    ]
-    for move in last:
-        move.start()
-    lax.fori_loop(0, STEPS, one, 0, unroll=2)
-    for move in moves + last:
-        move.wait()
+
+    flip = flip_ref[0]
+    heads = range(HEADS)
+    keys, features = [], []
+    for head in heads:
+        cols = slice(head * DH, (head + 1) * DH)
+        for which, rows in ((0, rows_k), (1, rows_v)):
+            rows[head, 0:RIM, :] = rim[which + 1, :, cols].astype(f32)
+            mine = own[which, 0:EDGE, cols].astype(f32)
+            theirs = other[which + 1, 0:EDGE, cols].astype(f32)
+            rows[head, RIM : RIM + EDGE, :] = jnp.where(core == 0, mine, theirs)
+    for head in heads:
+        cols = slice(head * DH, (head + 1) * DH)
+        k = convolve(rows_k.at[head], taps[1, :, cols], EDGE)
+        k_wide = k.astype(f32)
+        keys.append((k, jnp.sum(k_wide * k_wide, axis=1, keepdims=True)))
+    for head in heads:
+        k, norm = keys[head]
+        features.append(key_features(dot(k, omega[head]), norm))
+    for head in heads:
+        cols = slice(head * DH, (head + 1) * DH)
+        v = convolve(rows_v.at[head], taps[2, :, cols], EDGE)
+        first = features[head]
+        products = lax.dot_general(v, first, TN, preferred_element_type=f32)
+        total = jnp.sum(first.astype(f32), axis=0, keepdims=True)
+        total = jnp.broadcast_to(total, (STATE_ROWS - DH, M))
+        sums = (partial[head] + jnp.concatenate([products, total], axis=0)).astype(bf16)
+        piece = piece_of(head, flip)
+        state[piece] = sums[:, : M // 2]
+        state[piece + 1] = sums[:, M // 2 :]
 
 
 def scores_kernel(
-    core_ref, own_q, other_q, rim_q, taps_q, omega, key_map, query_map, scores, rows_q
+    core_ref, own_q, own_k, own_v, other_q, other_k, other_v, rim_q, rim_k, rim_v,
+    taps_q, taps_k, taps_v, omega, query_map, block, rows_q, rows_k, rows_v,
 ):
     core = core_ref[0]
+    ones = jnp.ones((M, M), bf16)
     causal = lax.broadcasted_iota(jnp.int32, (CHUNK, CHUNK), 0) >= lax.broadcasted_iota(
         jnp.int32, (CHUNK, CHUNK), 1
     )
     for head in range(GROUP):
         cols = slice(head * DH, (head + 1) * DH)
-        rows_q[head, 0:RIM, :] = rim_q[0, :, cols].astype(f32)
-        fill(core, own_q.at[0, :, cols], other_q.at[0, :, cols], rows_q.at[head])
-        q = convolve(rows_q.at[head], taps_q[0, :, cols], CHUNK)
-        mapped = query_features(dot(q, omega[head]))
-        query_map[head] = mapped
-        scores[head] = jnp.where(causal, dot_nt(mapped, key_map[head]), 0.0).astype(bf16)
+        convolved = []
+        for own, other, rim, taps, rows in (
+            (own_q, other_q, rim_q, taps_q, rows_q),
+            (own_k, other_k, rim_k, taps_k, rows_k),
+            (own_v, other_v, rim_v, taps_v, rows_v),
+        ):
+            rows[head, 0:RIM, :] = rim[0, :, cols].astype(f32)
+            fill(core, own.at[0, :, cols], other.at[0, :, cols], rows.at[head])
+            convolved.append(convolve(rows.at[head], taps[0, :, cols], CHUNK))
+        q, k, v = convolved
+        queries = query_features(dot(q, omega[head]))
+        query_map[head] = queries
+        products = dot_nt(queries, key_map_of(k, omega[head], ones))
+        scores = jnp.where(causal, products, 0.0).astype(bf16)
+        block[head] = dot(scores, jnp.concatenate([v, ones[:, :DH]], axis=1))
 
 
 def total_kernel(sums, out):
@@ -185,15 +190,13 @@
         running = running + sums[i].astype(f32)
 
 
-def attend_rows(rows, flip, scores, query_map, values, state, put, group):
-    ones = jnp.ones((CHUNK, DH), bf16)
+def attend_rows(rows, flip, block, query_map, state, put, group):
     for head in range(group * GROUP, (group + 1) * GROUP):
         piece = piece_of(head, flip)
         prior = jnp.concatenate([state[piece], state[piece + 1]], axis=1)
         total = jnp.broadcast_to(prior[DH : DH + 1], (DH, M))
         prior = jnp.concatenate([prior[:DH], total], axis=0)
-        both = dot(scores[head, rows, :], jnp.concatenate([values[head], ones], axis=1))
-        both = both + dot_nt(query_map[head, rows, :], prior)
+        both = block[head, rows, :] + dot_nt(query_map[head, rows, :], prior)
         put(head, (both[:, :DH] / both[:, DH:]).astype(bf16))
 
 
@@ -201,7 +204,7 @@
     return pl.ds(pl.multiple_of(start, DH), size)
 
 
-def attend_other_kernel(core_ref, flip_ref, scores, query_map, values, state, out):
+def attend_other_kernel(core_ref, flip_ref, block, query_map, state, out):
     start = pl.multiple_of((1 - core_ref[0]) * ROWS, ROWS)
 
     def put(head, block):
@@ -209,12 +212,12 @@
 
     for group in range(STEPS):
         attend_rows(
-            pl.ds(start, ROWS), flip_ref[0], scores, query_map, values, state, put, group
+            pl.ds(start, ROWS), flip_ref[0], block, query_map, state, put, group
         )
 
 
 def attend_own_kernel(
-    core_ref, flip_ref, scores, query_map, values, state, out, block_rows, sems
+    core_ref, flip_ref, block, query_map, state, out, block_rows, sems
 ):
     core = core_ref[0]
     rows = pl.ds(pl.multiple_of(core * ROWS, ROWS), ROWS)
@@ -230,7 +233,7 @@
         )
 
     for group in range(STEPS):
-        attend_rows(rows, flip_ref[0], scores, query_map, values, state, put, group)
+        attend_rows(rows, flip_ref[0], block, query_map, state, put, group)
         copy(group).start()
     for group in range(STEPS):
         copy(group).wait()
@@ -282,6 +285,10 @@
         (omega.at[pl.ds(core_ref[0] * HEADS, HEADS)], own_omega),
     ]
     run_copies(pairs, sems)
+
+
+def load_kernel(query_map, block, query_map_out, block_out, sems):
+    run_copies([(query_map, query_map_out), (block, block_out)], sems)
 
 
 def spec(shape, index):
@@ -399,41 +406,44 @@
         moved=5 * 2**20,
     )(cores, projected, conv_filter, frequencies)
     own, own_taps, own_omega, rim = in_chip(*fetched, rim)
-    raw = [pltpu.VMEM((GROUP, RIM + CHUNK, DH), f32)] * 2
-    maps, convolved = small_call(
+    raw = [pltpu.VMEM((GROUP, RIM + CHUNK, DH), f32)]
+    partial, other_main = small_call(
         maps_kernel,
         [SCALAR] + [WHOLE] * 4,
-        [WHOLE, WHOLE],
-        [chip(HEADS, CHUNK, M), chip(HEADS, CHUNK, DH)],
-        raw,
+        [WHOLE, ANYWHERE],
+        [pltpu.VMEM((HEADS, STATE_ROWS, M), f32), main(3, ROWS, COLS)],
+        raw * 2 + [pltpu.SemaphoreType.DMA],
         flops=3 * 10**9,
         moved=6 * 2**20,
     )(cores, own, other, own_taps, own_omega)
-    state, key_map, values, other_q = small_call(
+    state = small_call(
         state_kernel,
-        [SCALAR] * 2 + [WHOLE] * 7,
-        [WHOLE] + [ANYWHERE] * 3,
-        [chip(PIECES, STATE_ROWS, M // 2), main(HEADS, CHUNK, M), main(HEADS, CHUNK, DH)]
-        + [main(1, ROWS, COLS)],
-        [pltpu.VMEM((GROUP, RIM + EDGE, DH), f32)] * 2
-        + [pltpu.VMEM((HEADS, EDGE, M), bf16), pltpu.VMEM((HEADS, EDGE, DH), bf16)]
-        + [pltpu.SemaphoreType.DMA((5,))],
+        [SCALAR] * 2 + [WHOLE] * 6,
+        WHOLE,
+        chip(PIECES, STATE_ROWS, M // 2),
+        [pltpu.VMEM((HEADS, RIM + EDGE, DH), f32)] * 2,
         flops=2 * 10**9,
         moved=6 * 2**20,
-    )(cores, flips, own, other, rim, own_taps, own_omega, *in_chip(maps, convolved))
+    )(cores, flips, own, other, rim, own_taps, own_omega, *in_chip(partial))
     gathered = lax.all_to_all(state, PLANE, 0, 0, tiled=True)
-    key_map, values, other_q = in_main(key_map, values, other_q)
-    query_map, scores = call(
+    (other_main,) = in_main(other_main)
+    which = range(3)
+    query_map, block = call(
         scores_kernel,
-        [own_spec(0), other_spec(0), rim_spec(0), taps_spec(0), OMEGA_SPEC]
-        + [head_spec(CHUNK, M)],
-        [head_spec(CHUNK, M), head_spec(CHUNK, CHUNK)],
-        [main(HEADS, CHUNK, M), main(HEADS, CHUNK, CHUNK)],
-        [pltpu.VMEM((GROUP, RIM + CHUNK, DH), f32)],
+        [own_spec(w) for w in which]
+        + [other_spec(w) for w in which]
+        + [rim_spec(w) for w in which]
+        + [taps_spec(w) for w in which]
+        + [OMEGA_SPEC],
+        [head_spec(CHUNK, M), head_spec(CHUNK, 2 * DH)],
+        [main(HEADS, CHUNK, M), pltpu.HBM((HEADS, CHUNK, 2 * DH), f32)],
+        raw * 3,
         flops=8 * 10**9,
         moved=20 * 2**20,
-    )(cores, projected, other_q, rim, conv_filter, frequencies, key_map)
-    gathered, query_map, scores = lax.optimization_barrier((gathered, query_map, scores))
+    )(
+        cores, *[projected] * 3, *[other_main] * 3, *[rim] * 3, *[conv_filter] * 3, frequencies
+    )
+    gathered, query_map, block = lax.optimization_barrier((gathered, query_map, block))
     total = small_call(
         total_kernel, [WHOLE], WHOLE, chip(STATE_ROWS, M // 2), [], flops=10**6, moved=2**20
     )(*in_chip(gathered))
@@ -458,15 +468,21 @@
         prefix_kernel, [WHOLE] * 4, WHOLE, chip(PIECES, STATE_ROWS, M // 2), [],
         flops=10**6, moved=2 * 2**20,
     )(*in_chip(*before, gathered))
+    query_map, block = small_call(
+        load_kernel, [ANYWHERE] * 2, [WHOLE] * 2,
+        [chip(HEADS, CHUNK, M), pltpu.VMEM((HEADS, CHUNK, 2 * DH), f32)],
+        [pltpu.SemaphoreType.DMA((2,))], flops=0, moved=12 * 2**20,
+    )(*in_main(query_map, block))
+    prior, query_map, block = lax.optimization_barrier((prior, query_map, block))
     prior = lax.all_to_all(prior, PLANE, 0, 0, tiled=True)
-    operands = in_chip(scores, query_map, values, prior)
+    operands = in_chip(block, query_map, prior)
     attended = small_call(
-        attend_other_kernel, [SCALAR] * 2 + [WHOLE] * 4, WHOLE, chip(ROWS, COLS), [],
+        attend_other_kernel, [SCALAR] * 2 + [WHOLE] * 3, WHOLE, chip(ROWS, COLS), [],
         flops=2 * 10**9, moved=4 * 2**20,
     )(cores, flips, *operands)
     arrived = swap(attended)
     partial = small_call(
-        attend_own_kernel, [SCALAR] * 2 + [WHOLE] * 4, ANYWHERE, main(ROWS, D),
+        attend_own_kernel, [SCALAR] * 2 + [WHOLE] * 3, ANYWHERE, main(ROWS, D),
         [pltpu.VMEM((ROWS, COLS), bf16), pltpu.SemaphoreType.DMA((STEPS,))],
         flops=2 * 10**9, moved=4 * 2**20,
     )(cores, flips, *operands)

time: 81.7 us -> 82.2 us (level)
  Pallas kernels: 19.5 us -> 25.2 us
  waiting for transfers between devices: 12.4 us -> 7.34 us
  starting transfers between devices: 30 us -> 28.6 us
  blocking collectives: 19.3 us -> 20.6 us
    pallas_call x5 -> x6, Pallas kernels: 15.2 us -> 20.9 us  [the longest x1 9.78 us: per_device(): call(scores_kernel, [own_spec(w) for w in which] + [other_spec(w) for w i...]
    all_to_all x1, waiting for transfers between devices: 9.89 us -> 5.89 us  [per_device(): gathered = lax.all_to_all(state, PLANE, 0, 0, tiled=True)]
    all_to_all x1, blocking collectives: 19.3 us -> 20.6 us  [per_device(): prior = lax.all_to_all(prior, PLANE, 0, 0, tiled=True)]
    ppermute x2, starting transfers between devices: 8.1 us -> 6.85 us  [swap(): return lax.ppermute(array, 'c', [(0, 1), (1, 0)])]
    ppermute x3, waiting for transfers between devices: 1.04 us -> 0.01 us  [per_device(): lax.ppermute(total, ('zh', 'zl'), [(owner(group, plane), owner(group + by...]
  transfers between devices with their start and end apart: 7 -> 7, of which waited for: 3 -> 2; matrix products, arithmetic and copies ran while one was open for 0% -> 0% of each run, Pallas kernels for 16% -> 24%
where the time goes in v5:
time: 82.2 us; the launch traced here: 81.8 us
  starting transfers between devices  28.6 us (35%)
  Pallas kernels  25.2 us (31%)
  blocking collectives  20.6 us (25%)
  waiting for transfers between devices  7.34 us (9%)
    all_to_all x1, blocking collectives, per_device(): prior = lax.all_to_all(prior, PLANE, 0, 0, tiled=True)  20.6 us
    ppermute x3, starting transfers between devices, per_device(): lax.ppermute(total, ('zh', 'zl'), [(owner(group, plane), owner(group + by...  12.2 us
    pallas_call x1, Pallas kernels, per_device(): call(scores_kernel, [own_spec(w) for w in which] + [other_spec(w) for w i...  9.78 us
    all_to_all x1, starting transfers between devices, per_device(): gathered = lax.all_to_all(state, PLANE, 0, 0, tiled=True)  8.1 us
    ppermute x2, starting transfers between devices, swap(): return lax.ppermute(array, 'c', [(0, 1), (1, 0)])  6.85 us
    all_to_all x1, waiting for transfers between devices, per_device(): gathered = lax.all_to_all(state, PLANE, 0, 0, tiled=True)  5.89 us
    pallas_call x1, Pallas kernels, per_device(): small_call(maps_kernel, [SCALAR] + [WHOLE] * 4, [WHOLE, ANYWHERE], [pltpu...  4.19 us
    pallas_call x1, Pallas kernels, per_device(): small_call(load_kernel, [ANYWHERE] * 2, [WHOLE] * 2, [chip(HEADS, CHUNK,...  2.84 us
  transfers between devices with their start and end apart: 7, of which 2 were waited for; matrix products, arithmetic and copies ran while one was open for 0% of the time, Pallas kernels for 24%

profile of v5, /device:TPU:1, one launch (start us, length us, event | category | flops | bytes accessed | tf_op | source)
XLA Modules:
  0.0 81.8 jit_solution(12425718661148346351)
XLA Ops:
  0.0 1.4 %shard_map.38 = (bf16[3,128,2048]{2,1,0:T(8,128)(2,1)S(1)}, bf16[3,8,2048]{2,1,0:T(8,128)(2,1)S(1)}) custom-call(s32[1]{0:T(128)} %bitcast.core_ref, bf16[3,128,4096]{2,1,0:T(8,128)(2,1)} %own_v.1), custom_call_target="tpu_custom_call" | custom-call | bytes 3145728 | tf_op jit(solution)/shard_map/pallas_call | solution.py:383
  1.4 3.3 %collective-permute-start = (bf16[3,128,2048]{2,1,0:T(8,128)(2,1)S(1)}, bf16[3,128,2048]{2,1,0:T(8,128)(2,1)S(1)}, u32[]{:S(2)}, u32[]{:S(2)}) collective-permute-start(bf16[3,128,2048]{2,1,0:T(8,128)(2,1)S(1)} %get-tuple-element.23), channel_id=1, source_target_pairs={{0,1},{1,0},{2,3},{3,2},{4,5},{5,4},{6,7},{7,6},{8,9},{9,8},{10,11... | collective-permute-start | bytes 4718600 | tf_op jit(solution)/shard_map/ppermute | solution.py:375
  4.8 1.6 %shard_map.37 = (bf16[2,128,2048]{2,1,0:T(8,128)(2,1)S(1)}, f32[3,4,2048]{2,1,0:T(4,128)S(1)}, bf16[16,128,256]{2,1,0:T(8,128)(2,1)S(1)}) custom-call(s32[1]{0:T(128)} %bitcast.core_ref, bf16[3,128,4096]{2,1,0:T(8,128)(2,1)} %own_v.1, f32[3,4,4096]{2,1,0:T(4,128)} %taps_v.1, bf16[32,128,256]{2,1,0:T(8,128)(2,1)} %omega.3), custom_call_target="tpu_custom_call" | custom-call | bytes 5242880 | tf_op jit(solution)/shard_map/pallas_call | solution.py:399
  6.4 1.4 %collective-permute-done.other = bf16[3,128,2048]{2,1,0:T(8,128)(2,1)S(1)} collective-permute-done((bf16[3,128,2048]{2,1,0:T(8,128)(2,1)S(1)}, bf16[3,128,2048]{2,1,0:T(8,128)(2,1)S(1)}, u32[]{:S(2)}, u32[]{:S(2)}) %collective-permute-start) | collective-permute-done | bytes 1572896 | tf_op jit(solution)/shard_map/ppermute | solution.py:375
  7.8 1.5 %collective-permute-start.1 = (bf16[3,8,2048]{2,1,0:T(8,128)(2,1)S(1)}, bf16[3,8,2048]{2,1,0:T(8,128)(2,1)S(1)}, u32[]{:S(2)}, u32[]{:S(2)}) collective-permute-start(bf16[3,8,2048]{2,1,0:T(8,128)(2,1)S(1)} %shard_map.39), channel_id=1, source_target_pairs={{0,2},{1,3},{2,4},{3,5},{4,6},{5,7},{6,8},{7,9},{8,10},{9,11},{10,... | collective-permute-start | bytes 294920 | tf_op jit(solution)/shard_map/ppermute | solution.py:398
  9.3 4.2 %shard_map.40 = (f32[16,136,256]{2,1,0:T(8,128)S(1)}, bf16[3,128,2048]{2,1,0:T(8,128)(2,1)}) custom-call(s32[1]{0:T(128)} %bitcast.core_ref, bf16[2,128,2048]{2,1,0:T(8,128)(2,1)S(1)} %get-tuple-element.22.own, bf16[3,128,2048]{2,1,0:T(8,128)(2,1)S(1)} %collective-permute-done.other, f32[3,4,2048]{2,1,0:T(4,128)S(1)} %get-tuple-element.25.taps, ...), custom_call_target="tpu_custom_call" | custom-call | flops 3000000000 | bytes 6291456 | tf_op jit(solution)/shard_map/pallas_call | solution.py:410
  13.5 0.0 collective-permute-done.1.rim.rim_q.rim_k.rim_v
  13.5 1.7 %shard_map.41 = bf16[32,136,128]{2,1,0:T(8,128)(2,1)} custom-call(s32[1]{0:T(128)} %bitcast.core_ref, s32[1]{0:T(128)} %bitcast.1.flip_ref, bf16[2,128,2048]{2,1,0:T(8,128)(2,1)S(1)} %get-tuple-element.22.own, bf16[3,128,2048]{2,1,0:T(8,128)(2,1)S(1)} %collective-permute-done.other, bf16[3,8,2048]{2,1,0:T(8,128)(2,1)S(1)} %collective-permute-done.1.rim.rim_q.rim_k.rim_v, ...), custom_call_target="tpu_custom_call" | custom-call | flops 2000000000 | bytes 6291456 | tf_op jit(solution)/shard_map/pallas_call | solution.py:419
  15.2 8.1 %all-to-all-start = ((bf16[32,136,128]{2,1,0:T(8,128)(2,1)}), bf16[32,136,128]{2,1,0:T(8,128)(2,1)S(1)}, u32[]{:S(2)}, u32[]{:S(2)}) async-start(bf16[32,136,128]{2,1,0:T(8,128)(2,1)} %shard_map.41), calls=%async_computation | async-start | bytes 2228224 | tf_op jit(solution)/shard_map/all_to_all | solution.py:428
  23.3 9.8 %shard_map.42 = (bf16[16,256,256]{2,1,0:T(8,128)(2,1)}, f32[16,256,256]{2,1,0:T(8,128)}) custom-call(s32[1]{0:T(128)} %bitcast.core_ref, bf16[3,128,4096]{2,1,0:T(8,128)(2,1)} %own_v.1, bf16[3,128,4096]{2,1,0:T(8,128)(2,1)} %own_v.1, bf16[3,128,4096]{2,1,0:T(8,128)(2,1)} %own_v.1, bf16[3,128,2048]{2,1,0:T(8,128)(2,1)} %get-tuple-element.28.other_q.other_k.other_v, ...), custom_call_target="tpu_custom_call" | custom-call | flops 8000000000 | bytes 20971520 | tf_op jit(solution)/shard_map/pallas_call | solution.py:431
  33.1 5.9 %all-to-all-done.sums = bf16[32,136,128]{2,1,0:T(8,128)(2,1)S(1)} async-done(((bf16[32,136,128]{2,1,0:T(8,128)(2,1)}), bf16[32,136,128]{2,1,0:T(8,128)(2,1)S(1)}, u32[]{:S(2)}, u32[]{:S(2)}) %all-to-all-start) | async-done | bytes 1114144 | tf_op jit(solution)/shard_map/all_to_all | solution.py:428
  39.0 0.2 shard_map.43
  39.1 5.8 %collective-permute-start.4 = (bf16[136,128]{1,0:T(8,128)(2,1)S(1)}, bf16[136,128]{1,0:T(8,128)(2,1)S(1)}, u32[]{:S(2)}, u32[]{:S(2)}) collective-permute-start(bf16[136,128]{1,0:T(8,128)(2,1)S(1)} %shard_map.43), channel_id=1, source_target_pairs={{0,64},{32,96},{64,160},{96,128},{160,224},{128,192},{1,65},{33,97... | collective-permute-start | bytes 104456 | tf_op jit(solution)/shard_map/ppermute | solution.py:456
  45.0 5.1 %collective-permute-start.3 = (bf16[136,128]{1,0:T(8,128)(2,1)S(1)}, bf16[136,128]{1,0:T(8,128)(2,1)S(1)}, u32[]{:S(2)}, u32[]{:S(2)}) collective-permute-start(bf16[136,128]{1,0:T(8,128)(2,1)S(1)} %shard_map.43), channel_id=1, source_target_pairs={{0,160},{32,128},{64,224},{96,192},{1,161},{33,129},{65,225},{97,1... | collective-permute-start | bytes 104456 | tf_op jit(solution)/shard_map/ppermute | solution.py:456
  50.1 1.3 %collective-permute-start.2 = (bf16[136,128]{1,0:T(8,128)(2,1)S(1)}, bf16[136,128]{1,0:T(8,128)(2,1)S(1)}, u32[]{:S(2)}, u32[]{:S(2)}) collective-permute-start(bf16[136,128]{1,0:T(8,128)(2,1)S(1)} %shard_map.43), channel_id=1, source_target_pairs={{0,224},{32,192},{1,225},{33,193},{2,226},{34,194},{3,227},{35,195... | collective-permute-start | bytes 104456 | tf_op jit(solution)/shard_map/ppermute | solution.py:456
  51.4 2.8 %shard_map.45 = (bf16[16,256,256]{2,1,0:T(8,128)(2,1)S(1)}, f32[16,256,256]{2,1,0:T(8,128)S(1)}) custom-call(bf16[16,256,256]{2,1,0:T(8,128)(2,1)} %get-tuple-element.32.query_map, f32[16,256,256]{2,1,0:T(8,128)} %get-tuple-element.33.block), custom_call_target="tpu_custom_call" | custom-call | bytes 12582912 | tf_op jit(solution)/shard_map/pallas_call | solution.py:471
  54.2 0.0 collective-permute-done.4.before_3
  54.2 0.0 collective-permute-done.3.before_2
  54.2 0.0 collective-permute-done.2.before_1
  54.3 0.2 shard_map.44
  54.5 20.6 %all_to_all.10.state = bf16[32,136,128]{2,1,0:T(8,128)(2,1)S(1)} all-to-all(bf16[32,136,128]{2,1,0:T(8,128)(2,1)S(1)} %shard_map.44), channel_id=1, replica_groups=mesh['zh'=4,'zl'=2,'x'=4,'y'=4,'c'=2] {'zl','x','y'}, dimensions={0} | all-to-all | bytes 2228224 | tf_op jit(solution)/shard_map/all_to_all | solution.py:477
  75.0 0.9 %shard_map.46 = bf16[128,2048]{1,0:T(8,128)(2,1)S(1)} custom-call(s32[1]{0:T(128)} %bitcast.core_ref, s32[1]{0:T(128)} %bitcast.1.flip_ref, f32[16,256,256]{2,1,0:T(8,128)S(1)} %get-tuple-element.36.block, bf16[16,256,256]{2,1,0:T(8,128)(2,1)S(1)} %get-tuple-element.37.query_map, bf16[32,136,128]{2,1,0:T(8,128)(2,1)S(1)} %all_to_all.10.state), custom_call_target="tpu_custom_call" | custom-call | flops 2000000000 | bytes 4194304 | tf_op jit(solution)/shard_map/pallas_call | solution.py:479
  75.9 3.5 %collective-permute-start.5 = (bf16[128,2048]{1,0:T(8,128)(2,1)S(1)}, bf16[128,2048]{1,0:T(8,128)(2,1)S(1)}, u32[]{:S(2)}, u32[]{:S(2)}) collective-permute-start(bf16[128,2048]{1,0:T(8,128)(2,1)S(1)} %shard_map.46), channel_id=1, source_target_pairs={{0,1},{1,0},{2,3},{3,2},{4,5},{5,4},{6,7},{7,6},{8,9},{9,8},{10,11... | collective-permute-start | bytes 1572872 | tf_op jit(solution)/shard_map/ppermute | solution.py:375
  79.4 1.6 %shard_map.47.partial = bf16[128,4096]{1,0:T(8,128)(2,1)} custom-call(s32[1]{0:T(128)} %bitcast.core_ref, s32[1]{0:T(128)} %bitcast.1.flip_ref, f32[16,256,256]{2,1,0:T(8,128)S(1)} %get-tuple-element.36.block, bf16[16,256,256]{2,1,0:T(8,128)(2,1)S(1)} %get-tuple-element.37.query_map, bf16[32,136,128]{2,1,0:T(8,128)(2,1)S(1)} %all_to_all.10.state), custom_call_target="tpu_custom_call" | custom-call | flops 2000000000 | bytes 4194304 | tf_op jit(solution)/shard_map/pallas_call | solution.py:484
  81.0 0.0 collective-permute-done.5.arrived
  81.0 0.8 %shard_map.48 = bf16[128,4096]{1,0:T(8,128)(2,1)} custom-call(s32[1]{0:T(128)} %bitcast.core_ref, bf16[128,2048]{1,0:T(8,128)(2,1)S(1)} %collective-permute-done.5.arrived, bf16[128,4096]{1,0:T(8,128)(2,1)} %shard_map.47.partial), custom_call_target="tpu_custom_call", output_to_operand_aliasing={{}: (2, {})} | custom-call | bytes 1048576 | tf_op jit(solution)/shard_map/pallas_call | solution.py:489
  (1 shorter events, 0.0 us)
Async XLA Ops:
  1.4 6.4 %collective-permute-start = (bf16[3,128,2048]{2,1,0:T(8,128)(2,1)S(1)}, bf16[3,128,2048]{2,1,0:T(8,128)(2,1)S(1)}, u32[]{:S(2)}, u32[]{:S(2)}) collective-permute-start(bf16[3,128,2048]{2,1,0:T(8,128)(2,1)S(1)} %get-tuple-element.23), channel_id=1, source_target_pairs={{0,1},{1,0},{2,3},{3,2},{4,5},{5,4},{6,7},{7,6},{8,9},{9,8},{10,11... | collective-permute-start | bytes 4718600 | tf_op jit(solution)/shard_map/ppermute | solution.py:375
  7.8 5.7 %collective-permute-start.1 = (bf16[3,8,2048]{2,1,0:T(8,128)(2,1)S(1)}, bf16[3,8,2048]{2,1,0:T(8,128)(2,1)S(1)}, u32[]{:S(2)}, u32[]{:S(2)}) collective-permute-start(bf16[3,8,2048]{2,1,0:T(8,128)(2,1)S(1)} %shard_map.39), channel_id=1, source_target_pairs={{0,2},{1,3},{2,4},{3,5},{4,6},{5,7},{6,8},{7,9},{8,10},{9,11},{10,... | collective-permute-start | bytes 294920 | tf_op jit(solution)/shard_map/ppermute | solution.py:398
  15.2 23.8 %all-to-all-start = ((bf16[32,136,128]{2,1,0:T(8,128)(2,1)}), bf16[32,136,128]{2,1,0:T(8,128)(2,1)S(1)}, u32[]{:S(2)}, u32[]{:S(2)}) async-start(bf16[32,136,128]{2,1,0:T(8,128)(2,1)} %shard_map.41), calls=%async_computation | async-start | bytes 2228224 | tf_op jit(solution)/shard_map/all_to_all | solution.py:428
  39.1 15.1 %collective-permute-start.4 = (bf16[136,128]{1,0:T(8,128)(2,1)S(1)}, bf16[136,128]{1,0:T(8,128)(2,1)S(1)}, u32[]{:S(2)}, u32[]{:S(2)}) collective-permute-start(bf16[136,128]{1,0:T(8,128)(2,1)S(1)} %shard_map.43), channel_id=1, source_target_pairs={{0,64},{32,96},{64,160},{96,128},{160,224},{128,192},{1,65},{33,97... | collective-permute-start | bytes 104456 | tf_op jit(solution)/shard_map/ppermute | solution.py:456
  45.0 9.2 %collective-permute-start.3 = (bf16[136,128]{1,0:T(8,128)(2,1)S(1)}, bf16[136,128]{1,0:T(8,128)(2,1)S(1)}, u32[]{:S(2)}, u32[]{:S(2)}) collective-permute-start(bf16[136,128]{1,0:T(8,128)(2,1)S(1)} %shard_map.43), channel_id=1, source_target_pairs={{0,160},{32,128},{64,224},{96,192},{1,161},{33,129},{65,225},{97,1... | collective-permute-start | bytes 104456 | tf_op jit(solution)/shard_map/ppermute | solution.py:456
  50.1 4.2 %collective-permute-start.2 = (bf16[136,128]{1,0:T(8,128)(2,1)S(1)}, bf16[136,128]{1,0:T(8,128)(2,1)S(1)}, u32[]{:S(2)}, u32[]{:S(2)}) collective-permute-start(bf16[136,128]{1,0:T(8,128)(2,1)S(1)} %shard_map.43), channel_id=1, source_target_pairs={{0,224},{32,192},{1,225},{33,193},{2,226},{34,194},{3,227},{35,195... | collective-permute-start | bytes 104456 | tf_op jit(solution)/shard_map/ppermute | solution.py:456
  75.9 5.1 %collective-permute-start.5 = (bf16[128,2048]{1,0:T(8,128)(2,1)S(1)}, bf16[128,2048]{1,0:T(8,128)(2,1)S(1)}, u32[]{:S(2)}, u32[]{:S(2)}) collective-permute-start(bf16[128,2048]{1,0:T(8,128)(2,1)S(1)} %shard_map.46), channel_id=1, source_target_pairs={{0,1},{1,0},{2,3},{3,2},{4,5},{5,4},{6,7},{7,6},{8,9},{9,8},{10,11... | collective-permute-start | bytes 1572872 | tf_op jit(solution)/shard_map/ppermute | solution.py:375

commit v6 on v5

--- a/solution.py
+++ b/solution.py
@@ -181,6 +181,10 @@
     for i in range(1, PIECES):
         total = total + sums[i].astype(f32)
     out[...] = total.astype(bf16)
+
+
+def pair_kernel(own, before, out):
+    out[...] = (own[...].astype(f32) + before[...].astype(f32)).astype(bf16)
 
 
 def prefix_kernel(before_1, before_2, before_3, sums, out):
@@ -447,33 +451,28 @@
     total = small_call(
         total_kernel, [WHOLE], WHOLE, chip(STATE_ROWS, M // 2), [], flops=10**6, moved=2**20
     )(*in_chip(gathered))
-    groups = SIZES[0]
-
-    def owner(group, plane):
-        return 2 * group + (plane + group // 2) % 2
-
-    before = [
-        lax.ppermute(
-            total,
-            ("zh", "zl"),
-            [
-                (owner(group, plane), owner(group + by, plane))
-                for group in range(groups - by)
-                for plane in range(2)
-            ],
-        )
-        for by in reversed(range(1, groups))
-    ]
-    prior = small_call(
-        prefix_kernel, [WHOLE] * 4, WHOLE, chip(PIECES, STATE_ROWS, M // 2), [],
-        flops=10**6, moved=2 * 2**20,
-    )(*in_chip(*before, gathered))
+    def send(array, *pairs):
+        def owner(group, plane):
+            return 2 * group + (plane + group // 2) % 2
+
+        ways = [(owner(a, plane), owner(b, plane)) for a, b in pairs for plane in range(2)]
+        return lax.ppermute(array, ("zh", "zl"), ways)
+
+    nearest = send(total, (0, 1), (2, 3))
     query_map, block = small_call(
         load_kernel, [ANYWHERE] * 2, [WHOLE] * 2,
         [chip(HEADS, CHUNK, M), pltpu.VMEM((HEADS, CHUNK, 2 * DH), f32)],
         [pltpu.SemaphoreType.DMA((2,))], flops=0, moved=12 * 2**20,
     )(*in_main(query_map, block))
-    prior, query_map, block = lax.optimization_barrier((prior, query_map, block))
+    nearest, query_map, block = lax.optimization_barrier((nearest, query_map, block))
+    pair = small_call(
+        pair_kernel, [WHOLE] * 2, WHOLE, chip(STATE_ROWS, M // 2), [], flops=10**5, moved=10**5
+    )(*in_chip(total, nearest))
+    before = [nearest, send(pair, (1, 2)), send(pair, (1, 3))]
+    prior = small_call(
+        prefix_kernel, [WHOLE] * 4, WHOLE, chip(PIECES, STATE_ROWS, M // 2), [],
+        flops=10**6, moved=2 * 2**20,
+    )(*in_chip(*before, gathered))
     prior = lax.all_to_all(prior, PLANE, 0, 0, tiled=True)
     operands = in_chip(block, query_map, prior)
     attended = small_call(

time: 82.2 us -> 80.7 us (0.982)
  the two profiles are of different devices: /device:TPU:1 before, /device:TPU:129 now
where the time goes in v6:
time: 80.7 us; the launch traced here: 80.4 us
  Pallas kernels  25.2 us (31%)
  blocking collectives  20.6 us (26%)
  starting transfers between devices  17.9 us (22%)
  waiting for transfers between devices  16.5 us (20%)
    all_to_all x1, blocking collectives, per_device(): prior = lax.all_to_all(prior, PLANE, 0, 0, tiled=True)  20.6 us
    pallas_call x1, Pallas kernels, per_device(): call(scores_kernel, [own_spec(w) for w in which] + [other_spec(w) for w i...  9.77 us
    ppermute x2, starting transfers between devices, swap(): return lax.ppermute(array, 'c', [(0, 1), (1, 0)])  5.85 us
    ppermute x3, waiting for transfers between devices, send(): return lax.ppermute(array, ('zh', 'zl'), ways)  5.83 us
    all_to_all x1, waiting for transfers between devices, per_device(): gathered = lax.all_to_all(state, PLANE, 0, 0, tiled=True)  5.35 us
    ppermute x3, starting transfers between devices, send(): return lax.ppermute(array, ('zh', 'zl'), ways)  4.94 us
    pallas_call x1, Pallas kernels, per_device(): small_call(maps_kernel, [SCALAR] + [WHOLE] * 4, [WHOLE, ANYWHERE], [pltpu...  4.18 us
    all_to_all x1, starting transfers between devices, per_device(): gathered = lax.all_to_all(state, PLANE, 0, 0, tiled=True)  3.93 us
  transfers between devices with their start and end apart: 7, of which 4 were waited for; matrix products, arithmetic and copies ran while one was open for 0% of the time, Pallas kernels for 25%

profile of v6, /device:TPU:129, one launch (start us, length us, event | category | flops | bytes accessed | tf_op | source)
XLA Modules:
  0.0 80.4 jit_solution(3624572571152126273)
XLA Ops:
  0.0 1.4 %shard_map.38 = (bf16[3,128,2048]{2,1,0:T(8,128)(2,1)S(1)}, bf16[3,8,2048]{2,1,0:T(8,128)(2,1)S(1)}) custom-call(s32[1]{0:T(128)} %bitcast.core_ref, bf16[3,128,4096]{2,1,0:T(8,128)(2,1)} %own_v.1), custom_call_target="tpu_custom_call" | custom-call | bytes 3145728 | tf_op jit(solution)/shard_map/pallas_call | solution.py:387
  1.4 0.8 collective-permute-start
  2.2 1.6 %shard_map.37 = (bf16[2,128,2048]{2,1,0:T(8,128)(2,1)S(1)}, f32[3,4,2048]{2,1,0:T(4,128)S(1)}, bf16[16,128,256]{2,1,0:T(8,128)(2,1)S(1)}) custom-call(s32[1]{0:T(128)} %bitcast.core_ref, bf16[3,128,4096]{2,1,0:T(8,128)(2,1)} %own_v.1, f32[3,4,4096]{2,1,0:T(4,128)} %taps_v.1, bf16[32,128,256]{2,1,0:T(8,128)(2,1)} %omega.3), custom_call_target="tpu_custom_call" | custom-call | bytes 5242880 | tf_op jit(solution)/shard_map/pallas_call | solution.py:403
  3.8 1.4 %collective-permute-done.other = bf16[3,128,2048]{2,1,0:T(8,128)(2,1)S(1)} collective-permute-done((bf16[3,128,2048]{2,1,0:T(8,128)(2,1)S(1)}, bf16[3,128,2048]{2,1,0:T(8,128)(2,1)S(1)}, u32[]{:S(2)}, u32[]{:S(2)}) %collective-permute-start) | collective-permute-done | bytes 1572896 | tf_op jit(solution)/shard_map/ppermute | solution.py:379
  5.3 3.2 %collective-permute-start.1 = (bf16[3,8,2048]{2,1,0:T(8,128)(2,1)S(1)}, bf16[3,8,2048]{2,1,0:T(8,128)(2,1)S(1)}, u32[]{:S(2)}, u32[]{:S(2)}) collective-permute-start(bf16[3,8,2048]{2,1,0:T(8,128)(2,1)S(1)} %shard_map.39), channel_id=1, source_target_pairs={{0,2},{1,3},{2,4},{3,5},{4,6},{5,7},{6,8},{7,9},{8,10},{9,11},{10,... | collective-permute-start | bytes 294920 | tf_op jit(solution)/shard_map/ppermute | solution.py:402
  8.5 4.2 %shard_map.40 = (f32[16,136,256]{2,1,0:T(8,128)S(1)}, bf16[3,128,2048]{2,1,0:T(8,128)(2,1)}) custom-call(s32[1]{0:T(128)} %bitcast.core_ref, bf16[2,128,2048]{2,1,0:T(8,128)(2,1)S(1)} %get-tuple-element.22.own, bf16[3,128,2048]{2,1,0:T(8,128)(2,1)S(1)} %collective-permute-done.other, f32[3,4,2048]{2,1,0:T(4,128)S(1)} %get-tuple-element.25.taps, ...), custom_call_target="tpu_custom_call" | custom-call | flops 3000000000 | bytes 6291456 | tf_op jit(solution)/shard_map/pallas_call | solution.py:414
  12.7 3.9 %collective-permute-done.1.rim.rim_q.rim_k.rim_v = bf16[3,8,2048]{2,1,0:T(8,128)(2,1)S(1)} collective-permute-done((bf16[3,8,2048]{2,1,0:T(8,128)(2,1)S(1)}, bf16[3,8,2048]{2,1,0:T(8,128)(2,1)S(1)}, u32[]{:S(2)}, u32[]{:S(2)}) %collective-permute-start.1) | collective-permute-done | bytes 98336 | tf_op jit(solution)/shard_map/ppermute | solution.py:402
  16.6 1.7 %shard_map.41 = bf16[32,136,128]{2,1,0:T(8,128)(2,1)} custom-call(s32[1]{0:T(128)} %bitcast.core_ref, s32[1]{0:T(128)} %bitcast.1.flip_ref, bf16[2,128,2048]{2,1,0:T(8,128)(2,1)S(1)} %get-tuple-element.22.own, bf16[3,128,2048]{2,1,0:T(8,128)(2,1)S(1)} %collective-permute-done.other, bf16[3,8,2048]{2,1,0:T(8,128)(2,1)S(1)} %collective-permute-done.1.rim.rim_q.rim_k.rim_v, ...), custom_call_target="tpu_custom_call" | custom-call | flops 2000000000 | bytes 6291456 | tf_op jit(solution)/shard_map/pallas_call | solution.py:423
  18.3 3.9 %all-to-all-start = ((bf16[32,136,128]{2,1,0:T(8,128)(2,1)}), bf16[32,136,128]{2,1,0:T(8,128)(2,1)S(1)}, u32[]{:S(2)}, u32[]{:S(2)}) async-start(bf16[32,136,128]{2,1,0:T(8,128)(2,1)} %shard_map.41), calls=%async_computation | async-start | bytes 2228224 | tf_op jit(solution)/shard_map/all_to_all | solution.py:432
  22.2 9.8 %shard_map.42 = (bf16[16,256,256]{2,1,0:T(8,128)(2,1)}, f32[16,256,256]{2,1,0:T(8,128)}) custom-call(s32[1]{0:T(128)} %bitcast.core_ref, bf16[3,128,4096]{2,1,0:T(8,128)(2,1)} %own_v.1, bf16[3,128,4096]{2,1,0:T(8,128)(2,1)} %own_v.1, bf16[3,128,4096]{2,1,0:T(8,128)(2,1)} %own_v.1, bf16[3,128,2048]{2,1,0:T(8,128)(2,1)} %get-tuple-element.28.other_q.other_k.other_v, ...), custom_call_target="tpu_custom_call" | custom-call | flops 8000000000 | bytes 20971520 | tf_op jit(solution)/shard_map/pallas_call | solution.py:435
  32.0 5.3 %all-to-all-done.sums = bf16[32,136,128]{2,1,0:T(8,128)(2,1)S(1)} async-done(((bf16[32,136,128]{2,1,0:T(8,128)(2,1)}), bf16[32,136,128]{2,1,0:T(8,128)(2,1)S(1)}, u32[]{:S(2)}, u32[]{:S(2)}) %all-to-all-start) | async-done | bytes 1114144 | tf_op jit(solution)/shard_map/all_to_all | solution.py:432
  37.3 0.2 shard_map.43.own
  37.5 3.0 %collective-permute-start.2 = (bf16[136,128]{1,0:T(8,128)(2,1)S(1)}, bf16[136,128]{1,0:T(8,128)(2,1)S(1)}, u32[]{:S(2)}, u32[]{:S(2)}) collective-permute-start(bf16[136,128]{1,0:T(8,128)(2,1)S(1)} %shard_map.43.own), channel_id=1, source_target_pairs={{0,64},{32,96},{160,224},{128,192},{1,65},{33,97},{161,225},{129,1... | collective-permute-start | bytes 104456 | tf_op jit(solution)/shard_map/ppermute | solution.py:459
  40.5 2.8 %shard_map.44 = (bf16[16,256,256]{2,1,0:T(8,128)(2,1)S(1)}, f32[16,256,256]{2,1,0:T(8,128)S(1)}) custom-call(bf16[16,256,256]{2,1,0:T(8,128)(2,1)} %get-tuple-element.32.query_map, f32[16,256,256]{2,1,0:T(8,128)} %get-tuple-element.33.block), custom_call_target="tpu_custom_call" | custom-call | bytes 12582912 | tf_op jit(solution)/shard_map/pallas_call | solution.py:462
  43.3 0.0 collective-permute-done.2.before.before_1
  43.4 0.7 collective-permute-start.4
  44.0 1.3 %collective-permute-start.3 = (bf16[136,128]{1,0:T(8,128)(2,1)S(1)}, bf16[136,128]{1,0:T(8,128)(2,1)S(1)}, u32[]{:S(2)}, u32[]{:S(2)}) collective-permute-start(bf16[136,128]{1,0:T(8,128)(2,1)S(1)} %shard_map.45), channel_id=1, source_target_pairs={{64,160},{96,128},{65,161},{97,129},{66,162},{98,130},{67,163},{99... | collective-permute-start | bytes 104456 | tf_op jit(solution)/shard_map/ppermute | solution.py:459
  45.3 0.0 collective-permute-done.4.before_3
  45.4 5.8 %collective-permute-done.3.before_2 = bf16[136,128]{1,0:T(8,128)(2,1)S(1)} collective-permute-done((bf16[136,128]{1,0:T(8,128)(2,1)S(1)}, bf16[136,128]{1,0:T(8,128)(2,1)S(1)}, u32[]{:S(2)}, u32[]{:S(2)}) %collective-permute-start.3) | collective-permute-done | bytes 34848 | tf_op jit(solution)/shard_map/ppermute | solution.py:459
  51.2 0.2 shard_map.46
  51.4 20.6 %all_to_all.10.state = bf16[32,136,128]{2,1,0:T(8,128)(2,1)S(1)} all-to-all(bf16[32,136,128]{2,1,0:T(8,128)(2,1)S(1)} %shard_map.46), channel_id=1, replica_groups=mesh['zh'=4,'zl'=2,'x'=4,'y'=4,'c'=2] {'zl','x','y'}, dimensions={0} | all-to-all | bytes 2228224 | tf_op jit(solution)/shard_map/all_to_all | solution.py:476
  72.0 0.9 %shard_map.47 = bf16[128,2048]{1,0:T(8,128)(2,1)S(1)} custom-call(s32[1]{0:T(128)} %bitcast.core_ref, s32[1]{0:T(128)} %bitcast.1.flip_ref, f32[16,256,256]{2,1,0:T(8,128)S(1)} %get-tuple-element.36.block, bf16[16,256,256]{2,1,0:T(8,128)(2,1)S(1)} %get-tuple-element.37.query_map, bf16[32,136,128]{2,1,0:T(8,128)(2,1)S(1)} %all_to_all.10.state), custom_call_target="tpu_custom_call" | custom-call | flops 2000000000 | bytes 4194304 | tf_op jit(solution)/shard_map/pallas_call | solution.py:478
  72.9 5.1 %collective-permute-start.5 = (bf16[128,2048]{1,0:T(8,128)(2,1)S(1)}, bf16[128,2048]{1,0:T(8,128)(2,1)S(1)}, u32[]{:S(2)}, u32[]{:S(2)}) collective-permute-start(bf16[128,2048]{1,0:T(8,128)(2,1)S(1)} %shard_map.47), channel_id=1, source_target_pairs={{0,1},{1,0},{2,3},{3,2},{4,5},{5,4},{6,7},{7,6},{8,9},{9,8},{10,11... | collective-permute-start | bytes 1572872 | tf_op jit(solution)/shard_map/ppermute | solution.py:379
  78.0 1.6 %shard_map.48.partial = bf16[128,4096]{1,0:T(8,128)(2,1)} custom-call(s32[1]{0:T(128)} %bitcast.core_ref, s32[1]{0:T(128)} %bitcast.1.flip_ref, f32[16,256,256]{2,1,0:T(8,128)S(1)} %get-tuple-element.36.block, bf16[16,256,256]{2,1,0:T(8,128)(2,1)S(1)} %get-tuple-element.37.query_map, bf16[32,136,128]{2,1,0:T(8,128)(2,1)S(1)} %all_to_all.10.state), custom_call_target="tpu_custom_call" | custom-call | flops 2000000000 | bytes 4194304 | tf_op jit(solution)/shard_map/pallas_call | solution.py:483
  79.5 0.0 collective-permute-done.5.arrived
  79.5 0.8 %shard_map.49 = bf16[128,4096]{1,0:T(8,128)(2,1)} custom-call(s32[1]{0:T(128)} %bitcast.core_ref, bf16[128,2048]{1,0:T(8,128)(2,1)S(1)} %collective-permute-done.5.arrived, bf16[128,4096]{1,0:T(8,128)(2,1)} %shard_map.48.partial), custom_call_target="tpu_custom_call", output_to_operand_aliasing={{}: (2, {})} | custom-call | bytes 1048576 | tf_op jit(solution)/shard_map/pallas_call | solution.py:488
  (2 shorter events, 0.0 us)
Async XLA Ops:
  1.4 3.8 %collective-permute-start = (bf16[3,128,2048]{2,1,0:T(8,128)(2,1)S(1)}, bf16[3,128,2048]{2,1,0:T(8,128)(2,1)S(1)}, u32[]{:S(2)}, u32[]{:S(2)}) collective-permute-start(bf16[3,128,2048]{2,1,0:T(8,128)(2,1)S(1)} %get-tuple-element.23), channel_id=1, source_target_pairs={{0,1},{1,0},{2,3},{3,2},{4,5},{5,4},{6,7},{7,6},{8,9},{9,8},{10,11... | collective-permute-start | bytes 4718600 | tf_op jit(solution)/shard_map/ppermute | solution.py:379
  5.3 11.3 %collective-permute-start.1 = (bf16[3,8,2048]{2,1,0:T(8,128)(2,1)S(1)}, bf16[3,8,2048]{2,1,0:T(8,128)(2,1)S(1)}, u32[]{:S(2)}, u32[]{:S(2)}) collective-permute-start(bf16[3,8,2048]{2,1,0:T(8,128)(2,1)S(1)} %shard_map.39), channel_id=1, source_target_pairs={{0,2},{1,3},{2,4},{3,5},{4,6},{5,7},{6,8},{7,9},{8,10},{9,11},{10,... | collective-permute-start | bytes 294920 | tf_op jit(solution)/shard_map/ppermute | solution.py:402
  18.3 19.1 %all-to-all-start = ((bf16[32,136,128]{2,1,0:T(8,128)(2,1)}), bf16[32,136,128]{2,1,0:T(8,128)(2,1)S(1)}, u32[]{:S(2)}, u32[]{:S(2)}) async-start(bf16[32,136,128]{2,1,0:T(8,128)(2,1)} %shard_map.41), calls=%async_computation | async-start | bytes 2228224 | tf_op jit(solution)/shard_map/all_to_all | solution.py:432
  37.5 5.8 %collective-permute-start.2 = (bf16[136,128]{1,0:T(8,128)(2,1)S(1)}, bf16[136,128]{1,0:T(8,128)(2,1)S(1)}, u32[]{:S(2)}, u32[]{:S(2)}) collective-permute-start(bf16[136,128]{1,0:T(8,128)(2,1)S(1)} %shard_map.43.own), channel_id=1, source_target_pairs={{0,64},{32,96},{160,224},{128,192},{1,65},{33,97},{161,225},{129,1... | collective-permute-start | bytes 104456 | tf_op jit(solution)/shard_map/ppermute | solution.py:459
  43.4 2.0 %collective-permute-start.4 = (bf16[136,128]{1,0:T(8,128)(2,1)S(1)}, bf16[136,128]{1,0:T(8,128)(2,1)S(1)}, u32[]{:S(2)}, u32[]{:S(2)}) collective-permute-start(bf16[136,128]{1,0:T(8,128)(2,1)S(1)} %shard_map.45), channel_id=1, source_target_pairs={{64,224},{96,192},{65,225},{97,193},{66,226},{98,194},{67,227},{99... | collective-permute-start | bytes 104456 | tf_op jit(solution)/shard_map/ppermute | solution.py:459
  44.0 7.1 %collective-permute-start.3 = (bf16[136,128]{1,0:T(8,128)(2,1)S(1)}, bf16[136,128]{1,0:T(8,128)(2,1)S(1)}, u32[]{:S(2)}, u32[]{:S(2)}) collective-permute-start(bf16[136,128]{1,0:T(8,128)(2,1)S(1)} %shard_map.45), channel_id=1, source_target_pairs={{64,160},{96,128},{65,161},{97,129},{66,162},{98,130},{67,163},{99... | collective-permute-start | bytes 104456 | tf_op jit(solution)/shard_map/ppermute | solution.py:459
  72.9 6.7 %collective-permute-start.5 = (bf16[128,2048]{1,0:T(8,128)(2,1)S(1)}, bf16[128,2048]{1,0:T(8,128)(2,1)S(1)}, u32[]{:S(2)}, u32[]{:S(2)}) collective-permute-start(bf16[128,2048]{1,0:T(8,128)(2,1)S(1)} %shard_map.47), channel_id=1, source_target_pairs={{0,1},{1,0},{2,3},{3,2},{4,5},{5,4},{6,7},{7,6},{8,9},{9,8},{10,11... | collective-permute-start | bytes 1572872 | tf_op jit(solution)/shard_map/ppermute | solution.py:379

commit v7 on v6

--- a/solution.py
+++ b/solution.py
@@ -150,13 +150,19 @@
 
 def scores_kernel(
     core_ref, own_q, own_k, own_v, other_q, other_k, other_v, rim_q, rim_k, rim_v,
-    taps_q, taps_k, taps_v, omega, query_map, block, rows_q, rows_k, rows_v,
+    taps_q, taps_k, taps_v, omega, query_map, block, sums, rows_q, rows_k, rows_v,
 ):
     core = core_ref[0]
     ones = jnp.ones((M, M), bf16)
     causal = lax.broadcasted_iota(jnp.int32, (CHUNK, CHUNK), 0) >= lax.broadcasted_iota(
         jnp.int32, (CHUNK, CHUNK), 1
     )
+    lane = lax.broadcasted_iota(jnp.int32, (CHUNK, DH), 1)
+
+    @pl.when(pl.program_id(0) == 0)
+    def _():
+        sums[...] = jnp.zeros_like(sums)
+
     for head in range(GROUP):
         cols = slice(head * DH, (head + 1) * DH)
         convolved = []
@@ -173,7 +179,10 @@
         query_map[head] = queries
         products = dot_nt(queries, key_map_of(k, omega[head], ones))
         scores = jnp.where(causal, products, 0.0).astype(bf16)
-        block[head] = dot(scores, jnp.concatenate([v, ones[:, :DH]], axis=1))
+        both = dot(scores, jnp.concatenate([v, ones[:, :DH]], axis=1))
+        block[head] = both[:, :DH]
+        mine = lane == pl.program_id(0) * GROUP + head
+        sums[...] = jnp.where(mine, both[:, DH:], sums[...])
 
 
 def total_kernel(sums, out):
@@ -194,21 +203,23 @@
         running = running + sums[i].astype(f32)
 
 
-def attend_rows(rows, flip, block, query_map, state, put, group):
+def attend_rows(rows, flip, block, sums, query_map, state, put, group):
     for head in range(group * GROUP, (group + 1) * GROUP):
         piece = piece_of(head, flip)
         prior = jnp.concatenate([state[piece], state[piece + 1]], axis=1)
         total = jnp.broadcast_to(prior[DH : DH + 1], (DH, M))
         prior = jnp.concatenate([prior[:DH], total], axis=0)
-        both = block[head, rows, :] + dot_nt(query_map[head, rows, :], prior)
-        put(head, (both[:, :DH] / both[:, DH:]).astype(bf16))
+        both = dot_nt(query_map[head, rows, :], prior)
+        numerator = block[head, rows, :] + both[:, :DH]
+        denominator = sums[rows, head : head + 1] + both[:, DH:]
+        put(head, (numerator / denominator).astype(bf16))
 
 
 def columns(start, size):
     return pl.ds(pl.multiple_of(start, DH), size)
 
 
-def attend_other_kernel(core_ref, flip_ref, block, query_map, state, out):
+def attend_other_kernel(core_ref, flip_ref, block, sums, query_map, state, out):
     start = pl.multiple_of((1 - core_ref[0]) * ROWS, ROWS)
 
     def put(head, block):
@@ -216,12 +227,12 @@
 
     for group in range(STEPS):
         attend_rows(
-            pl.ds(start, ROWS), flip_ref[0], block, query_map, state, put, group
+            pl.ds(start, ROWS), flip_ref[0], block, sums, query_map, state, put, group
         )
 
 
 def attend_own_kernel(
-    core_ref, flip_ref, block, query_map, state, out, block_rows, sems
+    core_ref, flip_ref, block, sums, query_map, state, out, block_rows, sems
 ):
     core = core_ref[0]
     rows = pl.ds(pl.multiple_of(core * ROWS, ROWS), ROWS)
@@ -237,7 +248,7 @@
         )
 
     for group in range(STEPS):
-        attend_rows(rows, flip_ref[0], block, query_map, state, put, group)
+        attend_rows(rows, flip_ref[0], block, sums, query_map, state, put, group)
         copy(group).start()
     for group in range(STEPS):
         copy(group).wait()
@@ -269,10 +280,12 @@
 def split_kernel(core_ref, projected, sent, rim_own, sems):
     core = core_ref[0]
     last = pl.ds(ROWS - RIM, RIM)
-    pairs = [
-        (projected.at[:, :, columns((1 - core) * COLS, COLS)], sent),
-        (projected.at[:, last, columns(core * COLS, COLS)], rim_own),
-    ]
+    others = columns((1 - core) * COLS, COLS)
+    pairs = [(projected.at[:, last, columns(core * COLS, COLS)], rim_own)]
+    for which in range(3):
+        for start in range(0, ROWS, ROWS // 2):
+            part = (pl.ds(which, 1), pl.ds(start, ROWS // 2))
+            pairs.append((projected.at[(*part, others)], sent.at[part]))
     run_copies(pairs, sems)
 
 
@@ -289,10 +302,6 @@
         (omega.at[pl.ds(core_ref[0] * HEADS, HEADS)], own_omega),
     ]
     run_copies(pairs, sems)
-
-
-def load_kernel(query_map, block, query_map_out, block_out, sems):
-    run_copies([(query_map, query_map_out), (block, block_out)], sems)
 
 
 def spec(shape, index):
@@ -389,7 +398,7 @@
         [SCALAR, ANYWHERE],
         [WHOLE] * 2,
         [chip(3, ROWS, COLS), chip(3, RIM, COLS)],
-        [pltpu.SemaphoreType.DMA((2,))],
+        [pltpu.SemaphoreType.DMA((7,))],
         flops=0,
         moved=3 * 2**20,
     )(cores, projected)
@@ -432,22 +441,24 @@
     gathered = lax.all_to_all(state, PLANE, 0, 0, tiled=True)
     (other_main,) = in_main(other_main)
     which = range(3)
-    query_map, block = call(
+    query_map, block, sums = call(
         scores_kernel,
         [own_spec(w) for w in which]
         + [other_spec(w) for w in which]
         + [rim_spec(w) for w in which]
         + [taps_spec(w) for w in which]
         + [OMEGA_SPEC],
-        [head_spec(CHUNK, M), head_spec(CHUNK, 2 * DH)],
-        [main(HEADS, CHUNK, M), pltpu.HBM((HEADS, CHUNK, 2 * DH), f32)],
+        [head_spec(CHUNK, M), head_spec(CHUNK, DH), spec((CHUNK, DH), lambda i, core: (0, 0))],
+        [main(HEADS, CHUNK, M), pltpu.HBM((HEADS, CHUNK, DH), f32), pltpu.HBM((CHUNK, DH), f32)],
         raw * 3,
         flops=8 * 10**9,
         moved=20 * 2**20,
     )(
         cores, *[projected] * 3, *[other_main] * 3, *[rim] * 3, *[conv_filter] * 3, frequencies
     )
-    gathered, query_map, block = lax.optimization_barrier((gathered, query_map, block))
+    gathered, query_map, block, sums = lax.optimization_barrier(
+        (gathered, query_map, block, sums)
+    )
     total = small_call(
         total_kernel, [WHOLE], WHOLE, chip(STATE_ROWS, M // 2), [], flops=10**6, moved=2**20
     )(*in_chip(gathered))
@@ -458,30 +469,25 @@
         ways = [(owner(a, plane), owner(b, plane)) for a, b in pairs for plane in range(2)]
         return lax.ppermute(array, ("zh", "zl"), ways)
 
-    nearest = send(total, (0, 1), (2, 3))
-    query_map, block = small_call(
-        load_kernel, [ANYWHERE] * 2, [WHOLE] * 2,
-        [chip(HEADS, CHUNK, M), pltpu.VMEM((HEADS, CHUNK, 2 * DH), f32)],
-        [pltpu.SemaphoreType.DMA((2,))], flops=0, moved=12 * 2**20,
-    )(*in_main(query_map, block))
-    nearest, query_map, block = lax.optimization_barrier((nearest, query_map, block))
+    nearest = send(total, (0, 1), (1, 2))
+    skipping = send(total, (0, 2), (1, 3))
     pair = small_call(
         pair_kernel, [WHOLE] * 2, WHOLE, chip(STATE_ROWS, M // 2), [], flops=10**5, moved=10**5
-    )(*in_chip(total, nearest))
-    before = [nearest, send(pair, (1, 2)), send(pair, (1, 3))]
+    )(*in_chip(total, skipping))
+    before = [nearest, skipping, send(pair, (2, 3))]
     prior = small_call(
         prefix_kernel, [WHOLE] * 4, WHOLE, chip(PIECES, STATE_ROWS, M // 2), [],
         flops=10**6, moved=2 * 2**20,
     )(*in_chip(*before, gathered))
     prior = lax.all_to_all(prior, PLANE, 0, 0, tiled=True)
-    operands = in_chip(block, query_map, prior)
+    operands = in_chip(block, sums, query_map, prior)
     attended = small_call(
-        attend_other_kernel, [SCALAR] * 2 + [WHOLE] * 3, WHOLE, chip(ROWS, COLS), [],
+        attend_other_kernel, [SCALAR] * 2 + [WHOLE] * 4, WHOLE, chip(ROWS, COLS), [],
         flops=2 * 10**9, moved=4 * 2**20,
     )(cores, flips, *operands)
     arrived = swap(attended)
     partial = small_call(
-        attend_own_kernel, [SCALAR] * 2 + [WHOLE] * 3, ANYWHERE, main(ROWS, D),
+        attend_own_kernel, [SCALAR] * 2 + [WHOLE] * 4, ANYWHERE, main(ROWS, D),
         [pltpu.VMEM((ROWS, COLS), bf16), pltpu.SemaphoreType.DMA((STEPS,))],
         flops=2 * 10**9, moved=4 * 2**20,
     )(cores, flips, *operands)

time: 80.7 us -> 79.7 us (0.988)
  the two profiles are of different devices: /device:TPU:129 before, /device:TPU:1 now
where the time goes in v7:
time: 79.7 us; the launch traced here: 79 us
  starting transfers between devices  28.9 us (36%)
  Pallas kernels  22.2 us (28%)
  blocking collectives  19.9 us (25%)
  waiting for transfers between devices  7.75 us (10%)
    all_to_all x1, blocking collectives, per_device(): prior = lax.all_to_all(prior, PLANE, 0, 0, tiled=True)  19.9 us
    ppermute x3, starting transfers between devices, send(): return lax.ppermute(array, ('zh', 'zl'), ways)  11.6 us
    pallas_call x1, Pallas kernels, per_device(): call(scores_kernel, [own_spec(w) for w in which] + [other_spec(w) for w i...  9.66 us
    all_to_all x1, starting transfers between devices, per_device(): gathered = lax.all_to_all(state, PLANE, 0, 0, tiled=True)  8.09 us
    ppermute x2, starting transfers between devices, swap(): return lax.ppermute(array, 'c', [(0, 1), (1, 0)])  7.76 us
    all_to_all x1, waiting for transfers between devices, per_device(): gathered = lax.all_to_all(state, PLANE, 0, 0, tiled=True)  5.99 us
    pallas_call x1, Pallas kernels, per_device(): small_call(maps_kernel, [SCALAR] + [WHOLE] * 4, [WHOLE, ANYWHERE], [pltpu...  4.19 us
    pallas_call x1, Pallas kernels, per_device(): small_call(state_kernel, [SCALAR] * 2 + [WHOLE] * 6, WHOLE, chip(PIECES,...  1.62 us
  transfers between devices with their start and end apart: 7, of which 3 were waited for; matrix products, arithmetic and copies ran while one was open for 0% of the time, Pallas kernels for 22%

profile of v7, /device:TPU:1, one launch (start us, length us, event | category | flops | bytes accessed | tf_op | source)
XLA Modules:
  0.0 79.0 jit_solution(9894955278935974914)
XLA Ops:
  0.0 1.5 %shard_map.38 = (bf16[3,128,2048]{2,1,0:T(8,128)(2,1)S(1)}, bf16[3,8,2048]{2,1,0:T(8,128)(2,1)S(1)}) custom-call(s32[1]{0:T(128)} %bitcast.core_ref, bf16[3,128,4096]{2,1,0:T(8,128)(2,1)} %own_v.1), custom_call_target="tpu_custom_call" | custom-call | bytes 3145728 | tf_op jit(solution)/shard_map/pallas_call | solution.py:396
  1.5 3.3 %collective-permute-start = (bf16[3,128,2048]{2,1,0:T(8,128)(2,1)S(1)}, bf16[3,128,2048]{2,1,0:T(8,128)(2,1)S(1)}, u32[]{:S(2)}, u32[]{:S(2)}) collective-permute-start(bf16[3,128,2048]{2,1,0:T(8,128)(2,1)S(1)} %get-tuple-element.20), channel_id=1, source_target_pairs={{0,1},{1,0},{2,3},{3,2},{4,5},{5,4},{6,7},{7,6},{8,9},{9,8},{10,11... | collective-permute-start | bytes 4718600 | tf_op jit(solution)/shard_map/ppermute | solution.py:388
  4.8 1.6 %shard_map.37 = (bf16[2,128,2048]{2,1,0:T(8,128)(2,1)S(1)}, f32[3,4,2048]{2,1,0:T(4,128)S(1)}, bf16[16,128,256]{2,1,0:T(8,128)(2,1)S(1)}) custom-call(s32[1]{0:T(128)} %bitcast.core_ref, bf16[3,128,4096]{2,1,0:T(8,128)(2,1)} %own_v.1, f32[3,4,4096]{2,1,0:T(4,128)} %taps_v.1, bf16[32,128,256]{2,1,0:T(8,128)(2,1)} %omega.3), custom_call_target="tpu_custom_call" | custom-call | bytes 5242880 | tf_op jit(solution)/shard_map/pallas_call | solution.py:412
  6.4 1.4 %collective-permute-done.other = bf16[3,128,2048]{2,1,0:T(8,128)(2,1)S(1)} collective-permute-done((bf16[3,128,2048]{2,1,0:T(8,128)(2,1)S(1)}, bf16[3,128,2048]{2,1,0:T(8,128)(2,1)S(1)}, u32[]{:S(2)}, u32[]{:S(2)}) %collective-permute-start) | collective-permute-done | bytes 1572896 | tf_op jit(solution)/shard_map/ppermute | solution.py:388
  7.9 1.5 %collective-permute-start.1 = (bf16[3,8,2048]{2,1,0:T(8,128)(2,1)S(1)}, bf16[3,8,2048]{2,1,0:T(8,128)(2,1)S(1)}, u32[]{:S(2)}, u32[]{:S(2)}) collective-permute-start(bf16[3,8,2048]{2,1,0:T(8,128)(2,1)S(1)} %shard_map.39), channel_id=1, source_target_pairs={{0,2},{1,3},{2,4},{3,5},{4,6},{5,7},{6,8},{7,9},{8,10},{9,11},{10,... | collective-permute-start | bytes 294920 | tf_op jit(solution)/shard_map/ppermute | solution.py:411
  9.3 4.2 %shard_map.40 = (f32[16,136,256]{2,1,0:T(8,128)S(1)}, bf16[3,128,2048]{2,1,0:T(8,128)(2,1)}) custom-call(s32[1]{0:T(128)} %bitcast.core_ref, bf16[2,128,2048]{2,1,0:T(8,128)(2,1)S(1)} %get-tuple-element.19.own, bf16[3,128,2048]{2,1,0:T(8,128)(2,1)S(1)} %collective-permute-done.other, f32[3,4,2048]{2,1,0:T(4,128)S(1)} %get-tuple-element.22.taps, ...), custom_call_target="tpu_custom_call" | custom-call | flops 3000000000 | bytes 6291456 | tf_op jit(solution)/shard_map/pallas_call | solution.py:423
  13.5 0.0 collective-permute-done.1.rim.rim_q.rim_k.rim_v
  13.5 1.6 %shard_map.41 = bf16[32,136,128]{2,1,0:T(8,128)(2,1)} custom-call(s32[1]{0:T(128)} %bitcast.core_ref, s32[1]{0:T(128)} %bitcast.1.flip_ref, bf16[2,128,2048]{2,1,0:T(8,128)(2,1)S(1)} %get-tuple-element.19.own, bf16[3,128,2048]{2,1,0:T(8,128)(2,1)S(1)} %collective-permute-done.other, bf16[3,8,2048]{2,1,0:T(8,128)(2,1)S(1)} %collective-permute-done.1.rim.rim_q.rim_k.rim_v, ...), custom_call_target="tpu_custom_call" | custom-call | flops 2000000000 | bytes 6291456 | tf_op jit(solution)/shard_map/pallas_call | solution.py:432
  15.2 8.1 %all-to-all-start = ((bf16[32,136,128]{2,1,0:T(8,128)(2,1)}), bf16[32,136,128]{2,1,0:T(8,128)(2,1)S(1)}, u32[]{:S(2)}, u32[]{:S(2)}) async-start(bf16[32,136,128]{2,1,0:T(8,128)(2,1)} %shard_map.41), calls=%async_computation | async-start | bytes 2228224 | tf_op jit(solution)/shard_map/all_to_all | solution.py:441
  23.3 9.7 %shard_map.42 = (bf16[16,256,256]{2,1,0:T(8,128)(2,1)}, f32[16,256,128]{2,1,0:T(8,128)}, f32[256,128]{1,0:T(8,128)}) custom-call(s32[1]{0:T(128)} %bitcast.core_ref, bf16[3,128,4096]{2,1,0:T(8,128)(2,1)} %own_v.1, bf16[3,128,4096]{2,1,0:T(8,128)(2,1)} %own_v.1, bf16[3,128,4096]{2,1,0:T(8,128)(2,1)} %own_v.1, ...), custom_call_target="tpu_custom_call" | custom-call | flops 8000000000 | bytes 20971520 | tf_op jit(solution)/shard_map/pallas_call | solution.py:444
  32.9 6.0 %all-to-all-done.sums = bf16[32,136,128]{2,1,0:T(8,128)(2,1)S(1)} async-done(((bf16[32,136,128]{2,1,0:T(8,128)(2,1)}), bf16[32,136,128]{2,1,0:T(8,128)(2,1)S(1)}, u32[]{:S(2)}, u32[]{:S(2)}) %all-to-all-start) | async-done | bytes 1114144 | tf_op jit(solution)/shard_map/all_to_all | solution.py:441
  38.9 0.2 shard_map.43.own
  39.1 8.2 %collective-permute-start.3 = (bf16[136,128]{1,0:T(8,128)(2,1)S(1)}, bf16[136,128]{1,0:T(8,128)(2,1)S(1)}, u32[]{:S(2)}, u32[]{:S(2)}) collective-permute-start(bf16[136,128]{1,0:T(8,128)(2,1)S(1)} %shard_map.43.own), channel_id=1, source_target_pairs={{0,160},{32,128},{64,224},{96,192},{1,161},{33,129},{65,225},{97,1... | collective-permute-start | bytes 104456 | tf_op jit(solution)/shard_map/ppermute | solution.py:470
  47.3 2.7 %collective-permute-start.2 = (bf16[136,128]{1,0:T(8,128)(2,1)S(1)}, bf16[136,128]{1,0:T(8,128)(2,1)S(1)}, u32[]{:S(2)}, u32[]{:S(2)}) collective-permute-start(bf16[136,128]{1,0:T(8,128)(2,1)S(1)} %shard_map.43.own), channel_id=1, source_target_pairs={{0,64},{32,96},{64,160},{96,128},{1,65},{33,97},{65,161},{97,129},... | collective-permute-start | bytes 104456 | tf_op jit(solution)/shard_map/ppermute | solution.py:470
  50.0 0.0 collective-permute-done.3.before.before_2
  50.1 0.7 collective-permute-start.4
  50.7 0.3 collective-permute-done.2.before_1
  51.1 0.0 collective-permute-done.4.before_3
  51.1 0.0 copy-start.1
  51.1 0.2 shard_map.45
  51.3 0.0 copy-start
  51.3 0.0 copy-start.2
  51.3 19.9 %all_to_all.10.state = bf16[32,136,128]{2,1,0:T(8,128)(2,1)S(1)} all-to-all(bf16[32,136,128]{2,1,0:T(8,128)(2,1)S(1)} %shard_map.45), channel_id=1, replica_groups=mesh['zh'=4,'zl'=2,'x'=4,'y'=4,'c'=2] {'zl','x','y'}, dimensions={0} | all-to-all | bytes 2228224 | tf_op jit(solution)/shard_map/all_to_all | solution.py:482
  71.2 0.0 copy-done.1
  71.2 0.0 copy-done
  71.2 0.0 copy-done.2
  71.2 0.9 %shard_map.46 = bf16[128,2048]{1,0:T(8,128)(2,1)S(1)} custom-call(s32[1]{0:T(128)} %bitcast.core_ref, s32[1]{0:T(128)} %bitcast.1.flip_ref, f32[16,256,128]{2,1,0:T(8,128)S(1)} %copy-done.1, f32[256,128]{1,0:T(8,128)S(1)} %copy-done.2, bf16[16,256,256]{2,1,0:T(8,128)(2,1)S(1)} %copy-done, bf16[32,136,128]{2,1,0:T(8,128)(2,1)S(1)} %all_to_all.10.state), custom_call_target="tpu_custom_call" | custom-call | flops 2000000000 | bytes 4194304 | tf_op jit(solution)/shard_map/pallas_call | solution.py:484
  72.1 4.4 %collective-permute-start.5 = (bf16[128,2048]{1,0:T(8,128)(2,1)S(1)}, bf16[128,2048]{1,0:T(8,128)(2,1)S(1)}, u32[]{:S(2)}, u32[]{:S(2)}) collective-permute-start(bf16[128,2048]{1,0:T(8,128)(2,1)S(1)} %shard_map.46), channel_id=1, source_target_pairs={{0,1},{1,0},{2,3},{3,2},{4,5},{5,4},{6,7},{7,6},{8,9},{9,8},{10,11... | collective-permute-start | bytes 1572872 | tf_op jit(solution)/shard_map/ppermute | solution.py:388
  76.6 1.6 %shard_map.47.partial = bf16[128,4096]{1,0:T(8,128)(2,1)} custom-call(s32[1]{0:T(128)} %bitcast.core_ref, s32[1]{0:T(128)} %bitcast.1.flip_ref, f32[16,256,128]{2,1,0:T(8,128)S(1)} %copy-done.1, f32[256,128]{1,0:T(8,128)S(1)} %copy-done.2, bf16[16,256,256]{2,1,0:T(8,128)(2,1)S(1)} %copy-done, bf16[32,136,128]{2,1,0:T(8,128)(2,1)S(1)} %all_to_all.10.state), custom_call_target="tpu_custom_call" | custom-call | flops 2000000000 | bytes 4194304 | tf_op jit(solution)/shard_map/pallas_call | solution.py:489
  78.1 0.0 collective-permute-done.5.arrived
  78.2 0.8 %shard_map.48 = bf16[128,4096]{1,0:T(8,128)(2,1)} custom-call(s32[1]{0:T(128)} %bitcast.core_ref, bf16[128,2048]{1,0:T(8,128)(2,1)S(1)} %collective-permute-done.5.arrived, bf16[128,4096]{1,0:T(8,128)(2,1)} %shard_map.47.partial), custom_call_target="tpu_custom_call", output_to_operand_aliasing={{}: (2, {})} | custom-call | bytes 1048576 | tf_op jit(solution)/shard_map/pallas_call | solution.py:494
  (2 shorter events, 0.0 us)
Async XLA Ops:
  1.5 6.4 %collective-permute-start = (bf16[3,128,2048]{2,1,0:T(8,128)(2,1)S(1)}, bf16[3,128,2048]{2,1,0:T(8,128)(2,1)S(1)}, u32[]{:S(2)}, u32[]{:S(2)}) collective-permute-start(bf16[3,128,2048]{2,1,0:T(8,128)(2,1)S(1)} %get-tuple-element.20), channel_id=1, source_target_pairs={{0,1},{1,0},{2,3},{3,2},{4,5},{5,4},{6,7},{7,6},{8,9},{9,8},{10,11... | collective-permute-start | bytes 4718600 | tf_op jit(solution)/shard_map/ppermute | solution.py:388
  7.9 5.7 %collective-permute-start.1 = (bf16[3,8,2048]{2,1,0:T(8,128)(2,1)S(1)}, bf16[3,8,2048]{2,1,0:T(8,128)(2,1)S(1)}, u32[]{:S(2)}, u32[]{:S(2)}) collective-permute-start(bf16[3,8,2048]{2,1,0:T(8,128)(2,1)S(1)} %shard_map.39), channel_id=1, source_target_pairs={{0,2},{1,3},{2,4},{3,5},{4,6},{5,7},{6,8},{7,9},{8,10},{9,11},{10,... | collective-permute-start | bytes 294920 | tf_op jit(solution)/shard_map/ppermute | solution.py:411
  15.2 23.8 %all-to-all-start = ((bf16[32,136,128]{2,1,0:T(8,128)(2,1)}), bf16[32,136,128]{2,1,0:T(8,128)(2,1)S(1)}, u32[]{:S(2)}, u32[]{:S(2)}) async-start(bf16[32,136,128]{2,1,0:T(8,128)(2,1)} %shard_map.41), calls=%async_computation | async-start | bytes 2228224 | tf_op jit(solution)/shard_map/all_to_all | solution.py:441
  39.1 11.0 %collective-permute-start.3 = (bf16[136,128]{1,0:T(8,128)(2,1)S(1)}, bf16[136,128]{1,0:T(8,128)(2,1)S(1)}, u32[]{:S(2)}, u32[]{:S(2)}) collective-permute-start(bf16[136,128]{1,0:T(8,128)(2,1)S(1)} %shard_map.43.own), channel_id=1, source_target_pairs={{0,160},{32,128},{64,224},{96,192},{1,161},{33,129},{65,225},{97,1... | collective-permute-start | bytes 104456 | tf_op jit(solution)/shard_map/ppermute | solution.py:470
  47.3 3.8 %collective-permute-start.2 = (bf16[136,128]{1,0:T(8,128)(2,1)S(1)}, bf16[136,128]{1,0:T(8,128)(2,1)S(1)}, u32[]{:S(2)}, u32[]{:S(2)}) collective-permute-start(bf16[136,128]{1,0:T(8,128)(2,1)S(1)} %shard_map.43.own), channel_id=1, source_target_pairs={{0,64},{32,96},{64,160},{96,128},{1,65},{33,97},{65,161},{97,129},... | collective-permute-start | bytes 104456 | tf_op jit(solution)/shard_map/ppermute | solution.py:470
  50.1 1.0 %collective-permute-start.4 = (bf16[136,128]{1,0:T(8,128)(2,1)S(1)}, bf16[136,128]{1,0:T(8,128)(2,1)S(1)}, u32[]{:S(2)}, u32[]{:S(2)}) collective-permute-start(bf16[136,128]{1,0:T(8,128)(2,1)S(1)} %shard_map.44), channel_id=1, source_target_pairs={{160,224},{128,192},{161,225},{129,193},{162,226},{130,194},{163,2... | collective-permute-start | bytes 104456 | tf_op jit(solution)/shard_map/ppermute | solution.py:470
  51.1 20.2 %copy-start.1 = (f32[16,256,128]{2,1,0:T(8,128)S(1)}, f32[16,256,128]{2,1,0:T(8,128)}, u32[]{:S(2)}) copy-start(f32[16,256,128]{2,1,0:T(8,128)} %get-tuple-element.29.block) | copy-start | bytes 6291460
  51.3 20.0 %copy-start = (bf16[16,256,256]{2,1,0:T(8,128)(2,1)S(1)}, bf16[16,256,256]{2,1,0:T(8,128)(2,1)}, u32[]{:S(2)}) copy-start(bf16[16,256,256]{2,1,0:T(8,128)(2,1)} %get-tuple-element.31.query_map) | copy-start | bytes 6291460
  51.3 20.0 %copy-start.2 = (f32[256,128]{1,0:T(8,128)S(1)}, f32[256,128]{1,0:T(8,128)}, u32[]{:S(2)}) copy-start(f32[256,128]{1,0:T(8,128)} %get-tuple-element.30.sums) | copy-start | bytes 393220
  72.1 6.0 %collective-permute-start.5 = (bf16[128,2048]{1,0:T(8,128)(2,1)S(1)}, bf16[128,2048]{1,0:T(8,128)(2,1)S(1)}, u32[]{:S(2)}, u32[]{:S(2)}) collective-permute-start(bf16[128,2048]{1,0:T(8,128)(2,1)S(1)} %shard_map.46), channel_id=1, source_target_pairs={{0,1},{1,0},{2,3},{3,2},{4,5},{5,4},{6,7},{7,6},{8,9},{9,8},{10,11... | collective-permute-start | bytes 1572872 | tf_op jit(solution)/shard_map/ppermute | solution.py:388

commit v8 on v7

--- a/solution.py
+++ b/solution.py
@@ -469,8 +469,8 @@
         ways = [(owner(a, plane), owner(b, plane)) for a, b in pairs for plane in range(2)]
         return lax.ppermute(array, ("zh", "zl"), ways)
 
+    skipping = send(total, (0, 2), (1, 3))
     nearest = send(total, (0, 1), (1, 2))
-    skipping = send(total, (0, 2), (1, 3))
     pair = small_call(
         pair_kernel, [WHOLE] * 2, WHOLE, chip(STATE_ROWS, M // 2), [], flops=10**5, moved=10**5
     )(*in_chip(total, skipping))

time: 79.7 us -> 79.7 us (level)
  no operation moved by 1% of the time
where the time goes in v8:
time: 79.7 us; the launch traced here: 79 us
  starting transfers between devices  28.9 us (36%)
  Pallas kernels  22.2 us (28%)
  blocking collectives  19.9 us (25%)
  waiting for transfers between devices  7.75 us (10%)
    all_to_all x1, blocking collectives, per_device(): prior = lax.all_to_all(prior, PLANE, 0, 0, tiled=True)  19.9 us
    ppermute x3, starting transfers between devices, send(): return lax.ppermute(array, ('zh', 'zl'), ways)  11.6 us
    pallas_call x1, Pallas kernels, per_device(): call(scores_kernel, [own_spec(w) for w in which] + [other_spec(w) for w i...  9.66 us
    all_to_all x1, starting transfers between devices, per_device(): gathered = lax.all_to_all(state, PLANE, 0, 0, tiled=True)  8.09 us
    ppermute x2, starting transfers between devices, swap(): return lax.ppermute(array, 'c', [(0, 1), (1, 0)])  7.76 us
    all_to_all x1, waiting for transfers between devices, per_device(): gathered = lax.all_to_all(state, PLANE, 0, 0, tiled=True)  5.99 us
    pallas_call x1, Pallas kernels, per_device(): small_call(maps_kernel, [SCALAR] + [WHOLE] * 4, [WHOLE, ANYWHERE], [pltpu...  4.19 us
    pallas_call x1, Pallas kernels, per_device(): small_call(state_kernel, [SCALAR] * 2 + [WHOLE] * 6, WHOLE, chip(PIECES,...  1.62 us
  transfers between devices with their start and end apart: 7, of which 3 were waited for; matrix products, arithmetic and copies ran while one was open for 0% of the time, Pallas kernels for 22%

profile of v8, /device:TPU:1, one launch (start us, length us, event | category | flops | bytes accessed | tf_op | source)
XLA Modules:
  0.0 79.0 jit_solution(9894955278935974914)
XLA Ops:
  0.0 1.5 %shard_map.38 = (bf16[3,128,2048]{2,1,0:T(8,128)(2,1)S(1)}, bf16[3,8,2048]{2,1,0:T(8,128)(2,1)S(1)}) custom-call(s32[1]{0:T(128)} %bitcast.core_ref, bf16[3,128,4096]{2,1,0:T(8,128)(2,1)} %own_v.1), custom_call_target="tpu_custom_call" | custom-call | bytes 3145728 | tf_op jit(solution)/shard_map/pallas_call | solution.py:396
  1.5 3.3 %collective-permute-start = (bf16[3,128,2048]{2,1,0:T(8,128)(2,1)S(1)}, bf16[3,128,2048]{2,1,0:T(8,128)(2,1)S(1)}, u32[]{:S(2)}, u32[]{:S(2)}) collective-permute-start(bf16[3,128,2048]{2,1,0:T(8,128)(2,1)S(1)} %get-tuple-element.20), channel_id=1, source_target_pairs={{0,1},{1,0},{2,3},{3,2},{4,5},{5,4},{6,7},{7,6},{8,9},{9,8},{10,11... | collective-permute-start | bytes 4718600 | tf_op jit(solution)/shard_map/ppermute | solution.py:388
  4.8 1.6 %shard_map.37 = (bf16[2,128,2048]{2,1,0:T(8,128)(2,1)S(1)}, f32[3,4,2048]{2,1,0:T(4,128)S(1)}, bf16[16,128,256]{2,1,0:T(8,128)(2,1)S(1)}) custom-call(s32[1]{0:T(128)} %bitcast.core_ref, bf16[3,128,4096]{2,1,0:T(8,128)(2,1)} %own_v.1, f32[3,4,4096]{2,1,0:T(4,128)} %taps_v.1, bf16[32,128,256]{2,1,0:T(8,128)(2,1)} %omega.3), custom_call_target="tpu_custom_call" | custom-call | bytes 5242880 | tf_op jit(solution)/shard_map/pallas_call | solution.py:412
  6.4 1.4 %collective-permute-done.other = bf16[3,128,2048]{2,1,0:T(8,128)(2,1)S(1)} collective-permute-done((bf16[3,128,2048]{2,1,0:T(8,128)(2,1)S(1)}, bf16[3,128,2048]{2,1,0:T(8,128)(2,1)S(1)}, u32[]{:S(2)}, u32[]{:S(2)}) %collective-permute-start) | collective-permute-done | bytes 1572896 | tf_op jit(solution)/shard_map/ppermute | solution.py:388
  7.9 1.5 %collective-permute-start.1 = (bf16[3,8,2048]{2,1,0:T(8,128)(2,1)S(1)}, bf16[3,8,2048]{2,1,0:T(8,128)(2,1)S(1)}, u32[]{:S(2)}, u32[]{:S(2)}) collective-permute-start(bf16[3,8,2048]{2,1,0:T(8,128)(2,1)S(1)} %shard_map.39), channel_id=1, source_target_pairs={{0,2},{1,3},{2,4},{3,5},{4,6},{5,7},{6,8},{7,9},{8,10},{9,11},{10,... | collective-permute-start | bytes 294920 | tf_op jit(solution)/shard_map/ppermute | solution.py:411
  9.3 4.2 %shard_map.40 = (f32[16,136,256]{2,1,0:T(8,128)S(1)}, bf16[3,128,2048]{2,1,0:T(8,128)(2,1)}) custom-call(s32[1]{0:T(128)} %bitcast.core_ref, bf16[2,128,2048]{2,1,0:T(8,128)(2,1)S(1)} %get-tuple-element.19.own, bf16[3,128,2048]{2,1,0:T(8,128)(2,1)S(1)} %collective-permute-done.other, f32[3,4,2048]{2,1,0:T(4,128)S(1)} %get-tuple-element.22.taps, ...), custom_call_target="tpu_custom_call" | custom-call | flops 3000000000 | bytes 6291456 | tf_op jit(solution)/shard_map/pallas_call | solution.py:423
  13.5 0.0 collective-permute-done.1.rim.rim_q.rim_k.rim_v
  13.5 1.6 %shard_map.41 = bf16[32,136,128]{2,1,0:T(8,128)(2,1)} custom-call(s32[1]{0:T(128)} %bitcast.core_ref, s32[1]{0:T(128)} %bitcast.1.flip_ref, bf16[2,128,2048]{2,1,0:T(8,128)(2,1)S(1)} %get-tuple-element.19.own, bf16[3,128,2048]{2,1,0:T(8,128)(2,1)S(1)} %collective-permute-done.other, bf16[3,8,2048]{2,1,0:T(8,128)(2,1)S(1)} %collective-permute-done.1.rim.rim_q.rim_k.rim_v, ...), custom_call_target="tpu_custom_call" | custom-call | flops 2000000000 | bytes 6291456 | tf_op jit(solution)/shard_map/pallas_call | solution.py:432
  15.2 8.1 %all-to-all-start = ((bf16[32,136,128]{2,1,0:T(8,128)(2,1)}), bf16[32,136,128]{2,1,0:T(8,128)(2,1)S(1)}, u32[]{:S(2)}, u32[]{:S(2)}) async-start(bf16[32,136,128]{2,1,0:T(8,128)(2,1)} %shard_map.41), calls=%async_computation | async-start | bytes 2228224 | tf_op jit(solution)/shard_map/all_to_all | solution.py:441
  23.3 9.7 %shard_map.42 = (bf16[16,256,256]{2,1,0:T(8,128)(2,1)}, f32[16,256,128]{2,1,0:T(8,128)}, f32[256,128]{1,0:T(8,128)}) custom-call(s32[1]{0:T(128)} %bitcast.core_ref, bf16[3,128,4096]{2,1,0:T(8,128)(2,1)} %own_v.1, bf16[3,128,4096]{2,1,0:T(8,128)(2,1)} %own_v.1, bf16[3,128,4096]{2,1,0:T(8,128)(2,1)} %own_v.1, ...), custom_call_target="tpu_custom_call" | custom-call | flops 8000000000 | bytes 20971520 | tf_op jit(solution)/shard_map/pallas_call | solution.py:444
  32.9 6.0 %all-to-all-done.sums = bf16[32,136,128]{2,1,0:T(8,128)(2,1)S(1)} async-done(((bf16[32,136,128]{2,1,0:T(8,128)(2,1)}), bf16[32,136,128]{2,1,0:T(8,128)(2,1)S(1)}, u32[]{:S(2)}, u32[]{:S(2)}) %all-to-all-start) | async-done | bytes 1114144 | tf_op jit(solution)/shard_map/all_to_all | solution.py:441
  38.9 0.2 shard_map.43.own
  39.1 8.2 %collective-permute-start.3 = (bf16[136,128]{1,0:T(8,128)(2,1)S(1)}, bf16[136,128]{1,0:T(8,128)(2,1)S(1)}, u32[]{:S(2)}, u32[]{:S(2)}) collective-permute-start(bf16[136,128]{1,0:T(8,128)(2,1)S(1)} %shard_map.43.own), channel_id=1, source_target_pairs={{0,160},{32,128},{64,224},{96,192},{1,161},{33,129},{65,225},{97,1... | collective-permute-start | bytes 104456 | tf_op jit(solution)/shard_map/ppermute | solution.py:470
  47.3 2.7 %collective-permute-start.2 = (bf16[136,128]{1,0:T(8,128)(2,1)S(1)}, bf16[136,128]{1,0:T(8,128)(2,1)S(1)}, u32[]{:S(2)}, u32[]{:S(2)}) collective-permute-start(bf16[136,128]{1,0:T(8,128)(2,1)S(1)} %shard_map.43.own), channel_id=1, source_target_pairs={{0,64},{32,96},{64,160},{96,128},{1,65},{33,97},{65,161},{97,129},... | collective-permute-start | bytes 104456 | tf_op jit(solution)/shard_map/ppermute | solution.py:470
  50.0 0.0 collective-permute-done.3.before.before_2
  50.1 0.7 collective-permute-start.4
  50.7 0.3 collective-permute-done.2.before_1
  51.1 0.0 collective-permute-done.4.before_3
  51.1 0.0 copy-start.1
  51.1 0.2 shard_map.45
  51.3 0.0 copy-start
  51.3 0.0 copy-start.2
  51.3 19.9 %all_to_all.10.state = bf16[32,136,128]{2,1,0:T(8,128)(2,1)S(1)} all-to-all(bf16[32,136,128]{2,1,0:T(8,128)(2,1)S(1)} %shard_map.45), channel_id=1, replica_groups=mesh['zh'=4,'zl'=2,'x'=4,'y'=4,'c'=2] {'zl','x','y'}, dimensions={0} | all-to-all | bytes 2228224 | tf_op jit(solution)/shard_map/all_to_all | solution.py:482
  71.2 0.0 copy-done.1
  71.2 0.0 copy-done
  71.2 0.0 copy-done.2
  71.2 0.9 %shard_map.46 = bf16[128,2048]{1,0:T(8,128)(2,1)S(1)} custom-call(s32[1]{0:T(128)} %bitcast.core_ref, s32[1]{0:T(128)} %bitcast.1.flip_ref, f32[16,256,128]{2,1,0:T(8,128)S(1)} %copy-done.1, f32[256,128]{1,0:T(8,128)S(1)} %copy-done.2, bf16[16,256,256]{2,1,0:T(8,128)(2,1)S(1)} %copy-done, bf16[32,136,128]{2,1,0:T(8,128)(2,1)S(1)} %all_to_all.10.state), custom_call_target="tpu_custom_call" | custom-call | flops 2000000000 | bytes 4194304 | tf_op jit(solution)/shard_map/pallas_call | solution.py:484
  72.1 4.4 %collective-permute-start.5 = (bf16[128,2048]{1,0:T(8,128)(2,1)S(1)}, bf16[128,2048]{1,0:T(8,128)(2,1)S(1)}, u32[]{:S(2)}, u32[]{:S(2)}) collective-permute-start(bf16[128,2048]{1,0:T(8,128)(2,1)S(1)} %shard_map.46), channel_id=1, source_target_pairs={{0,1},{1,0},{2,3},{3,2},{4,5},{5,4},{6,7},{7,6},{8,9},{9,8},{10,11... | collective-permute-start | bytes 1572872 | tf_op jit(solution)/shard_map/ppermute | solution.py:388
  76.6 1.6 %shard_map.47.partial = bf16[128,4096]{1,0:T(8,128)(2,1)} custom-call(s32[1]{0:T(128)} %bitcast.core_ref, s32[1]{0:T(128)} %bitcast.1.flip_ref, f32[16,256,128]{2,1,0:T(8,128)S(1)} %copy-done.1, f32[256,128]{1,0:T(8,128)S(1)} %copy-done.2, bf16[16,256,256]{2,1,0:T(8,128)(2,1)S(1)} %copy-done, bf16[32,136,128]{2,1,0:T(8,128)(2,1)S(1)} %all_to_all.10.state), custom_call_target="tpu_custom_call" | custom-call | flops 2000000000 | bytes 4194304 | tf_op jit(solution)/shard_map/pallas_call | solution.py:489
  78.1 0.0 collective-permute-done.5.arrived
  78.2 0.8 %shard_map.48 = bf16[128,4096]{1,0:T(8,128)(2,1)} custom-call(s32[1]{0:T(128)} %bitcast.core_ref, bf16[128,2048]{1,0:T(8,128)(2,1)S(1)} %collective-permute-done.5.arrived, bf16[128,4096]{1,0:T(8,128)(2,1)} %shard_map.47.partial), custom_call_target="tpu_custom_call", output_to_operand_aliasing={{}: (2, {})} | custom-call | bytes 1048576 | tf_op jit(solution)/shard_map/pallas_call | solution.py:494
  (2 shorter events, 0.0 us)
Async XLA Ops:
  1.5 6.4 %collective-permute-start = (bf16[3,128,2048]{2,1,0:T(8,128)(2,1)S(1)}, bf16[3,128,2048]{2,1,0:T(8,128)(2,1)S(1)}, u32[]{:S(2)}, u32[]{:S(2)}) collective-permute-start(bf16[3,128,2048]{2,1,0:T(8,128)(2,1)S(1)} %get-tuple-element.20), channel_id=1, source_target_pairs={{0,1},{1,0},{2,3},{3,2},{4,5},{5,4},{6,7},{7,6},{8,9},{9,8},{10,11... | collective-permute-start | bytes 4718600 | tf_op jit(solution)/shard_map/ppermute | solution.py:388
  7.9 5.7 %collective-permute-start.1 = (bf16[3,8,2048]{2,1,0:T(8,128)(2,1)S(1)}, bf16[3,8,2048]{2,1,0:T(8,128)(2,1)S(1)}, u32[]{:S(2)}, u32[]{:S(2)}) collective-permute-start(bf16[3,8,2048]{2,1,0:T(8,128)(2,1)S(1)} %shard_map.39), channel_id=1, source_target_pairs={{0,2},{1,3},{2,4},{3,5},{4,6},{5,7},{6,8},{7,9},{8,10},{9,11},{10,... | collective-permute-start | bytes 294920 | tf_op jit(solution)/shard_map/ppermute | solution.py:411
  15.2 23.8 %all-to-all-start = ((bf16[32,136,128]{2,1,0:T(8,128)(2,1)}), bf16[32,136,128]{2,1,0:T(8,128)(2,1)S(1)}, u32[]{:S(2)}, u32[]{:S(2)}) async-start(bf16[32,136,128]{2,1,0:T(8,128)(2,1)} %shard_map.41), calls=%async_computation | async-start | bytes 2228224 | tf_op jit(solution)/shard_map/all_to_all | solution.py:441
  39.1 11.0 %collective-permute-start.3 = (bf16[136,128]{1,0:T(8,128)(2,1)S(1)}, bf16[136,128]{1,0:T(8,128)(2,1)S(1)}, u32[]{:S(2)}, u32[]{:S(2)}) collective-permute-start(bf16[136,128]{1,0:T(8,128)(2,1)S(1)} %shard_map.43.own), channel_id=1, source_target_pairs={{0,160},{32,128},{64,224},{96,192},{1,161},{33,129},{65,225},{97,1... | collective-permute-start | bytes 104456 | tf_op jit(solution)/shard_map/ppermute | solution.py:470
  47.3 3.8 %collective-permute-start.2 = (bf16[136,128]{1,0:T(8,128)(2,1)S(1)}, bf16[136,128]{1,0:T(8,128)(2,1)S(1)}, u32[]{:S(2)}, u32[]{:S(2)}) collective-permute-start(bf16[136,128]{1,0:T(8,128)(2,1)S(1)} %shard_map.43.own), channel_id=1, source_target_pairs={{0,64},{32,96},{64,160},{96,128},{1,65},{33,97},{65,161},{97,129},... | collective-permute-start | bytes 104456 | tf_op jit(solution)/shard_map/ppermute | solution.py:470
  50.1 1.0 %collective-permute-start.4 = (bf16[136,128]{1,0:T(8,128)(2,1)S(1)}, bf16[136,128]{1,0:T(8,128)(2,1)S(1)}, u32[]{:S(2)}, u32[]{:S(2)}) collective-permute-start(bf16[136,128]{1,0:T(8,128)(2,1)S(1)} %shard_map.44), channel_id=1, source_target_pairs={{160,224},{128,192},{161,225},{129,193},{162,226},{130,194},{163,2... | collective-permute-start | bytes 104456 | tf_op jit(solution)/shard_map/ppermute | solution.py:470
  51.1 20.2 %copy-start.1 = (f32[16,256,128]{2,1,0:T(8,128)S(1)}, f32[16,256,128]{2,1,0:T(8,128)}, u32[]{:S(2)}) copy-start(f32[16,256,128]{2,1,0:T(8,128)} %get-tuple-element.29.block) | copy-start | bytes 6291460
  51.3 20.0 %copy-start = (bf16[16,256,256]{2,1,0:T(8,128)(2,1)S(1)}, bf16[16,256,256]{2,1,0:T(8,128)(2,1)}, u32[]{:S(2)}) copy-start(bf16[16,256,256]{2,1,0:T(8,128)(2,1)} %get-tuple-element.31.query_map) | copy-start | bytes 6291460
  51.3 20.0 %copy-start.2 = (f32[256,128]{1,0:T(8,128)S(1)}, f32[256,128]{1,0:T(8,128)}, u32[]{:S(2)}) copy-start(f32[256,128]{1,0:T(8,128)} %get-tuple-element.30.sums) | copy-start | bytes 393220
  72.1 6.0 %collective-permute-start.5 = (bf16[128,2048]{1,0:T(8,128)(2,1)S(1)}, bf16[128,2048]{1,0:T(8,128)(2,1)S(1)}, u32[]{:S(2)}, u32[]{:S(2)}) collective-permute-start(bf16[128,2048]{1,0:T(8,128)(2,1)S(1)} %shard_map.46), channel_id=1, source_target_pairs={{0,1},{1,0},{2,3},{3,2},{4,5},{5,4},{6,7},{7,6},{8,9},{9,8},{10,11... | collective-permute-start | bytes 1572872 | tf_op jit(solution)/shard_map/ppermute | solution.py:388
